TPU v7x, 128 devices: a whole 4x4x4 slice. The times are simulated.
128 devices in a mesh: seq: 32 (over z, y, core), tp: 4 (over x).
Axes of the slice: x: 4, y: 4, z: 4, core: 2. Of those that a mesh axis runs over, the one named last changes fastest.
Arguments:
- tokens: bfloat16 [32768, 2048], P('seq', 'tp'), may hold values from -8 to 8
- col_order: int32 [32768], P('seq'), may hold values from 0 to 32767, as said below
- in_gain: float32 [2, 2048], replicated, may hold values from 0.5 to 1.5
- w_in: bfloat16 [2, 2048, 2, 2048], P(None, None, None, 'tp'), may hold values from -0.125 to 0.125
- w_bc: bfloat16 [2, 2048, 256], replicated, may hold values from -0.0625 to 0.0625
- w_dt: bfloat16 [2, 2048, 32], P(None, None, 'tp'), may hold values from -2 to 2
- conv_x: float32 [2, 4, 2048], P(None, None, 'tp'), may hold values from -3 to 3
- conv_bc: float32 [2, 4, 256], replicated, may hold values from -3 to 3
- dt_bias: float32 [2, 32], P(None, 'tp'), may hold values from -1 to 0.5
- a_log: float32 [2, 32], P(None, 'tp'), may hold values from -16 to -2, as said below
- d_skip: float32 [2, 32], P(None, 'tp'), may hold values from 0.5 to 2
- out_gain: float32 [2, 2048], P(None, 'tp'), may hold values from 0.5 to 1.5
- w_out: bfloat16 [2, 2048, 2048], P(None, 'tp'), may hold values from -0.125 to 0.125
Outputs:
- mixed_out: bfloat16 [32768, 2048], P('seq', 'tp')
Inputs may be any that keep to these rules, and one draw needn't show every extreme that they name: `col_order`: A permutation of the 32768 positions of a frame of 64 rows and 512 columns stored row by row: the column order visits the columns one after another in a drawn order, each from top to bottom or from bottom to top as drawn. So every aligned block of 1024 positions takes exactly 32 row-order positions from each aligned block of 1024 row-order positions. Each head's decay rate exp(a_log) is either between about one in fifty and one in seventeen a step or between 0.3 / 32768 and 2 / 32768 a step.
All inputs are finite; a program needn't handle non-finite values.
Results may differ from a plain program's by a relative error of at most 0.024.
Values may be sent and summed in bfloat16 or wider, within the bound.
No kernel may reach another device: no remote copies, remote signals or barrier semaphores. Data moves between devices by JAX's collectives and lax.ppermute only.
A program may use at most 128 MiB of HBM per device.

v0:
```python
import jax
import jax.numpy as jnp
from jax import lax
from jax.sharding import Mesh
from jax.sharding import PartitionSpec as P

HEAD_DIM = 64
STATE = 128
STRETCH = 128
SEQ = ("seq_0", "seq_1", "seq_2")


highest = lax.Precision.HIGHEST
epsilon = 1e-05


def laid_out(blocks, dim):
    blocks = jnp.moveaxis(blocks, 0, dim)
    lengths = blocks.shape
    return blocks.reshape(*lengths[:dim], lengths[dim] * lengths[dim + 1], *lengths[dim + 2 :])


def sent_to_all(x, axis):
    devices = lax.axis_size(axis)
    return lax.all_to_all(jnp.broadcast_to(x[None], (devices, *x.shape)), axis, 0, 0, tiled=True)


def gathered_copies(x, axis, dim):
    return laid_out(sent_to_all(x, axis), dim)


def passed_along(x, axis, by):
    devices = lax.axis_size(axis)
    pairs = [(i, i + by) for i in range(devices) if 0 <= i + by < devices]
    return lax.ppermute(x, axis, pairs)


def in_blocks(x, dim, devices):
    lengths = x.shape
    blocks = x.reshape(*lengths[:dim], devices, lengths[dim] // devices, *lengths[dim + 1 :])
    return jnp.moveaxis(blocks, dim, 0)


def moved_by_axis(blocks, axes, turns):
    lengths = [lax.axis_size(a) for a in axes]
    blocks = blocks.reshape(*lengths, *blocks.shape[1:])
    for k in turns:
        blocks = lax.all_to_all(blocks, axes[k], split_axis=k, concat_axis=k, tiled=True)
    return blocks.reshape(-1, *blocks.shape[len(axes) :])


def exchange_by_chip(x, groups, turns, split_dim, concat_dim):
    devices = lax.axis_size(groups[0]) * lax.axis_size(groups[1])
    blocks = in_blocks(x, split_dim, devices)
    return laid_out(moved_by_axis(blocks, groups, turns), concat_dim)


def causal_mix(current, rim, taps):
    length = current.shape[0]
    extended = jnp.concatenate([rim, current], axis=0).astype(jnp.float32)
    mixed = jnp.zeros(current.shape, jnp.float32)
    for offset in range(taps.shape[0]):
        mixed = mixed + taps[offset] * extended[offset : offset + length]
    return mixed


def advance(state, pieces):
    factor, fresh = pieces
    return (factor[:, None, None] * state + fresh, state)


def incoming_state(local_end, device_log):
    count = lax.axis_size(SEQ)
    own_index = lax.axis_index(SEQ)
    gathered = gathered_copies(device_log, SEQ, 0).reshape(count, device_log.shape[0])
    before = jnp.cumsum(gathered, axis=0) - gathered
    earlier = (jnp.arange(count) < own_index)[:, None]
    own_prefix = jnp.sum(jnp.where(earlier, gathered, 0.0), axis=0)
    spans = jnp.where(earlier, own_prefix[None, :] - before - gathered, -jnp.inf)
    factors = jnp.exp(spans)
    return jnp.zeros(local_end.shape, jnp.float32) + jnp.einsum(
        "mh,mhpn->hpn",
        factors,
        lax.all_gather(local_end[None].astype(jnp.bfloat16), SEQ, axis=0, tiled=True).astype(
            jnp.float32
        ),
        precision=highest,
    )


def mixer(full, which, params):
    in_gain, w_in, w_bc, w_dt, conv_x, conv_bc, dt_bias, a_log, d_skip, out_gain, w_out = params
    row_count, model_width = full.shape
    inner = w_in.shape[3]
    head_count = inner // HEAD_DIM
    lag = conv_x.shape[1] - 1
    widen = full.astype(jnp.float32)
    scale = lax.rsqrt(jnp.mean(widen * widen, axis=-1, keepdims=True) + epsilon)
    normed = (widen * scale * in_gain[which]).astype(jnp.bfloat16)
    projected = jnp.dot(
        normed, w_in[which].reshape(model_width, 2 * inner), preferred_element_type=jnp.float32
    )
    pre_x = projected[:, :inner].astype(jnp.bfloat16)
    gate_z = projected[:, inner:].astype(jnp.bfloat16)
    pre_bc = jnp.dot(normed, w_bc[which], preferred_element_type=jnp.float32).astype(jnp.bfloat16)
    dt_raw = jnp.dot(normed, w_dt[which], preferred_element_type=jnp.float32)
    rim_x, rim_bc = passed_along((pre_x[row_count - lag :], pre_bc[row_count - lag :]), SEQ, 1)
    conv_out = jax.nn.silu(causal_mix(pre_x, rim_x, conv_x[which]))
    bc_out = jax.nn.silu(causal_mix(pre_bc, rim_bc, conv_bc[which]))
    step_size = jax.nn.softplus(dt_raw + dt_bias[which])
    decay_log = -step_size * jnp.exp(a_log[which])
    heads_in = conv_out.reshape(row_count, head_count, HEAD_DIM)
    feed = heads_in * step_size[:, :, None]
    blocks = row_count // STRETCH
    log_blocks = decay_log.reshape(blocks, STRETCH, head_count)
    b_blocks = bc_out[:, :STATE].reshape(blocks, STRETCH, STATE)
    c_blocks = bc_out[:, STATE:].reshape(blocks, STRETCH, STATE)
    feed_blocks = feed.reshape(blocks, STRETCH, head_count, HEAD_DIM)
    cumul = jnp.cumsum(log_blocks, axis=1)
    cumul_t = jnp.transpose(cumul, (0, 2, 1))
    lower = jnp.arange(STRETCH)[:, None] >= jnp.arange(STRETCH)[None, :]
    spread = jnp.where(lower[None, None], cumul_t[..., :, None] - cumul_t[..., None, :], -jnp.inf)
    intersection = jnp.einsum("cqn,ckn->cqk", c_blocks, b_blocks, precision=highest)
    inside = jnp.einsum(
        "chqk,ckhp->cqhp", intersection[:, None] * jnp.exp(spread), feed_blocks, precision=highest
    )
    to_end = jnp.exp(cumul_t[..., -1:] - cumul_t)
    fresh = jnp.einsum("chk,ckn,ckhp->chpn", to_end, b_blocks, feed_blocks, precision=highest)
    block_decay = jnp.exp(cumul_t[..., -1])
    start_state = jnp.zeros((head_count, HEAD_DIM, STATE), jnp.float32)
    local_end, entering = lax.scan(advance, start_state, (block_decay, fresh))
    carried = (
        jnp.einsum("cqn,chpn->cqhp", c_blocks, entering, precision=highest)
        * jnp.exp(cumul)[..., None]
    )
    block_sums = cumul[:, -1, :]
    prior = jnp.cumsum(block_sums, axis=0) - block_sums
    device_cumul = cumul + prior[:, None, :]
    device_log = jnp.sum(block_sums, axis=0)
    arriving = incoming_state(local_end, device_log)
    correction = (
        jnp.einsum("cqn,hpn->cqhp", c_blocks, arriving, precision=highest)
        * jnp.exp(device_cumul)[..., None]
    )
    ssd = (inside + carried + correction).reshape(row_count, head_count, HEAD_DIM) + d_skip[which][
        None, :, None
    ] * heads_in
    gated = ssd * jax.nn.silu(gate_z.astype(jnp.float32).reshape(row_count, head_count, HEAD_DIM))
    norm_scale = lax.rsqrt(jnp.mean(gated * gated, axis=-1, keepdims=True) + epsilon)
    mixed_heads = (
        (gated * norm_scale * out_gain[which].reshape(head_count, HEAD_DIM))
        .reshape(row_count, inner)
        .astype(jnp.bfloat16)
    )
    return jnp.dot(mixed_heads, w_out[which], preferred_element_type=jnp.float32)


def spread_features(piece):
    return lax.all_gather(piece, "tp", axis=1, tiled=True)


def collect_heads(partial_sum):
    return lax.psum_scatter(
        partial_sum.astype(jnp.bfloat16), "tp", scatter_dimension=1, tiled=True
    ).astype(jnp.float32)


def reorder_rows(stream, col_order):
    count = lax.axis_size(SEQ)
    row_count = stream.shape[0]
    block_rows = row_count // count
    source = col_order // row_count
    local_index = col_order % row_count
    grouping = jnp.argsort(source, stable=True)
    wanted = local_index[grouping].reshape(count, block_rows)
    asked = exchange_by_chip(wanted, (("seq_0", "seq_1"), "seq_2"), (1, 0), 0, 0)
    payload = stream[asked.reshape(-1)].reshape(count, block_rows, stream.shape[1])
    arrived = exchange_by_chip(payload, (("seq_0", "seq_1"), "seq_2"), (1, 0), 0, 0).reshape(
        row_count, stream.shape[1]
    )
    placement = jnp.argsort(grouping)
    return arrived[placement]


def body(
    tokens,
    col_order,
    in_gain,
    w_in,
    w_bc,
    w_dt,
    conv_x,
    conv_bc,
    dt_bias,
    a_log,
    d_skip,
    out_gain,
    w_out,
):
    params = (in_gain, w_in, w_bc, w_dt, conv_x, conv_bc, dt_bias, a_log, d_skip, out_gain, w_out)
    first_full = spread_features(tokens)
    first_part = mixer(first_full, 0, params)
    row_result = (tokens.astype(jnp.float32) + collect_heads(first_part)).astype(jnp.bfloat16)
    own_rows = reorder_rows(row_result, col_order)
    second_full = spread_features(own_rows)
    second_part = mixer(second_full, 1, params)
    return (own_rows.astype(jnp.float32) + collect_heads(second_part)).astype(jnp.bfloat16)


def solution(mesh):
    torus = Mesh(mesh.devices.reshape(4, 4, 2, mesh.shape["tp"]), ("seq_0", "seq_1", "seq_2", "tp"))
    return jax.shard_map(
        body,
        mesh=torus,
        in_specs=(
            P(SEQ, "tp"),
            P(SEQ),
            P(),
            P(None, None, None, "tp"),
            P(),
            P(None, None, "tp"),
            P(None, None, "tp"),
            P(),
            P(None, "tp"),
            P(None, "tp"),
            P(None, "tp"),
            P(None, "tp"),
            P(None, "tp", None),
        ),
        out_specs=P(SEQ, "tp"),
        check_vma=False,
    )
```

profile of v0, /device:TPU:0, one launch (start us, length us, event | category | flops | bytes accessed | tf_op | source)
XLA Modules:
  0.0 575.0 jit_solution(12658820675319592210)
XLA Ops:
  7.3 7.9 %fusion.98 = (bf16[1,2048,2,512]{3,2,1,0:T(2,128)(2,1)}, bf16[1,2048,2,512]{3,2,1,0:T(2,128)(2,1)S(1)}) fusion(bf16[2,2048,2,512]{3,2,1,0:T(2,128)(2,1)} %param.20), kind=kLoop, calls=%fused_computation.187 | loop fusion | bytes 16777216 | tf_op jit(solution)/shard_map/slice | solution.py:101
  20.9 38.8 %all-gather.8.cloned.1.call-done = bf16[1024,2048]{1,0:T(8,128)(2,1)} async-done(((bf16[1024,512]{1,0:T(8,128)(2,1)}), bf16[1024,2048]{1,0:T(8,128)(2,1)}) %all-gather.8.cloned.1.call-update) | async-done | bytes 4194320 | tf_op jit(solution)/shard_map/all_gather | solution.py:159
  63.2 7.2 %convolution_convert_fusion.3 = bf16[1024,1024]{1,0:T(8,128)(2,1)S(1)} fusion(bf16[2048,1024]{1,0:T(8,128)(2,1)} %bitcast.229, bf16[1024,2048]{1,0:T(8,128)(2,1)S(1)} %copy-done.14, f32[2048]{0:T(1024)S(1)} %bitcast.255, f32[1024]{0:T(1024)S(1)} %add_rsqrt_fusion.1), kind=kOutput, calls=%fused_computation.92 | convolution fusion | flops 4304404480 | bytes 10498048 | tf_op jit(solution)/shard_map/dot_general | solution.py:100
  74.2 23.3 %fusion.107 = f32[8,128,8]{2,0,1:T(8,128)S(1)} fusion(f32[8,128,8]{2,0,1:T(8,128)S(1)} %copy.146), kind=kOutput, calls=%fused_computation.197 | output fusion | flops 1040384 | bytes 65536 | tf_op jit(solution)/shard_map/jit(cumsum)/reduce_window_sum | solution.py:119
  128.3 19.8 %while.26 = (s32[]{:T(128)}, f32[8,64,128]{2,1,0:T(8,128)S(1)}, f32[8,8,64,128]{3,2,1,0:T(8,128)}, f32[8,8]{1,0:T(8,128)}, f32[8,8,64,128]{3,2,1,0:T(8,128)}, /*index=5*/s32[]{:T(128)}, s32[]{:T(128)}) while((s32[]{:T(128)}, f32[8,64,128]{2,1,0:T(8,128)S(1)}, f32[8,8,64,128]{3,2,1,0:T(8,128)}, f32[8,8]{1,0:T(8,128)}, ...), condition=%wide.region_3.4_spmd.clone, body=%wide.region_2.3_spmd.clone.sunk | while | flops 262147 | bytes 1311424 | solution.py:131
  151.9 7.8 %all-to-all-start = ((f32[32,1,8]{2,1,0:T(1,128)}), f32[32,1,8]{2,1,0:T(1,128)S(1)}, u32[]{:S(2)}, u32[]{:S(2)}) async-start(f32[32,1,8]{2,1,0:T(1,128)} %broadcast_in_dim.64), calls=%async_computation | async-start | bytes 32768 | tf_op jit(solution)/shard_map/all_to_all | solution.py:25
  174.9 9.7 %fusion.17 = f32[8,8,64,128]{3,2,1,0:T(8,128)} fusion(f32[8,128,8,64]{1,0,3,2:T(8,128)S(1)} %copy-done.18, f32[8,8,128]{2,1,0:T(8,128)S(1)} %copy.147, f32[8,128,128]{2,1,0:T(8,128)S(1)} %fusion.109, pred[128,128]{1,0:T(8,128)(4,1)S(1)} %iota_compare_fusion), kind=kOutput, calls=%fused_computation.30 | convolution fusion | flops 808452096 | bytes 4767744 | tf_op jit(solution)/shard_map/chqk,ckhp->cqhp/dot_general | solution.py:124
  184.6 11.7 %all-gather.10.cloned.1.call-done = bf16[256,64,128]{2,1,0:T(8,128)(2,1)} async-done(((bf16[8,64,128]{2,1,0:T(8,128)(2,1)}), bf16[256,64,128]{2,1,0:T(8,128)(2,1)}) %all-gather.10.cloned.1.call-update) | async-done | bytes 4194320 | tf_op jit(solution)/shard_map/all_gather | solution.py:84
  196.3 6.2 %fusion.10 = f32[8,1,64,128]{3,1,2,0:T(1,128)S(1)} fusion(f32[32,8,1,1]{0,2,3,1:T(1,128)S(1)} %copy.184, bf16[32,8,64,128]{3,2,1,0:T(8,128)(2,1)} %bitcast.226), kind=kOutput, calls=%fused_computation.23 | convolution fusion | flops 25165824 | bytes 4457472 | tf_op jit(solution)/shard_map/mh,mhpn->hpn/dot_general | solution.py:81
  217.4 8.5 %convolution_convert_fusion.1 = bf16[1024,2048]{1,0:T(8,128)(2,1)} fusion(bf16[2,512,2048]{2,1,0:T(8,128)(2,1)} %param.29, f32[1024,512]{1,0:T(8,128)} %copy.160, f32[1024,512]{1,0:T(8,128)} %reshape.289, f32[1024,512]{1,0:T(8,128)} %divide_multiply_fusion.1, f32[512]{0:T(512)S(1)} %bitcast.267, f32[512]{0:T(512)S(1)} %copy-done.39, ...), kind=kOutput, calls=%fused_computation.36 | convolution fusion | flops 2155347968 | bytes 13635584 | tf_op jit(solution)/shard_map/dot_general | solution.py:155
  241.4 12.4 %all_to_all.39 = s32[16,2,1,32]{3,2,1,0:T(1,128)S(1)} all-to-all(s32[16,2,1,32]{3,2,1,0:T(1,128)S(1)} %copy.162), channel_id=1, replica_groups=mesh['seq_0'=4,'seq_1'=4,'seq_2'=2,'tp'=4] {'seq_0','seq_1'}, dimensions={0} | all-to-all | bytes 8192 | tf_op jit(solution)/shard_map/all_to_all | solution.py:48
  255.1 17.1 %reduce-scatter.3.cloned.1.call-done = bf16[1024,512]{1,0:T(8,128)(2,1)} async-done(((bf16[1024,2048]{1,0:T(8,128)(2,1)}), bf16[1024,512]{1,0:T(8,128)(2,1)}) %reduce-scatter.3.cloned.1.call-update) | async-done | bytes 1048592 | tf_op jit(solution)/shard_map/reduce_scatter | solution.py:163
  283.4 7.0 %all-to-all-start.4 = ((bf16[16,2,1,32,512]{4,3,1,2,0:T(8,128)(2,1)}), bf16[16,2,1,32,512]{4,3,1,2,0:T(8,128)(2,1)S(1)}, u32[]{:S(2)}, u32[]{:S(2)}) async-start(bf16[16,2,1,32,512]{4,3,1,2,0:T(8,128)(2,1)} %copy.164), calls=%async_computation.5 | async-start | bytes 2097152 | tf_op jit(solution)/shard_map/all_to_all | solution.py:48
  294.8 13.4 %all-to-all-done.4 = bf16[16,2,1,32,512]{4,3,1,2,0:T(8,128)(2,1)S(1)} async-done(((bf16[16,2,1,32,512]{4,3,1,2,0:T(8,128)(2,1)}), bf16[16,2,1,32,512]{4,3,1,2,0:T(8,128)(2,1)S(1)}, u32[]{:S(2)}, u32[]{:S(2)}) %all-to-all-start.4) | async-done | bytes 1048608 | tf_op jit(solution)/shard_map/all_to_all | solution.py:48
  319.1 38.5 %all-gather.12.cloned.1.call-done = bf16[1024,2048]{1,0:T(8,128)(2,1)} async-done(((bf16[1024,512]{1,0:T(8,128)(2,1)}), bf16[1024,2048]{1,0:T(8,128)(2,1)}) %all-gather.12.cloned.1.call-update) | async-done | bytes 4194320 | tf_op jit(solution)/shard_map/all_gather | solution.py:159
  366.9 23.3 %fusion.108 = f32[8,128,8]{2,0,1:T(8,128)S(1)} fusion(f32[8,128,8]{2,0,1:T(8,128)S(1)} %copy.167), kind=kOutput, calls=%fused_computation.198 | output fusion | flops 1040384 | bytes 65536 | tf_op jit(solution)/shard_map/jit(cumsum)/reduce_window_sum | solution.py:119
  390.3 8.0 %convolution_convert_fusion.2 = bf16[1024,1024]{1,0:T(8,128)(2,1)S(1)} fusion(bf16[2048,1024]{1,0:T(8,128)(2,1)} %bitcast.230, bf16[1024,2048]{1,0:T(8,128)(2,1)} %all-gather.12.cloned.1.call-done, f32[2048]{0:T(1024)S(1)} %bitcast.254, f32[1024]{0:T(1024)S(1)} %add_rsqrt_fusion), kind=kOutput, calls=%fused_computation.91 | convolution fusion | flops 4304404480 | bytes 10498048 | tf_op jit(solution)/shard_map/dot_general | solution.py:100
  422.8 19.8 %while.27 = (s32[]{:T(128)}, f32[8,64,128]{2,1,0:T(8,128)S(1)}, f32[8,8,64,128]{3,2,1,0:T(8,128)}, f32[8,8]{1,0:T(8,128)}, f32[8,8,64,128]{3,2,1,0:T(8,128)}, /*index=5*/s32[]{:T(128)}, s32[]{:T(128)}) while((s32[]{:T(128)}, f32[8,64,128]{2,1,0:T(8,128)S(1)}, f32[8,8,64,128]{3,2,1,0:T(8,128)}, f32[8,8]{1,0:T(8,128)}, ...), condition=%wide.region_15.16_spmd.clone, body=%wide.region_14.15_spmd.clone.sunk | while | flops 262147 | bytes 1311424 | solution.py:131
  444.2 7.0 %all-to-all-start.5 = ((f32[32,1,8]{2,1,0:T(1,128)}), f32[32,1,8]{2,1,0:T(1,128)S(1)}, u32[]{:S(2)}, u32[]{:S(2)}) async-start(f32[32,1,8]{2,1,0:T(1,128)} %broadcast_in_dim.112), calls=%async_computation.6 | async-start | bytes 32768 | tf_op jit(solution)/shard_map/all_to_all | solution.py:25
  466.5 9.7 %fusion.12 = f32[8,8,64,128]{3,2,1,0:T(8,128)} fusion(f32[8,128,8,64]{1,0,3,2:T(8,128)S(1)} %copy-done.19, f32[8,8,128]{2,1,0:T(8,128)S(1)} %copy.168, f32[8,128,128]{2,1,0:T(8,128)S(1)} %fusion.111, pred[128,128]{1,0:T(8,128)(4,1)S(1)} %iota_compare_fusion), kind=kOutput, calls=%fused_computation.25 | convolution fusion | flops 808452096 | bytes 4767744 | tf_op jit(solution)/shard_map/chqk,ckhp->cqhp/dot_general | solution.py:124
  476.2 13.8 %all-gather.14.cloned.1.call-done = bf16[256,64,128]{2,1,0:T(8,128)(2,1)} async-done(((bf16[8,64,128]{2,1,0:T(8,128)(2,1)}), bf16[256,64,128]{2,1,0:T(8,128)(2,1)}) %all-gather.14.cloned.1.call-update) | async-done | bytes 4194320 | tf_op jit(solution)/shard_map/all_gather | solution.py:84
  490.0 6.0 %fusion.8 = f32[8,1,64,128]{3,1,2,0:T(1,128)S(1)} fusion(f32[32,8,1,1]{0,2,3,1:T(1,128)S(1)} %copy.189, bf16[32,8,64,128]{3,2,1,0:T(8,128)(2,1)} %bitcast.227), kind=kOutput, calls=%fused_computation.21 | convolution fusion | flops 25165824 | bytes 4457472 | tf_op jit(solution)/shard_map/mh,mhpn->hpn/dot_general | solution.py:81
  510.9 8.4 %convolution_convert_fusion = bf16[1024,2048]{1,0:T(8,128)(2,1)} fusion(bf16[2,512,2048]{2,1,0:T(8,128)(2,1)} %param.29, f32[1024,512]{1,0:T(8,128)} %copy.181, f32[1024,512]{1,0:T(8,128)} %reshape.290, f32[1024,512]{1,0:T(8,128)} %divide_multiply_fusion, f32[512]{0:T(512)S(1)} %bitcast.266, f32[512]{0:T(512)S(1)} %mul.565, bf16[1024,1024]{1,0:T(8,128)(2,1)} %copy-done.17), kind=kOutput, calls=%fused_computation.35 | convolution fusion | flops 2155347968 | bytes 13635584 | tf_op jit(solution)/shard_map/dot_general | solution.py:155
  519.3 46.2 %reduce-scatter.5.cloned.1.call-done = bf16[1024,512]{1,0:T(8,128)(2,1)} async-done(((bf16[1024,2048]{1,0:T(8,128)(2,1)}), bf16[1024,512]{1,0:T(8,128)(2,1)}) %reduce-scatter.5.cloned.1.call-update) | async-done | bytes 1048592 | tf_op jit(solution)/shard_map/reduce_scatter | solution.py:163
  (314 shorter events, 228.3 us)
Async XLA Ops:
  6.5 53.2 %all-gather.8.cloned.1.call-start = ((), (), s32[]{:S(2)}) async-start(), calls=%async_computation.8 | async-start | bytes 5242880 | tf_op jit(solution)/shard_map/all_gather | solution.py:159
  7.3 189.0 %all-gather.10.cloned.1.call-start = ((), (), s32[]{:S(2)}) async-start(), calls=%async_computation.11 | async-start | bytes 4325376 | tf_op jit(solution)/shard_map/all_gather | solution.py:84
  98.2 14.6 %collective-permute-start = (bf16[3,512]{1,0:T(4,128)(2,1)}, bf16[3,512]{1,0:T(4,128)(2,1)S(1)}, u32[]{:S(2)}, u32[]{:S(2)}) collective-permute-start(bf16[3,512]{1,0:T(4,128)(2,1)} %slice.314), channel_id=1, source_target_pairs={{0,4},{4,8},{8,12},{12,16},{16,20},{20,24},{24,28},{28,32},{32,36}... | collective-permute-start | bytes 9224 | tf_op jit(solution)/shard_map/ppermute | solution.py:35
  103.7 6.8 %copy-start.34 = (f32[1,1,256]{2,1,0:T(1,128)S(1)}, f32[1,1,256]{2,1,0:T(1,128)}, u32[]{:S(2)}) copy-start(f32[1,1,256]{2,1,0:T(1,128)} %get-tuple-element.160) | copy-start | bytes 3076
  103.7 6.8 %copy-start.35 = (f32[1,1,256]{2,1,0:T(1,128)S(1)}, f32[1,1,256]{2,1,0:T(1,128)}, u32[]{:S(2)}) copy-start(f32[1,1,256]{2,1,0:T(1,128)} %get-tuple-element.161) | copy-start | bytes 3076
  104.5 4.9 collective-permute-start.1
  128.3 20.5 %copy-start.47 = (f32[2,8]{1,0:T(2,128)S(1)}, f32[2,8]{1,0:T(2,128)}, u32[]{:S(2)}) copy-start(f32[2,8]{1,0:T(2,128)} %param.27) | copy-start | bytes 196
  128.3 22.3 %copy-start.37 = (f32[2,512]{1,0:T(2,128)S(1)}, f32[2,512]{1,0:T(2,128)}, u32[]{:S(2)}) copy-start(f32[2,512]{1,0:T(2,128)} %param.28) | copy-start | bytes 12292
  151.9 18.3 %all-to-all-start = ((f32[32,1,8]{2,1,0:T(1,128)}), f32[32,1,8]{2,1,0:T(1,128)S(1)}, u32[]{:S(2)}, u32[]{:S(2)}) async-start(f32[32,1,8]{2,1,0:T(1,128)} %broadcast_in_dim.64), calls=%async_computation | async-start | bytes 32768 | tf_op jit(solution)/shard_map/all_to_all | solution.py:25
  159.7 112.5 %reduce-scatter.3.cloned.1.call-start = ((), (), s32[]{:S(2)}) async-start(), calls=%async_computation.9 | async-start | bytes 5242880 | tf_op jit(solution)/shard_map/reduce_scatter | solution.py:163
  196.3 6.3 %copy-start.21 = (f32[8,128,8,64]{1,3,2,0:T(8,128)S(1)}, f32[8,128,8,64]{1,3,2,0:T(8,128)}, u32[]{:S(2)}) copy-start(f32[8,128,8,64]{1,3,2,0:T(8,128)} %copy.159) | copy-start | bytes 6291460
  196.3 6.3 %copy-start.42 = (f32[8]{0:T(128)S(1)}, f32[8]{0:T(128)}, u32[]{:S(2)}) copy-start(f32[8]{0:T(128)} %copy-done.41) | copy-start | bytes 100
  231.0 41.2 %copy-start.11 = (bf16[1024,512]{1,0:T(8,128)(2,1)S(1)}, bf16[1024,512]{1,0:T(8,128)(2,1)}, u32[]{:S(2)}) copy-start(bf16[1024,512]{1,0:T(8,128)(2,1)} %param.17) | copy-start | bytes 3145732
  283.4 24.8 %all-to-all-start.4 = ((bf16[16,2,1,32,512]{4,3,1,2,0:T(8,128)(2,1)}), bf16[16,2,1,32,512]{4,3,1,2,0:T(8,128)(2,1)S(1)}, u32[]{:S(2)}, u32[]{:S(2)}) async-start(bf16[16,2,1,32,512]{4,3,1,2,0:T(8,128)(2,1)} %copy.164), calls=%async_computation.5 | async-start | bytes 2097152 | tf_op jit(solution)/shard_map/all_to_all | solution.py:48
  290.4 67.2 %all-gather.12.cloned.1.call-start = ((), (), s32[]{:S(2)}) async-start(), calls=%async_computation.12 | async-start | bytes 5242880 | tf_op jit(solution)/shard_map/all_gather | solution.py:159
  313.3 176.7 %all-gather.14.cloned.1.call-start = ((), (), s32[]{:S(2)}) async-start(), calls=%async_computation.13 | async-start | bytes 4325376 | tf_op jit(solution)/shard_map/all_gather | solution.py:84
  313.5 47.3 %copy-start.49 = (bf16[2,2048,256]{2,1,0:T(8,128)(2,1)S(1)}, bf16[2,2048,256]{2,1,0:T(8,128)(2,1)}, u32[]{:S(2)}) copy-start(bf16[2,2048,256]{2,1,0:T(8,128)(2,1)} %param.21) | copy-start | bytes 6291460
  319.1 41.7 %copy-start.29 = (f32[1,2048]{1,0:T(1,128)S(1)}, f32[1,2048]{1,0:T(1,128)}, u32[]{:S(2)}) copy-start(f32[1,2048]{1,0:T(1,128)} %get-tuple-element.155) | copy-start | bytes 24580
  363.0 41.7 %collective-permute-start.3 = (bf16[3,256]{1,0:T(4,128)(2,1)}, bf16[3,256]{1,0:T(4,128)(2,1)}, u32[]{:S(2)}, u32[]{:S(2)}) collective-permute-start(bf16[3,256]{1,0:T(4,128)(2,1)} %slice.336), channel_id=1, source_target_pairs={{0,4},{4,8},{8,12},{12,16},{16,20},{20,24},{24,28},{28,32},{32,36}... | collective-permute-start | bytes 4616 | tf_op jit(solution)/shard_map/ppermute | solution.py:35
  401.3 6.1 %collective-permute-start.2 = (bf16[3,512]{1,0:T(4,128)(2,1)}, bf16[3,512]{1,0:T(4,128)(2,1)S(1)}, u32[]{:S(2)}, u32[]{:S(2)}) collective-permute-start(bf16[3,512]{1,0:T(4,128)(2,1)} %slice.330), channel_id=1, source_target_pairs={{0,4},{4,8},{8,12},{12,16},{16,20},{20,24},{24,28},{28,32},{32,36}... | collective-permute-start | bytes 9224 | tf_op jit(solution)/shard_map/ppermute | solution.py:35
  422.8 20.5 %copy-start.40 = (f32[8]{0:T(128)S(1)}, f32[8]{0:T(128)}, u32[]{:S(2)}) copy-start(f32[8]{0:T(128)} %get-tuple-element.169) | copy-start | bytes 100
  444.2 17.6 %all-to-all-start.5 = ((f32[32,1,8]{2,1,0:T(1,128)}), f32[32,1,8]{2,1,0:T(1,128)S(1)}, u32[]{:S(2)}, u32[]{:S(2)}) async-start(f32[32,1,8]{2,1,0:T(1,128)} %broadcast_in_dim.112), calls=%async_computation.6 | async-start | bytes 32768 | tf_op jit(solution)/shard_map/all_to_all | solution.py:25
  451.1 114.4 %reduce-scatter.5.cloned.1.call-start = ((), (), s32[]{:S(2)}) async-start(), calls=%async_computation.10 | async-start | bytes 5242880 | tf_op jit(solution)/shard_map/reduce_scatter | solution.py:163
  519.3 46.2 %copy-start = (bf16[1024,512]{1,0:T(8,128)(2,1)S(1)}, bf16[1024,512]{1,0:T(8,128)(2,1)}, u32[]{:S(2)}) copy-start(bf16[1024,512]{1,0:T(8,128)(2,1)} %gather_fusion.2) | copy-start | bytes 3145732
  (41 other events, 147.1 us)
Sparse Core Ops, SparseCore 0:
  9.0 50.6 all-gather.7
  148.9 47.3 all-gather.9
  226.1 46.0 reduce-scatter.2
  313.4 44.0 all-gather.11
  443.5 46.4 all-gather.13
  519.5 46.0 reduce-scatter.4
where the time goes:
time: 584 us; the launch traced here: 575 us
  waiting for transfers between devices  180 us (31%)
  other arithmetic  118 us (20%)
  local copies, waits for them, and re-layouts  110 us (19%)
  matrix products  97.5 us (17%)
  starting transfers between devices  34 us (6%)
  blocking collectives  20.6 us (4%)
  between operations  14.5 us (2%)
    all_gather x2, waiting for transfers between devices, spread_features(): return lax.all_gather(piece, 'tp', axis=1, tiled=True)  77.3 us
    reduce_scatter x2, waiting for transfers between devices, collect_heads(): lax.psum_scatter(partial_sum.astype(jnp.bfloat16), 'tp', scatter_dimensio...  63.3 us
    another operation x2, other arithmetic, mixer(): cumul = jnp.cumsum(log_blocks, axis=1)  46.6 us
    all_gather x2, waiting for transfers between devices, incoming_state(): lax.all_gather(local_end[None].astype(jnp.bfloat16), SEQ, axis=0, tiled=T...  25.4 us
    all_to_all x3, blocking collectives, moved_by_axis(): lax.all_to_all(blocks, axes[k], split_axis=k, concat_axis=k, tiled=True)  20.6 us
    dot_general x2, matrix products, mixer(): jnp.einsum('chqk,ckhp->cqhp', intersection[:, None] * jnp.exp(spread), fe...  19.3 us
    dot_general x2, matrix products, mixer(): jnp.dot(mixed_heads, w_out[which], preferred_element_type=jnp.float32)  16.9 us
    unnamed x111, local copies, waits for them, and re-layouts  16.7 us
  transfers between devices with their start and end apart: 13, of which 8 were waited for; matrix products, arithmetic and copies ran while one was open for 24% of the time, Pallas kernels for 0%

commit v1 on v0

v1 whole, which is shorter than its diff:
```python
import functools

import jax
import jax.numpy as jnp
from jax import lax
from jax.experimental import pallas as pl
from jax.experimental.pallas import tpu as pltpu
from jax.sharding import Mesh
from jax.sharding import PartitionSpec as P

HEAD_DIM = 64
STATE = 128
STRETCH = 128
HEADS = 8
LANES = 512
HALO = 16
BLOCK = 256
MSG = 144
SEQ = ("seq_0", "seq_1", "seq_2")
TP = 4
epsilon = 1e-05
f32 = jnp.float32
bf16 = jnp.bfloat16
NT = (((1,), (1,)), ((), ()))
TN = (((0,), (0,)), ((), ()))
VMEM_BYTES = 56 * 2**20


def dot(a, b, dims=None):
    dims = dims or (((1,), (0,)), ((), ()))
    return lax.dot_general(a, b, dims, preferred_element_type=f32)


def silu(x):
    return x / (1.0 + jnp.exp(-x))


def softplus(x):
    return jnp.maximum(x, 0.0) + jnp.log1p(jnp.exp(-jnp.abs(x)))


def spread_heads(values, fan):
    high = values.astype(bf16)
    low = (values - high.astype(f32)).astype(bf16)
    return dot(jnp.concatenate([high, low], axis=0), fan, TN)


def head_fan():
    row = lax.broadcasted_iota(jnp.int32, (2 * HEADS, LANES), 0)
    lane = lax.broadcasted_iota(jnp.int32, (2 * HEADS, LANES), 1)
    return (row % HEADS == lane // HEAD_DIM).astype(bf16)


def entry_kernel(first, last, rows, *refs):
    (order, own, left, right, opposite) = refs[:5]
    refs = refs[5:]
    if first:
        halos, refs = refs[:4], refs[4:]
    else:
        tail_in, state_in, total_in, refs = *refs[:3], refs[3:]
    (gain, w_any, wbc_any, wdt, taps, dt_bias, a_log), refs = refs[:7], refs[7:]
    (z_out, xc_out, b_out, c_out, cum_out, step_out, ent_out, pri_out), refs = refs[:8], refs[8:]
    if last:
        (msg_out,), refs = refs[:1], refs[1:]
    else:
        (tail_out, state_out, total_out), refs = refs[:3], refs[3:]
    wv, wbcv, nbuf, xbuf, sems = refs

    copies = []
    for p in range(4):
        source = pl.ds(pl.multiple_of(order[p] * 512, 512), 512)
        target = pl.ds(p * 512, 512)
        copies.append(pltpu.make_async_copy(w_any.at[source, :], wv.at[target, :], sems.at[0, p]))
        copies.append(
            pltpu.make_async_copy(wbc_any.at[source, :], wbcv.at[target, :], sems.at[1, p])
        )
    for c in copies:
        c.start()

    fan = head_fan()
    k_pos = lax.broadcasted_iota(jnp.int32, (STRETCH, STRETCH), 0)
    q_pos = lax.broadcasted_iota(jnp.int32, (STRETCH, STRETCH), 1)
    upto = (k_pos <= q_pos).astype(f32)
    lane = lax.broadcasted_iota(jnp.int32, (HEADS, STRETCH), 1)
    rate = jnp.exp(a_log[...])
    if first:
        state = jnp.zeros((STATE, LANES), f32)
        total = jnp.zeros((HEADS, 1), f32)
    else:
        state = state_in[...]
        total = total_in[:, 0:1]
        xbuf[0:HALO, :] = tail_in[...]
    waited = False
    for i in range(rows // BLOCK):
        span = pl.ds(i * BLOCK, BLOCK)
        pieces = [r[span, :] for r in (own, left, right, opposite)]
        widen = [x.astype(f32) for x in pieces]
        square = sum(jnp.sum(x * x, axis=1, keepdims=True) for x in widen)
        scale = lax.rsqrt(square * (1.0 / 2048) + epsilon)
        for p in range(4):
            nbuf[HALO : HALO + BLOCK, p * 512 : (p + 1) * 512] = (
                widen[p] * scale * gain[order[p]]
            ).astype(bf16)
        if first and i == 0:
            widen = [r[...].astype(f32) for r in halos]
            square = sum(jnp.sum(x * x, axis=1, keepdims=True) for x in widen)
            scale = lax.rsqrt(square * (1.0 / 2048) + epsilon)
            for p in range(4):
                nbuf[0:HALO, p * 512 : (p + 1) * 512] = (
                    widen[p] * scale * gain[order[p]]
                ).astype(bf16)
        if not waited:
            for c in copies:
                c.wait()
            waited = True
        low = 0 if first and i == 0 else HALO
        if low and i > 0:
            xbuf[0:HALO, :] = xbuf[BLOCK : BLOCK + HALO, :]
        normed = nbuf[low : HALO + BLOCK, :]
        xbuf[low : HALO + BLOCK, 0:LANES] = dot(normed, wv[:, 0:LANES]).astype(bf16).astype(f32)
        z_out[span, :] = dot(nbuf[HALO:, :], wv[:, LANES:]).astype(bf16)
        xbuf[low : HALO + BLOCK, LANES:] = dot(normed, wbcv[...]).astype(bf16).astype(f32)
        dt = sum(
            dot(wdt[order[p]], nbuf[HALO:, p * 512 : (p + 1) * 512], NT) for p in range(4)
        )
        mixed = jnp.zeros((BLOCK, LANES + 2 * STATE), f32)
        for k in range(4):
            mixed = mixed + taps[k : k + 1, :] * xbuf[pl.ds(HALO - 3 + k, BLOCK), :]
        mixed = silu(mixed)
        xc = mixed[:, 0:LANES]
        b = mixed[:, LANES : LANES + STATE].astype(bf16)
        xc_out[span, :] = xc.astype(bf16)
        b_out[span, :] = b
        c_out[span, :] = mixed[:, LANES + STATE :].astype(bf16)
        step = softplus(dt + dt_bias[...])
        decay = -step * rate
        step_out[:, i * BLOCK : (i + 1) * BLOCK] = step
        cums, marks = [], jnp.zeros((HEADS, STRETCH), f32)
        for j in range(2):
            part = decay[:, j * STRETCH : (j + 1) * STRETCH]
            cum = lax.dot_general(
                part,
                upto,
                (((1,), (0,)), ((), ())),
                preferred_element_type=f32,
                precision=lax.Precision.HIGHEST,
            )
            cum_out[:, i * BLOCK + j * STRETCH : i * BLOCK + (j + 1) * STRETCH] = cum
            end = cum[:, STRETCH - 1 : STRETCH]
            marks = jnp.where(lane == j, end, jnp.where(lane == 2 + j, total, marks))
            total = total + end
            cums.append((cum, end))
        marks = jnp.where(lane == 4, total, marks)
        marks = spread_heads(jnp.exp(marks), fan)
        for j in range(2):
            cum, end = cums[j]
            here = slice(j * STRETCH, (j + 1) * STRETCH)
            weight = spread_heads(step[:, here] * jnp.exp(end - cum), fan)
            fresh = dot(b[here, :], (xc[here, :] * weight).astype(bf16), TN)
            ent_out[2 * i + j] = state
            pri_out[2 * i + j] = marks[2 + j : 3 + j, :]
            state = state * marks[j : j + 1, :] + fresh
    if last:
        msg_out[0:STATE, :] = state.astype(bf16)
        decayed = marks[4:5, :]
        high = decayed.astype(bf16).astype(f32)
        row = lax.broadcasted_iota(jnp.int32, (MSG - STATE, LANES), 0)
        msg_out[STATE:MSG, :] = jnp.where(
            row == 0, high, jnp.where(row == 1, decayed - high, 0.0)
        ).astype(bf16)
    else:
        tail_out[...] = xbuf[BLOCK : BLOCK + HALO, :]
        state_out[...] = state
        total_out[...] = jnp.broadcast_to(total, (HEADS, STRETCH))


def vmem():
    return pl.BlockSpec(memory_space=pltpu.VMEM)


def smem():
    return pl.BlockSpec(memory_space=pltpu.SMEM)


def anywhere():
    return pl.BlockSpec(memory_space=pl.ANY)


def entry(order, pieces, halos, carry, gain, w, wbc, wdt, taps, dt_bias, a_log, last):
    rows = pieces[0].shape[0]
    first = carry is None
    shape = jax.ShapeDtypeStruct
    outs = [
        shape((rows, LANES), bf16),
        shape((rows, LANES), bf16),
        shape((rows, STATE), bf16),
        shape((rows, STATE), bf16),
        shape((HEADS, rows), f32),
        shape((HEADS, rows), f32),
        shape((rows // STRETCH, STATE, LANES), f32),
        shape((rows // STRETCH, 1, LANES), f32),
    ]
    if last:
        outs += [shape((MSG, LANES), bf16)]
    else:
        outs += [
            shape((HALO, LANES + 2 * STATE), f32),
            shape((STATE, LANES), f32),
            shape((HEADS, STRETCH), f32),
        ]
    extra = list(halos) if first else list(carry)
    operands = [order, *pieces, *extra, gain, w, wbc, wdt, taps, dt_bias, a_log]
    specs = [smem()] + [vmem()] * (4 + len(extra) + 1) + [anywhere()] * 2 + [vmem()] * 4
    return pl.pallas_call(
        functools.partial(entry_kernel, first, last, rows),
        out_shape=outs,
        in_specs=specs,
        out_specs=[vmem()] * len(outs),
        scratch_shapes=[
            pltpu.VMEM((2048, 2 * LANES), bf16),
            pltpu.VMEM((2048, 2 * STATE), bf16),
            pltpu.VMEM((HALO + BLOCK, 2048), bf16),
            pltpu.VMEM((HALO + BLOCK, LANES + 2 * STATE), f32),
            pltpu.SemaphoreType.DMA((2, 4)),
        ],
        compiler_params=pltpu.CompilerParams(vmem_limit_bytes=VMEM_BYTES),
        name="entry",
    )(*operands)


def inside_kernel(rows, xc, b, c, cum, step, skip, y_out):
    q_pos = lax.broadcasted_iota(jnp.int32, (STRETCH, STRETCH), 0)
    k_pos = lax.broadcasted_iota(jnp.int32, (STRETCH, STRETCH), 1)
    causal = k_pos <= q_pos
    low_half = k_pos < HEAD_DIM
    for j in range(rows // STRETCH):
        here = slice(j * STRETCH, (j + 1) * STRETCH)
        match = jnp.where(causal, dot(c[here, :], b[here, :], NT), 0.0)
        cum_rows = cum[:, here]
        step_rows = step[:, here]
        cum_cols = jnp.transpose(cum_rows)
        for pair in range(HEADS // 2):
            weights = []
            for h in (2 * pair, 2 * pair + 1):
                gap = jnp.minimum(cum_cols[:, h : h + 1] - cum_rows[h : h + 1, :], 0.0)
                weights.append((match * (jnp.exp(gap) * step_rows[h : h + 1, :])).astype(bf16))
            lanes = slice(pair * STRETCH, (pair + 1) * STRETCH)
            x = xc[here, lanes].astype(f32)
            stacked = jnp.concatenate(
                [jnp.where(low_half, x, 0.0), jnp.where(low_half, 0.0, x)], axis=0
            ).astype(bf16)
            y_out[here, lanes] = (
                dot(jnp.concatenate(weights, axis=1), stacked) + skip[:, lanes] * x
            )


def inside(xc, b, c, cum, step, skip):
    rows = xc.shape[0]
    return pl.pallas_call(
        functools.partial(inside_kernel, rows),
        out_shape=jax.ShapeDtypeStruct((rows, LANES), f32),
        in_specs=[vmem()] * 6,
        out_specs=vmem(),
        compiler_params=pltpu.CompilerParams(vmem_limit_bytes=VMEM_BYTES),
        name="inside",
    )(xc, b, c, cum, step, skip)


def exit_kernel(rows, order, arriving, y, z, c, cum, ent, pri, gain, w_any, *refs):
    outs, (wv, sems) = refs[:4], refs[4:]
    copies = []
    for p in range(4):
        source = pl.ds(pl.multiple_of(order[p] * 512, 512), 512)
        copies.append(pltpu.make_async_copy(w_any.at[:, source], wv.at[p], sems.at[p]))
    for k in copies:
        k.start()
    fan = head_fan()
    row = lax.broadcasted_iota(jnp.int32, (BLOCK, BLOCK), 0) // HEAD_DIM
    lane = lax.broadcasted_iota(jnp.int32, (BLOCK, BLOCK), 1) // HEAD_DIM
    same_head = (row == lane).astype(bf16)
    came = arriving[...]
    waited = False
    for i in range(rows // BLOCK):
        mixed = []
        for j in (2 * i, 2 * i + 1):
            here = slice(j * STRETCH, (j + 1) * STRETCH)
            entering = (ent[j] + pri[j] * came).astype(bf16)
            carried = dot(c[here, :], entering) * spread_heads(jnp.exp(cum[:, here]), fan)
            gated = (y[here, :] + carried) * silu(z[here, :].astype(f32))
            square = (gated * gated).astype(bf16)
            sums = jnp.concatenate(
                [dot(square[:, 0:BLOCK], same_head), dot(square[:, BLOCK:], same_head)], axis=1
            )
            scale = lax.rsqrt(sums * (1.0 / HEAD_DIM) + epsilon)
            mixed.append((gated * scale * gain[...]).astype(bf16))
        mixed = jnp.concatenate(mixed, axis=0)
        if not waited:
            for k in copies:
                k.wait()
            waited = True
        for p in range(4):
            outs[p][i * BLOCK : (i + 1) * BLOCK, :] = dot(mixed, wv[p]).astype(bf16)


def leave(order, arriving, y, z, c, cum, ent, pri, gain, w):
    rows = y.shape[0]
    return pl.pallas_call(
        functools.partial(exit_kernel, rows),
        out_shape=[jax.ShapeDtypeStruct((rows, LANES), bf16)] * 4,
        in_specs=[smem()] + [vmem()] * 8 + [anywhere()],
        out_specs=[vmem()] * 4,
        scratch_shapes=[pltpu.VMEM((4, LANES, LANES), bf16), pltpu.SemaphoreType.DMA((4,))],
        compiler_params=pltpu.CompilerParams(vmem_limit_bytes=VMEM_BYTES),
        name="leave",
    )(order, arriving, y, z, c, cum, ent, pri, gain, w)


def turned(by):
    return [(i, (i + by) % TP) for i in range(TP)]


def around(x, by):
    return lax.ppermute(x, "tp", turned(by))


def halo_from(shard, by):
    count = lax.axis_size(SEQ)
    pairs = [
        (s * TP + t, (s + 1) * TP + (t + by) % TP) for s in range(count - 1) for t in range(TP)
    ]
    return lax.ppermute(shard[-HALO:], SEQ + ("tp",), pairs)


def arriving_state(msg):
    core, y = lax.axis_index("seq_2"), lax.axis_index("seq_1")

    def opened(m):
        m = m.astype(f32)
        return m[:STATE], m[STATE : STATE + 1] + m[STATE + 1 : STATE + 2]

    def closed(state, decay):
        high = decay.astype(bf16).astype(f32)
        blank = jnp.zeros((MSG - STATE - 2, LANES), f32)
        return jnp.concatenate([state, high, decay - high, blank], axis=0).astype(bf16)

    def after(a, b):
        return b[0] + b[1] * a[0], a[1] * b[1]

    def chosen(pred, a, b):
        return jnp.where(pred, a[0], b[0]), jnp.where(pred, a[1], b[1])

    nothing = (jnp.zeros((STATE, LANES), f32), jnp.ones((1, LANES), f32))
    mine = opened(msg)
    other = opened(lax.ppermute(msg, "seq_2", [(0, 1), (1, 0)]))
    is_one = core == 1
    both = after(chosen(is_one, other, mine), chosen(is_one, mine, other))
    before_core = chosen(is_one, other, nothing)
    both_msg = closed(*both)
    ring = [both_msg] + [lax.ppermute(both_msg, "seq_1", turned(k)) for k in (1, 2, 3)]
    ring = [opened(m) for m in ring]
    row, before_y = nothing, nothing
    for at in range(4):
        here = ring[0]
        for k in range(1, 4):
            here = chosen((y - at) % 4 == k, ring[k], here)
        before_y = chosen(at < y, after(before_y, here), before_y)
        row = after(row, here)
    row_msg = closed(*row)
    before = nothing
    for k in (3, 2, 1):
        pairs = [(i, i + k) for i in range(4 - k)]
        before = after(before, opened(lax.ppermute(row_msg, "seq_0", pairs)))
    return after(after(before, before_y), before_core)[0]


def layer(shard, order, out_order, params):
    gain, w, wbc, wdt, taps, dt_bias, a_log, skip, out_gain, w_out = params
    halos = [halo_from(shard, by) for by in (0, 1, -1, 2)]
    half = shard.shape[0] // 2
    own = [shard[:half], shard[half:]]
    left = [around(own[0], 1), None]
    right = [around(own[0], -1), None]
    opposite = [around(left[0], 1), None]
    left[1], right[1] = around(own[1], 1), around(own[1], -1)
    opposite[1] = around(right[1], -1)
    carry = None
    kept = []
    for i in range(2):
        out = entry(
            order,
            (own[i], left[i], right[i], opposite[i]),
            halos,
            carry,
            gain,
            w,
            wbc,
            wdt,
            taps,
            dt_bias,
            a_log,
            i == 1,
        )
        kept.append(out[:8])
        carry = out[8:]
    arriving = arriving_state(carry[0])
    sums = []
    for i in range(2):
        z, xc, b, c, cum, step, ent, pri = kept[i]
        y = inside(xc, b, c, cum, step, skip)
        mine, plus, minus, opp = leave(out_order, arriving, y, z, c, cum, ent, pri, out_gain, w_out)
        quarter = half // 2
        from_left = around(opp[:quarter], 1)
        from_right = around(opp[quarter:], -1)
        up = jnp.concatenate(
            [(plus[:quarter].astype(f32) + from_left.astype(f32)).astype(bf16), plus[quarter:]], 0
        )
        down = jnp.concatenate(
            [minus[:quarter], (minus[quarter:].astype(f32) + from_right.astype(f32)).astype(bf16)],
            0,
        )
        up, down = around(up, 1), around(down, -1)
        sums.append(own[i].astype(f32) + mine.astype(f32) + up.astype(f32) + down.astype(f32))
    return jnp.concatenate(sums, axis=0).astype(bf16)


def permuted(x, source):
    pick = (source[:, None] == jnp.arange(x.shape[0])[None, :]).astype(bf16)
    return jnp.dot(pick, x, preferred_element_type=f32).astype(bf16)


def body(
    tokens,
    col_order,
    in_gain,
    w_in,
    w_bc,
    w_dt,
    conv_x,
    conv_bc,
    dt_bias,
    a_log,
    d_skip,
    out_gain,
    w_out,
):
    x = lax.axis_index("tp")
    order = jnp.stack([x, (x + 3) % TP, (x + 1) % TP, (x + 2) % TP]).astype(jnp.int32)
    out_order = jnp.stack([x, (x + 1) % TP, (x + 3) % TP, (x + 2) % TP]).astype(jnp.int32)

    def params(which):
        return (
            in_gain[which].reshape(TP, 1, 512),
            w_in[which].reshape(2048, 2 * LANES),
            w_bc[which],
            w_dt[which].T.reshape(HEADS, TP, 512).transpose(1, 0, 2),
            jnp.concatenate([conv_x[which], conv_bc[which]], axis=1),
            dt_bias[which].reshape(HEADS, 1),
            a_log[which].reshape(HEADS, 1),
            jnp.repeat(d_skip[which], HEAD_DIM).reshape(1, LANES),
            out_gain[which].reshape(1, LANES),
            w_out[which],
        )

    heads_of = col_order.reshape(16, 64)[:, 0]
    columns = lax.all_gather(heads_of % 512, SEQ, axis=0, tiled=True)
    upward = heads_of >= 512
    slot = jnp.arange(1024)
    give = (slot % 2) * 512 + columns[slot // 2]
    visit, along = slot // 64, slot % 64
    row = jnp.where(upward[visit], 63 - along, along)
    take = (row // 2) * 32 + visit * 2 + row % 2

    row_result = layer(tokens, order, out_order, params(0))
    payload = permuted(row_result, give).reshape(32, 32, 512)
    arrived = lax.all_to_all(payload, SEQ, 0, 0, tiled=True).reshape(1024, 512)
    own_rows = permuted(arrived, take)
    return layer(own_rows, order, out_order, params(1))


def solution(mesh):
    torus = Mesh(mesh.devices.reshape(4, 4, 2, mesh.shape["tp"]), ("seq_0", "seq_1", "seq_2", "tp"))
    return jax.shard_map(
        body,
        mesh=torus,
        in_specs=(
            P(SEQ, "tp"),
            P(SEQ),
            P(),
            P(None, None, None, "tp"),
            P(),
            P(None, None, "tp"),
            P(None, None, "tp"),
            P(),
            P(None, "tp"),
            P(None, "tp"),
            P(None, "tp"),
            P(None, "tp"),
            P(None, "tp", None),
        ),
        out_specs=P(SEQ, "tp"),
        check_vma=False,
    )
```

time: 584 us -> 393 us (0.67)
  matrix products: 97.5 us -> 3.59 us
  other arithmetic: 118 us -> 29.9 us
  waiting for transfers between devices: 180 us -> 92 us
  Pallas kernels: 0 us -> 80 us
  starting transfers between devices: 34 us -> 110 us
  local copies, waits for them, and re-layouts: 110 us -> 53.5 us
  between operations: 14.5 us -> 1.93 us
    all_gather x4 -> x0, waiting for transfers between devices: 103 us -> none  [the longest x2 77.3 us: spread_features(): return lax.all_gather(piece, 'tp', axis=1, tiled=True)]
    ppermute x4 -> x50, starting transfers between devices: 11.8 us -> 106 us  [the longest x28 44.6 us: around(): return lax.ppermute(x, 'tp', turned(by))]
    dot_general x20 -> x2, matrix products: 97.5 us -> 3.59 us  [permuted(): return jnp.dot(pick, x, preferred_element_type=f32).astype(bf16)]
    ppermute x4 -> x50, waiting for transfers between devices: 0.1 us -> 85.6 us  [the longest x28 38.6 us: around(): return lax.ppermute(x, 'tp', turned(by))]
    pallas_call x0 -> x12, Pallas kernels: none -> 80 us  [the longest x4 41.9 us: entry(): pl.pallas_call(functools.partial(entry_kernel, first, last, rows), out_sh...]
    reduce_scatter x2 -> x0, waiting for transfers between devices: 63.3 us -> none  [collect_heads(): lax.psum_scatter(partial_sum.astype(jnp.bfloat16), 'tp', scatter_dimensio...]
    another operation x6 -> x13, other arithmetic: 46.8 us -> 6.41 us  [the longest x2 46.6 us: mixer(): cumul = jnp.cumsum(log_blocks, axis=1)]
    reshape x10 -> x1, local copies, waits for them, and re-layouts: 29 us -> 0.07 us  [body(): heads_of = col_order.reshape(16, 64)[:, 0]]
  transfers between devices with their start and end apart: 13 -> 51, of which waited for: 8 -> 26; matrix products, arithmetic and copies ran while one was open for 24% -> 18% of each run, Pallas kernels for 0% -> 12%
where the time goes in v1:
time: 393 us; the launch traced here: 387 us
  starting transfers between devices  110 us (28%)
  waiting for transfers between devices  92 us (23%)
  Pallas kernels  80 us (20%)
  local copies, waits for them, and re-layouts  53.5 us (14%)
  other arithmetic  29.9 us (8%)
  blocking collectives  15.4 us (4%)
    ppermute x28, starting transfers between devices, around(): return lax.ppermute(x, 'tp', turned(by))  44.6 us
    pallas_call x4, Pallas kernels, entry(): pl.pallas_call(functools.partial(entry_kernel, first, last, rows), out_sh...  41.9 us
    ppermute x28, waiting for transfers between devices, around(): return lax.ppermute(x, 'tp', turned(by))  38.6 us
    ppermute x8, starting transfers between devices, halo_from(): return lax.ppermute(shard[-HALO:], SEQ + ('tp',), pairs)  24.9 us
    pallas_call x4, Pallas kernels, leave(): pl.pallas_call(functools.partial(exit_kernel, rows), out_shape=[jax.Shape...  24.5 us
    ppermute x8, waiting for transfers between devices, halo_from(): return lax.ppermute(shard[-HALO:], SEQ + ('tp',), pairs)  21.4 us
    ppermute x6, waiting for transfers between devices, arriving_state(): lax.ppermute(both_msg, 'seq_1', turned(k))  18 us
    ppermute x6, starting transfers between devices, arriving_state(): before = after(before, opened(lax.ppermute(row_msg, 'seq_0', pairs)))  16 us
  transfers between devices with their start and end apart: 51, of which 26 were waited for; matrix products, arithmetic and copies ran while one was open for 18% of the time, Pallas kernels for 12%

profile of v1, /device:TPU:0, one launch (start us, length us, event | category | flops | bytes accessed | tf_op | source)
XLA Modules:
  0.0 386.5 jit_solution(10305719254917753222)
XLA Ops:
  10.1 8.9 %fusion.58 = (bf16[1,2048,2,512]{3,2,1,0:T(2,128)(2,1)}, bf16[1,2048,2,512]{3,2,1,0:T(2,128)(2,1)}) fusion(bf16[2,2048,2,512]{3,2,1,0:T(2,128)(2,1)} %param.16), kind=kLoop, calls=%fused_computation.219 | loop fusion | bytes 16777216 | tf_op jit(solution)/shard_map/slice | solution.py:453
  35.7 6.7 %collective-permute-start.8 = (bf16[16,512]{1,0:T(8,128)(2,1)S(1)}, bf16[16,512]{1,0:T(8,128)(2,1)S(1)}, u32[]{:S(2)}, u32[]{:S(2)}) collective-permute-start(bf16[16,512]{1,0:T(8,128)(2,1)S(1)} %slice.330), channel_id=1, source_target_pairs={{0,7},{1,4},{2,5},{3,6},{4,11},{5,8},{6,9},{7,10},{8,15},{9,12},{1... | collective-permute-start | bytes 49160 | tf_op jit(solution)/shard_map/ppermute | solution.py:331
  56.3 10.4 %entry.4 = (bf16[512,512]{1,0:T(8,128)(2,1)}, bf16[512,512]{1,0:T(8,128)(2,1)}, bf16[512,128]{1,0:T(8,128)(2,1)}, bf16[512,128]{1,0:T(8,128)(2,1)}, f32[8,512]{1...) custom-call(s32[4]{0:T(128)} %add_add_fusion.1.refs_0_, ...), custom_call_target="tpu_custom_call" | custom-call | tf_op jit(solution)/shard_map/entry/pallas_call | solution.py:214
  66.8 10.6 %entry.5 = (bf16[512,512]{1,0:T(8,128)(2,1)}, bf16[512,512]{1,0:T(8,128)(2,1)}, bf16[512,128]{1,0:T(8,128)(2,1)}, bf16[512,128]{1,0:T(8,128)(2,1)}, f32[8,512]{1...) custom-call(s32[4]{0:T(128)} %add_add_fusion.1.refs_0_, ...), custom_call_target="tpu_custom_call" | custom-call | tf_op jit(solution)/shard_map/entry/pallas_call | solution.py:214
  81.8 7.9 %collective-permute-start.11 = (bf16[144,512]{1,0:T(8,128)(2,1)S(1)}, bf16[144,512]{1,0:T(8,128)(2,1)S(1)}, u32[]{:S(2)}, u32[]{:S(2)}) collective-permute-start(bf16[144,512]{1,0:T(8,128)(2,1)S(1)} %get-tuple-element.176), channel_id=1, source_target_pairs={{0,24},{8,0},{16,8},{24,16},{1,25},{9,1},{17,9},{25,17},{2,26},{10... | collective-permute-start | bytes 442376 | tf_op jit(solution)/shard_map/ppermute | solution.py:359
  90.6 5.5 %collective-permute-done.11 = bf16[144,512]{1,0:T(8,128)(2,1)S(1)} collective-permute-done((bf16[144,512]{1,0:T(8,128)(2,1)S(1)}, bf16[144,512]{1,0:T(8,128)(2,1)S(1)}, u32[]{:S(2)}, u32[]{:S(2)}) %collective-permute-start.11) | collective-permute-done | bytes 147488 | tf_op jit(solution)/shard_map/ppermute | solution.py:359
  119.9 6.1 %leave.5 = (bf16[512,512]{1,0:T(8,128)(2,1)}, bf16[512,512]{1,0:T(8,128)(2,1)}, bf16[512,512]{1,0:T(8,128)(2,1)}, bf16[512,512]{1,0:T(8,128)(2,1)}) custom-call(s32[4]{0:T(128)} %add_add_fusion.order, f32[128,512]{1,0:T(8,128)} %fusion.24.arriving, f32[512,512]{1,0:T(8,128)} %inside.5.y, bf16[512,512]{1,0:T(8,128)(2,1)} %get-tuple-element.82.z, ...), custom_call_target="tpu_custom_call" | custom-call | tf_op jit(solution)/shard_map/leave/pallas_call | solution.py:307
  130.2 15.4 %all-reduce = s32[512]{0:T(512)S(1)} all-reduce(s32[512]{0:T(512)S(1)} %fusion.47), channel_id=1, replica_groups=mesh['seq_0'=4,'seq_1'=4,'seq_2'=2,'tp'=4] {'seq_0','seq_1','seq_2'}, use_global_device_ids=true, to_apply=%add | all-reduce | flops 512 | bytes 4096
  151.3 6.2 %leave.4 = (bf16[512,512]{1,0:T(8,128)(2,1)}, bf16[512,512]{1,0:T(8,128)(2,1)}, bf16[512,512]{1,0:T(8,128)(2,1)}, bf16[512,512]{1,0:T(8,128)(2,1)}) custom-call(s32[4]{0:T(128)} %add_add_fusion.order, f32[128,512]{1,0:T(8,128)} %fusion.24.arriving, f32[512,512]{1,0:T(8,128)} %inside.4.y, bf16[512,512]{1,0:T(8,128)(2,1)} %get-tuple-element.70.z, ...), custom_call_target="tpu_custom_call" | custom-call | tf_op jit(solution)/shard_map/leave/pallas_call | solution.py:307
  174.6 6.9 %gather_fusion = s32[1024]{0:T(1024)S(1)} fusion(s32[512]{0:T(512)S(1)} %all-reduce, s32[1024]{0:T(1024)S(1)} %broadcast_clamp_fusion), kind=kCustom, calls=%fused_computation | custom fusion | bytes 12288 | tf_op jit(solution)/shard_map/gather | solution.py:468
  182.0 6.9 %collective-permute-done.18 = bf16[512,512]{1,0:T(8,128)(2,1)} collective-permute-done((bf16[512,512]{1,0:T(8,128)(2,1)}, bf16[512,512]{1,0:T(8,128)(2,1)}, u32[]{:S(2)}, u32[]{:S(2)}) %collective-permute-start.18) | collective-permute-done | bytes 524320 | tf_op jit(solution)/shard_map/ppermute | solution.py:323
  203.9 5.5 %fusion.27 = s32[1024]{0:T(1024)S(1)} fusion(pred[1024]{0:T(1024)(128)(4,1)S(1)} %compare_reduce_fusion, pred[1024]{0:T(1024)(128)(4,1)S(1)} %compare_reduce_fusion.1, pred[1024]{0:T(1024)(128)(4,1)S(1)} %compare_reduce_fusion.2, pred[1024]{0:T(1024)(128)(4,1)S(1)} %compare_reduce_fusion.3, pred[1024]{0:T(1024)(128)(4,1)S(1)} %compare_reduce_fusion.4, ...), kind=kLoop, calls=%fused_computation.108 | loop fusion | flops 47104 | bytes 14345 | tf_op jit(solution)/shard_map/add | solution.py:471
  209.4 6.4 %all-to-all-done = bf16[32,32,512]{2,1,0:T(8,128)(2,1)S(1)} async-done(((bf16[32,32,512]{2,1,0:T(8,128)(2,1)}), bf16[32,32,512]{2,1,0:T(8,128)(2,1)S(1)}, u32[]{:S(2)}, u32[]{:S(2)}) %all-to-all-start) | async-done | bytes 1048608 | tf_op jit(solution)/shard_map/all_to_all | solution.py:475
  222.4 10.2 %collective-permute-done.28.refs_2_ = bf16[512,512]{1,0:T(8,128)(2,1)S(1)} collective-permute-done((bf16[512,512]{1,0:T(8,128)(2,1)S(1)}, bf16[512,512]{1,0:T(8,128)(2,1)S(1)}, u32[]{:S(2)}, u32[]{:S(2)}) %collective-permute-start.28) | collective-permute-done | bytes 524320 | tf_op jit(solution)/shard_map/ppermute | solution.py:323
  240.8 14.4 %collective-permute-done.32.refs_6_ = bf16[16,512]{1,0:T(8,128)(2,1)S(1)} collective-permute-done((bf16[16,512]{1,0:T(8,128)(2,1)S(1)}, bf16[16,512]{1,0:T(8,128)(2,1)S(1)}, u32[]{:S(2)}, u32[]{:S(2)}) %collective-permute-start.32) | collective-permute-done | bytes 16416 | tf_op jit(solution)/shard_map/ppermute | solution.py:331
  255.3 5.4 %collective-permute-start.33 = (bf16[16,512]{1,0:T(8,128)(2,1)S(1)}, bf16[16,512]{1,0:T(8,128)(2,1)S(1)}, u32[]{:S(2)}, u32[]{:S(2)}) collective-permute-start(bf16[16,512]{1,0:T(8,128)(2,1)S(1)} %slice.483), channel_id=1, source_target_pairs={{0,7},{1,4},{2,5},{3,6},{4,11},{5,8},{6,9},{7,10},{8,15},{9,12},{1... | collective-permute-start | bytes 49160 | tf_op jit(solution)/shard_map/ppermute | solution.py:331
  271.0 10.4 %entry.6 = (bf16[512,512]{1,0:T(8,128)(2,1)}, bf16[512,512]{1,0:T(8,128)(2,1)}, bf16[512,128]{1,0:T(8,128)(2,1)}, bf16[512,128]{1,0:T(8,128)(2,1)}, f32[8,512]{1...) custom-call(s32[4]{0:T(128)} %add_add_fusion.1.refs_0_, ...), custom_call_target="tpu_custom_call" | custom-call | tf_op jit(solution)/shard_map/entry/pallas_call | solution.py:214
  281.4 10.6 %entry.7 = (bf16[512,512]{1,0:T(8,128)(2,1)}, bf16[512,512]{1,0:T(8,128)(2,1)}, bf16[512,128]{1,0:T(8,128)(2,1)}, bf16[512,128]{1,0:T(8,128)(2,1)}, f32[8,512]{1...) custom-call(s32[4]{0:T(128)} %add_add_fusion.1.refs_0_, ...), custom_call_target="tpu_custom_call" | custom-call | tf_op jit(solution)/shard_map/entry/pallas_call | solution.py:214
  295.5 6.2 %collective-permute-start.36 = (bf16[144,512]{1,0:T(8,128)(2,1)S(1)}, bf16[144,512]{1,0:T(8,128)(2,1)S(1)}, u32[]{:S(2)}, u32[]{:S(2)}) collective-permute-start(bf16[144,512]{1,0:T(8,128)(2,1)S(1)} %get-tuple-element.174), channel_id=1, source_target_pairs={{0,24},{8,0},{16,8},{24,16},{1,25},{9,1},{17,9},{25,17},{2,26},{10... | collective-permute-start | bytes 442376 | tf_op jit(solution)/shard_map/ppermute | solution.py:359
  302.6 5.8 %collective-permute-done.36 = bf16[144,512]{1,0:T(8,128)(2,1)S(1)} collective-permute-done((bf16[144,512]{1,0:T(8,128)(2,1)S(1)}, bf16[144,512]{1,0:T(8,128)(2,1)S(1)}, u32[]{:S(2)}, u32[]{:S(2)}) %collective-permute-start.36) | collective-permute-done | bytes 147488 | tf_op jit(solution)/shard_map/ppermute | solution.py:359
  328.4 6.1 %leave.7 = (bf16[512,512]{1,0:T(8,128)(2,1)}, bf16[512,512]{1,0:T(8,128)(2,1)}, bf16[512,512]{1,0:T(8,128)(2,1)}, bf16[512,512]{1,0:T(8,128)(2,1)}) custom-call(s32[4]{0:T(128)} %add_add_fusion.order, f32[128,512]{1,0:T(8,128)} %fusion.16.arriving, f32[512,512]{1,0:T(8,128)} %inside.7.y, bf16[512,512]{1,0:T(8,128)(2,1)} %get-tuple-element.110.z, ...), custom_call_target="tpu_custom_call" | custom-call | tf_op jit(solution)/shard_map/leave/pallas_call | solution.py:307
  344.3 6.1 %leave.6 = (bf16[512,512]{1,0:T(8,128)(2,1)}, bf16[512,512]{1,0:T(8,128)(2,1)}, bf16[512,512]{1,0:T(8,128)(2,1)}, bf16[512,512]{1,0:T(8,128)(2,1)}) custom-call(s32[4]{0:T(128)} %add_add_fusion.order, f32[128,512]{1,0:T(8,128)} %fusion.16.arriving, f32[512,512]{1,0:T(8,128)} %inside.6.y, bf16[512,512]{1,0:T(8,128)(2,1)} %get-tuple-element.98.z, ...), custom_call_target="tpu_custom_call" | custom-call | tf_op jit(solution)/shard_map/leave/pallas_call | solution.py:307
  367.2 7.1 %collective-permute-done.47 = bf16[512,512]{1,0:T(8,128)(2,1)S(1)} collective-permute-done((bf16[512,512]{1,0:T(8,128)(2,1)}, bf16[512,512]{1,0:T(8,128)(2,1)S(1)}, u32[]{:S(2)}, u32[]{:S(2)}) %collective-permute-start.47) | collective-permute-done | bytes 524320 | tf_op jit(solution)/shard_map/ppermute | solution.py:323
  374.9 8.4 %collective-permute-done.43 = bf16[512,512]{1,0:T(8,128)(2,1)} collective-permute-done((bf16[512,512]{1,0:T(8,128)(2,1)}, bf16[512,512]{1,0:T(8,128)(2,1)}, u32[]{:S(2)}, u32[]{:S(2)}) %collective-permute-start.43) | collective-permute-done | bytes 524320 | tf_op jit(solution)/shard_map/ppermute | solution.py:323
  (305 shorter events, 190.5 us)
Async XLA Ops:
  1.3 22.7 %collective-permute-start.3 = (bf16[512,512]{1,0:T(8,128)(2,1)S(1)}, bf16[512,512]{1,0:T(8,128)(2,1)S(1)}, u32[]{:S(2)}, u32[]{:S(2)}) collective-permute-start(bf16[512,512]{1,0:T(8,128)(2,1)S(1)} %get-tuple-element.163.refs_1_), channel_id=1, source_target_pairs={{0,1},{1,2},{2,3},{3,0},{4,5},{5,6},{6,7},{7,4},{8,9},{9,10},{10,1... | collective-permute-start | bytes 1572872 | tf_op jit(solution)/shard_map/ppermute | solution.py:323
  2.9 52.4 %collective-permute-start.4 = (bf16[512,512]{1,0:T(8,128)(2,1)S(1)}, bf16[512,512]{1,0:T(8,128)(2,1)S(1)}, u32[]{:S(2)}, u32[]{:S(2)}) collective-permute-start(bf16[512,512]{1,0:T(8,128)(2,1)S(1)} %get-tuple-element.163.refs_1_), channel_id=1, source_target_pairs={{0,3},{1,0},{2,1},{3,2},{4,7},{5,4},{6,5},{7,6},{8,11},{9,8},{10,9... | collective-permute-start | bytes 1572872 | tf_op jit(solution)/shard_map/ppermute | solution.py:323
  4.6 23.0 %collective-permute-start.1 = (bf16[512,512]{1,0:T(8,128)(2,1)S(1)}, bf16[512,512]{1,0:T(8,128)(2,1)S(1)}, u32[]{:S(2)}, u32[]{:S(2)}) collective-permute-start(bf16[512,512]{1,0:T(8,128)(2,1)S(1)} %get-tuple-element.164.refs_1_), channel_id=1, source_target_pairs={{0,3},{1,0},{2,1},{3,2},{4,7},{5,4},{6,5},{7,6},{8,11},{9,8},{10,9... | collective-permute-start | bytes 1572872 | tf_op jit(solution)/shard_map/ppermute | solution.py:323
  6.2 60.5 %collective-permute-start = (bf16[512,512]{1,0:T(8,128)(2,1)S(1)}, bf16[512,512]{1,0:T(8,128)(2,1)}, u32[]{:S(2)}, u32[]{:S(2)}) collective-permute-start(bf16[512,512]{1,0:T(8,128)(2,1)S(1)} %get-tuple-element.164.refs_1_), channel_id=1, source_target_pairs={{0,1},{1,2},{2,3},{3,0},{4,5},{5,6},{6,7},{7,4},{8,9},{9,10},{10,1... | collective-permute-start | bytes 1572872 | tf_op jit(solution)/shard_map/ppermute | solution.py:323
  7.3 23.1 %collective-permute-start.6 = (bf16[16,512]{1,0:T(8,128)(2,1)S(1)}, bf16[16,512]{1,0:T(8,128)(2,1)S(1)}, u32[]{:S(2)}, u32[]{:S(2)}) collective-permute-start(bf16[16,512]{1,0:T(8,128)(2,1)S(1)} %slice.330), channel_id=1, source_target_pairs={{0,4},{1,5},{2,6},{3,7},{4,8},{5,9},{6,10},{7,11},{8,12},{9,13},{1... | collective-permute-start | bytes 49160 | tf_op jit(solution)/shard_map/ppermute | solution.py:331
  24.0 31.4 %collective-permute-start.5 = (bf16[512,512]{1,0:T(8,128)(2,1)S(1)}, bf16[512,512]{1,0:T(8,128)(2,1)S(1)}, u32[]{:S(2)}, u32[]{:S(2)}) collective-permute-start(bf16[512,512]{1,0:T(8,128)(2,1)S(1)} %collective-permute-done.3.refs_2_), channel_id=1, source_target_pairs={{0,1},{1,2},{2,3},{3,0},{4,5},{5,6},{6,7},{7,4},{8,9},{9,10},{10,1... | collective-permute-start | bytes 1572872 | tf_op jit(solution)/shard_map/ppermute | solution.py:323
  27.6 39.2 %collective-permute-start.2 = (bf16[512,512]{1,0:T(8,128)(2,1)S(1)}, bf16[512,512]{1,0:T(8,128)(2,1)}, u32[]{:S(2)}, u32[]{:S(2)}) collective-permute-start(bf16[512,512]{1,0:T(8,128)(2,1)S(1)} %collective-permute-done.1.refs_3_), channel_id=1, source_target_pairs={{0,3},{1,0},{2,1},{3,2},{4,7},{5,4},{6,5},{7,6},{8,11},{9,8},{10,9... | collective-permute-start | bytes 1572872 | tf_op jit(solution)/shard_map/ppermute | solution.py:323
  127.0 37.0 %collective-permute-start.21 = (bf16[256,512]{1,0:T(8,128)(2,1)S(1)}, bf16[256,512]{1,0:T(8,128)(2,1)S(1)}, u32[]{:S(2)}, u32[]{:S(2)}) collective-permute-start(bf16[256,512]{1,0:T(8,128)(2,1)S(1)} %get-tuple-element.171), channel_id=1, source_target_pairs={{0,1},{1,2},{2,3},{3,0},{4,5},{5,6},{6,7},{7,4},{8,9},{9,10},{10,1... | collective-permute-start | bytes 786440 | tf_op jit(solution)/shard_map/ppermute | solution.py:323
  165.0 16.5 %collective-permute-start.22 = (bf16[512,512]{1,0:T(8,128)(2,1)}, bf16[512,512]{1,0:T(8,128)(2,1)S(1)}, u32[]{:S(2)}, u32[]{:S(2)}) collective-permute-start(bf16[512,512]{1,0:T(8,128)(2,1)} %pad_maximum_fusion.3), channel_id=1, source_target_pairs={{0,1},{1,2},{2,3},{3,0},{4,5},{5,6},{6,7},{7,4},{8,9},{9,10},{10,1... | collective-permute-start | bytes 1572872 | tf_op jit(solution)/shard_map/ppermute | solution.py:323
  170.0 18.9 %collective-permute-start.18 = (bf16[512,512]{1,0:T(8,128)(2,1)}, bf16[512,512]{1,0:T(8,128)(2,1)}, u32[]{:S(2)}, u32[]{:S(2)}) collective-permute-start(bf16[512,512]{1,0:T(8,128)(2,1)} %pad_maximum_fusion.1), channel_id=1, source_target_pairs={{0,1},{1,2},{2,3},{3,0},{4,5},{5,6},{6,7},{7,4},{8,9},{9,10},{10,1... | collective-permute-start | bytes 1572872 | tf_op jit(solution)/shard_map/ppermute | solution.py:323
  171.7 18.7 %collective-permute-start.20 = (bf16[512,512]{1,0:T(8,128)(2,1)}, bf16[512,512]{1,0:T(8,128)(2,1)}, u32[]{:S(2)}, u32[]{:S(2)}) collective-permute-start(bf16[512,512]{1,0:T(8,128)(2,1)} %pad_maximum_fusion.2), channel_id=1, source_target_pairs={{0,3},{1,0},{2,1},{3,2},{4,7},{5,4},{6,5},{7,6},{8,11},{9,8},{10,9... | collective-permute-start | bytes 1572872 | tf_op jit(solution)/shard_map/ppermute | solution.py:323
  194.5 21.4 %all-to-all-start = ((bf16[32,32,512]{2,1,0:T(8,128)(2,1)}), bf16[32,32,512]{2,1,0:T(8,128)(2,1)S(1)}, u32[]{:S(2)}, u32[]{:S(2)}) async-start(bf16[32,32,512]{2,1,0:T(8,128)(2,1)} %bitcast.44), calls=%async_computation | async-start | bytes 2097152 | tf_op jit(solution)/shard_map/all_to_all | solution.py:475
  217.6 15.6 %collective-permute-start.26 = (bf16[512,512]{1,0:T(8,128)(2,1)S(1)}, bf16[512,512]{1,0:T(8,128)(2,1)}, u32[]{:S(2)}, u32[]{:S(2)}) collective-permute-start(bf16[512,512]{1,0:T(8,128)(2,1)S(1)} %get-tuple-element.160.refs_1_), channel_id=1, source_target_pairs={{0,3},{1,0},{2,1},{3,2},{4,7},{5,4},{6,5},{7,6},{8,11},{9,8},{10,9... | collective-permute-start | bytes 1572872 | tf_op jit(solution)/shard_map/ppermute | solution.py:323
  220.5 49.7 %collective-permute-start.29 = (bf16[512,512]{1,0:T(8,128)(2,1)S(1)}, bf16[512,512]{1,0:T(8,128)(2,1)S(1)}, u32[]{:S(2)}, u32[]{:S(2)}) collective-permute-start(bf16[512,512]{1,0:T(8,128)(2,1)S(1)} %get-tuple-element.159.refs_1_), channel_id=1, source_target_pairs={{0,3},{1,0},{2,1},{3,2},{4,7},{5,4},{6,5},{7,6},{8,11},{9,8},{10,9... | collective-permute-start | bytes 1572872 | tf_op jit(solution)/shard_map/ppermute | solution.py:323
  232.6 37.6 %collective-permute-start.30 = (bf16[512,512]{1,0:T(8,128)(2,1)S(1)}, bf16[512,512]{1,0:T(8,128)(2,1)}, u32[]{:S(2)}, u32[]{:S(2)}) collective-permute-start(bf16[512,512]{1,0:T(8,128)(2,1)S(1)} %collective-permute-done.28.refs_2_), channel_id=1, source_target_pairs={{0,1},{1,2},{2,3},{3,0},{4,5},{5,6},{6,7},{7,4},{8,9},{9,10},{10,1... | collective-permute-start | bytes 1572872 | tf_op jit(solution)/shard_map/ppermute | solution.py:323
  232.6 48.8 %collective-permute-start.25 = (bf16[512,512]{1,0:T(8,128)(2,1)S(1)}, bf16[512,512]{1,0:T(8,128)(2,1)}, u32[]{:S(2)}, u32[]{:S(2)}) collective-permute-start(bf16[512,512]{1,0:T(8,128)(2,1)S(1)} %get-tuple-element.160.refs_1_), channel_id=1, source_target_pairs={{0,1},{1,2},{2,3},{3,0},{4,5},{5,6},{6,7},{7,4},{8,9},{9,10},{10,1... | collective-permute-start | bytes 1572872 | tf_op jit(solution)/shard_map/ppermute | solution.py:323
  233.3 48.1 %collective-permute-start.27 = (bf16[512,512]{1,0:T(8,128)(2,1)}, bf16[512,512]{1,0:T(8,128)(2,1)}, u32[]{:S(2)}, u32[]{:S(2)}) collective-permute-start(bf16[512,512]{1,0:T(8,128)(2,1)} %collective-permute-done.26.refs_3_), channel_id=1, source_target_pairs={{0,3},{1,0},{2,1},{3,2},{4,7},{5,4},{6,5},{7,6},{8,11},{9,8},{10,9... | collective-permute-start | bytes 1572872 | tf_op jit(solution)/shard_map/ppermute | solution.py:323
  238.8 16.5 %collective-permute-start.32 = (bf16[16,512]{1,0:T(8,128)(2,1)S(1)}, bf16[16,512]{1,0:T(8,128)(2,1)S(1)}, u32[]{:S(2)}, u32[]{:S(2)}) collective-permute-start(bf16[16,512]{1,0:T(8,128)(2,1)S(1)} %slice.483), channel_id=1, source_target_pairs={{0,5},{1,6},{2,7},{3,4},{4,9},{5,10},{6,11},{7,8},{8,13},{9,14},{1... | collective-permute-start | bytes 49160 | tf_op jit(solution)/shard_map/ppermute | solution.py:331
  335.6 21.5 %collective-permute-start.46 = (bf16[256,512]{1,0:T(8,128)(2,1)S(1)}, bf16[256,512]{1,0:T(8,128)(2,1)S(1)}, u32[]{:S(2)}, u32[]{:S(2)}) collective-permute-start(bf16[256,512]{1,0:T(8,128)(2,1)S(1)} %get-tuple-element.167), channel_id=1, source_target_pairs={{0,1},{1,2},{2,3},{3,0},{4,5},{5,6},{6,7},{7,4},{8,9},{9,10},{10,1... | collective-permute-start | bytes 786440 | tf_op jit(solution)/shard_map/ppermute | solution.py:323
  342.0 16.1 %collective-permute-start.48 = (bf16[256,512]{1,0:T(8,128)(2,1)S(1)}, bf16[256,512]{1,0:T(8,128)(2,1)S(1)}, u32[]{:S(2)}, u32[]{:S(2)}) collective-permute-start(bf16[256,512]{1,0:T(8,128)(2,1)S(1)} %get-tuple-element.168), channel_id=1, source_target_pairs={{0,3},{1,0},{2,1},{3,2},{4,7},{5,4},{6,5},{7,6},{8,11},{9,8},{10,9... | collective-permute-start | bytes 786440 | tf_op jit(solution)/shard_map/ppermute | solution.py:323
  358.0 16.3 %collective-permute-start.47 = (bf16[512,512]{1,0:T(8,128)(2,1)}, bf16[512,512]{1,0:T(8,128)(2,1)S(1)}, u32[]{:S(2)}, u32[]{:S(2)}) collective-permute-start(bf16[512,512]{1,0:T(8,128)(2,1)} %pad_maximum_fusion.7), channel_id=1, source_target_pairs={{0,1},{1,2},{2,3},{3,0},{4,5},{5,6},{6,7},{7,4},{8,9},{9,10},{10,1... | collective-permute-start | bytes 1572872 | tf_op jit(solution)/shard_map/ppermute | solution.py:323
  359.0 15.9 %collective-permute-start.49 = (bf16[512,512]{1,0:T(8,128)(2,1)}, bf16[512,512]{1,0:T(8,128)(2,1)S(1)}, u32[]{:S(2)}, u32[]{:S(2)}) collective-permute-start(bf16[512,512]{1,0:T(8,128)(2,1)} %pad_maximum_fusion.8), channel_id=1, source_target_pairs={{0,3},{1,0},{2,1},{3,2},{4,7},{5,4},{6,5},{7,6},{8,11},{9,8},{10,9... | collective-permute-start | bytes 1572872 | tf_op jit(solution)/shard_map/ppermute | solution.py:323
  363.1 20.2 %collective-permute-start.43 = (bf16[512,512]{1,0:T(8,128)(2,1)}, bf16[512,512]{1,0:T(8,128)(2,1)}, u32[]{:S(2)}, u32[]{:S(2)}) collective-permute-start(bf16[512,512]{1,0:T(8,128)(2,1)} %pad_maximum_fusion.5), channel_id=1, source_target_pairs={{0,1},{1,2},{2,3},{3,0},{4,5},{5,6},{6,7},{7,4},{8,9},{9,10},{10,1... | collective-permute-start | bytes 1572872 | tf_op jit(solution)/shard_map/ppermute | solution.py:323
  364.0 19.5 %collective-permute-start.45 = (bf16[512,512]{1,0:T(8,128)(2,1)}, bf16[512,512]{1,0:T(8,128)(2,1)}, u32[]{:S(2)}, u32[]{:S(2)}) collective-permute-start(bf16[512,512]{1,0:T(8,128)(2,1)} %pad_maximum_fusion.6), channel_id=1, source_target_pairs={{0,3},{1,0},{2,1},{3,2},{4,7},{5,4},{6,5},{7,6},{8,11},{9,8},{10,9... | collective-permute-start | bytes 1572872 | tf_op jit(solution)/shard_map/ppermute | solution.py:323
  (69 other events, 1019.1 us)

commit v2 on v1

--- a/solution.py
+++ b/solution.py
@@ -13,6 +13,7 @@
 STRETCH = 128
 HEADS = 8
 LANES = 512
+HALF = 256
 HALO = 16
 BLOCK = 256
 MSG = 144
@@ -23,7 +24,7 @@
 bf16 = jnp.bfloat16
 NT = (((1,), (1,)), ((), ()))
 TN = (((0,), (0,)), ((), ()))
-VMEM_BYTES = 56 * 2**20
+VMEM_BYTES = 18 * 2**20
 
 
 def dot(a, b, dims=None):
@@ -45,23 +46,46 @@
     return dot(jnp.concatenate([high, low], axis=0), fan, TN)
 
 
+def packed(state, decay):
+    high = decay.astype(bf16).astype(f32)
+    row = lax.broadcasted_iota(jnp.int32, (MSG - STATE, decay.shape[1]), 0)
+    rest = jnp.where(row == 0, high, jnp.where(row == 1, decay - high, 0.0))
+    return jnp.concatenate([state, rest], axis=0)
+
+
+def opened(msg):
+    msg = msg[...].astype(f32)
+    return msg[:STATE], msg[STATE : STATE + 1] + msg[STATE + 1 : STATE + 2]
+
+
+def after(a, b):
+    return b[0] + b[1] * a[0], a[1] * b[1]
+
+
+def chosen(pred, a, b):
+    return jnp.where(pred, a[0], b[0]), jnp.where(pred, a[1], b[1])
+
+
+def nothing():
+    return jnp.zeros((STATE, HALF), f32), jnp.ones((1, HALF), f32)
+
+
 def head_fan():
     row = lax.broadcasted_iota(jnp.int32, (2 * HEADS, LANES), 0)
     lane = lax.broadcasted_iota(jnp.int32, (2 * HEADS, LANES), 1)
     return (row % HEADS == lane // HEAD_DIM).astype(bf16)
 
 
-def entry_kernel(first, last, rows, *refs):
+def entry_kernel(which, first, last, rows, *refs):
     (order, own, left, right, opposite) = refs[:5]
     refs = refs[5:]
-    if first:
-        halos, refs = refs[:4], refs[4:]
-    else:
+    ahead = HALO if first else 0
+    if not first:
         tail_in, state_in, total_in, refs = *refs[:3], refs[3:]
     (gain, w_any, wbc_any, wdt, taps, dt_bias, a_log), refs = refs[:7], refs[7:]
     (z_out, xc_out, b_out, c_out, cum_out, step_out, ent_out, pri_out), refs = refs[:8], refs[8:]
     if last:
-        (msg_out,), refs = refs[:1], refs[1:]
+        (keep_out, send_out), refs = refs[:2], refs[2:]
     else:
         (tail_out, state_out, total_out), refs = refs[:3], refs[3:]
     wv, wbcv, nbuf, xbuf, sems = refs
@@ -70,9 +94,11 @@
     for p in range(4):
         source = pl.ds(pl.multiple_of(order[p] * 512, 512), 512)
         target = pl.ds(p * 512, 512)
-        copies.append(pltpu.make_async_copy(w_any.at[source, :], wv.at[target, :], sems.at[0, p]))
+        copies.append(pltpu.make_async_copy(w_any.at[which, source, :], wv.at[target, :], sems.at[0, p]))
         copies.append(
-            pltpu.make_async_copy(wbc_any.at[source, :], wbcv.at[target, :], sems.at[1, p])
+            pltpu.make_async_copy(
+                wbc_any.at[which, source, :], wbcv.at[target, :], sems.at[1, p]
+            )
         )
     for c in copies:
         c.start()
@@ -93,7 +119,8 @@
     waited = False
     for i in range(rows // BLOCK):
         span = pl.ds(i * BLOCK, BLOCK)
-        pieces = [r[span, :] for r in (own, left, right, opposite)]
+        above = pl.ds(ahead + i * BLOCK, BLOCK)
+        pieces = [r[above, :] for r in (own, left, right, opposite)]
         widen = [x.astype(f32) for x in pieces]
         square = sum(jnp.sum(x * x, axis=1, keepdims=True) for x in widen)
         scale = lax.rsqrt(square * (1.0 / 2048) + epsilon)
@@ -102,7 +129,7 @@
                 widen[p] * scale * gain[order[p]]
             ).astype(bf16)
         if first and i == 0:
-            widen = [r[...].astype(f32) for r in halos]
+            widen = [r[0:HALO, :].astype(f32) for r in (own, left, right, opposite)]
             square = sum(jnp.sum(x * x, axis=1, keepdims=True) for x in widen)
             scale = lax.rsqrt(square * (1.0 / 2048) + epsilon)
             for p in range(4):
@@ -161,13 +188,11 @@
             pri_out[2 * i + j] = marks[2 + j : 3 + j, :]
             state = state * marks[j : j + 1, :] + fresh
     if last:
-        msg_out[0:STATE, :] = state.astype(bf16)
-        decayed = marks[4:5, :]
-        high = decayed.astype(bf16).astype(f32)
-        row = lax.broadcasted_iota(jnp.int32, (MSG - STATE, LANES), 0)
-        msg_out[STATE:MSG, :] = jnp.where(
-            row == 0, high, jnp.where(row == 1, decayed - high, 0.0)
-        ).astype(bf16)
+        whole = packed(state, marks[4:5, :])
+        near, far = whole[:, 0:HALF], whole[:, HALF:]
+        even = order[4] == 0
+        keep_out[...] = jnp.where(even, near, far).astype(bf16)
+        send_out[...] = jnp.where(even, far, near).astype(bf16)
     else:
         tail_out[...] = xbuf[BLOCK : BLOCK + HALO, :]
         state_out[...] = state
@@ -186,9 +211,9 @@
     return pl.BlockSpec(memory_space=pl.ANY)
 
 
-def entry(order, pieces, halos, carry, gain, w, wbc, wdt, taps, dt_bias, a_log, last):
-    rows = pieces[0].shape[0]
+def entry(which, order, pieces, carry, gain, w, wbc, wdt, taps, dt_bias, a_log, last):
     first = carry is None
+    rows = pieces[0].shape[0] - (HALO if first else 0)
     shape = jax.ShapeDtypeStruct
     outs = [
         shape((rows, LANES), bf16),
@@ -201,18 +226,18 @@
         shape((rows // STRETCH, 1, LANES), f32),
     ]
     if last:
-        outs += [shape((MSG, LANES), bf16)]
+        outs += [shape((MSG, HALF), bf16)] * 2
     else:
         outs += [
             shape((HALO, LANES + 2 * STATE), f32),
             shape((STATE, LANES), f32),
             shape((HEADS, STRETCH), f32),
         ]
-    extra = list(halos) if first else list(carry)
+    extra = [] if first else list(carry)
     operands = [order, *pieces, *extra, gain, w, wbc, wdt, taps, dt_bias, a_log]
     specs = [smem()] + [vmem()] * (4 + len(extra) + 1) + [anywhere()] * 2 + [vmem()] * 4
     return pl.pallas_call(
-        functools.partial(entry_kernel, first, last, rows),
+        functools.partial(entry_kernel, which, first, last, rows),
         out_shape=outs,
         in_specs=specs,
         out_specs=[vmem()] * len(outs),
@@ -266,19 +291,22 @@
     )(xc, b, c, cum, step, skip)
 
 
-def exit_kernel(rows, order, arriving, y, z, c, cum, ent, pri, gain, w_any, *refs):
-    outs, (wv, sems) = refs[:4], refs[4:]
+def exit_kernel(which, rows, order, mine, other, y, z, c, cum, ent, pri, gain, w_any, *refs):
+    (own, plus_a, plus_b, minus_a, minus_b, opp_a, opp_b), (wv, sems) = refs[:7], refs[7:]
+    outs = ((own, own), (plus_a, plus_b), (minus_a, minus_b), (opp_a, opp_b))
     copies = []
     for p in range(4):
         source = pl.ds(pl.multiple_of(order[p] * 512, 512), 512)
-        copies.append(pltpu.make_async_copy(w_any.at[:, source], wv.at[p], sems.at[p]))
+        copies.append(pltpu.make_async_copy(w_any.at[which, :, source], wv.at[p], sems.at[p]))
     for k in copies:
         k.start()
     fan = head_fan()
     row = lax.broadcasted_iota(jnp.int32, (BLOCK, BLOCK), 0) // HEAD_DIM
     lane = lax.broadcasted_iota(jnp.int32, (BLOCK, BLOCK), 1) // HEAD_DIM
     same_head = (row == lane).astype(bf16)
-    came = arriving[...]
+    here, there = mine[...].astype(f32), other[...].astype(f32)
+    even = order[4] == 0
+    came = jnp.concatenate([jnp.where(even, here, there), jnp.where(even, there, here)], axis=1)
     waited = False
     for i in range(rows // BLOCK):
         mixed = []
@@ -299,97 +327,129 @@
                 k.wait()
             waited = True
         for p in range(4):
-            outs[p][i * BLOCK : (i + 1) * BLOCK, :] = dot(mixed, wv[p]).astype(bf16)
-
-
-def leave(order, arriving, y, z, c, cum, ent, pri, gain, w):
+            out = outs[p][i]
+            at = i * BLOCK if p == 0 else 0
+            out[at : at + BLOCK, :] = dot(mixed, wv[p]).astype(bf16)
+
+
+def leave(which, order, mine, other, y, z, c, cum, ent, pri, gain, w):
     rows = y.shape[0]
+    shape = jax.ShapeDtypeStruct
+    outs = [shape((rows, LANES), bf16)] + [shape((BLOCK, LANES), bf16)] * 6
     return pl.pallas_call(
-        functools.partial(exit_kernel, rows),
-        out_shape=[jax.ShapeDtypeStruct((rows, LANES), bf16)] * 4,
-        in_specs=[smem()] + [vmem()] * 8 + [anywhere()],
-        out_specs=[vmem()] * 4,
+        functools.partial(exit_kernel, which, rows),
+        out_shape=outs,
+        in_specs=[smem()] + [vmem()] * 9 + [anywhere()],
+        out_specs=[vmem()] * len(outs),
         scratch_shapes=[pltpu.VMEM((4, LANES, LANES), bf16), pltpu.SemaphoreType.DMA((4,))],
         compiler_params=pltpu.CompilerParams(vmem_limit_bytes=VMEM_BYTES),
         name="leave",
-    )(order, arriving, y, z, c, cum, ent, pri, gain, w)
-
-
-def turned(by):
-    return [(i, (i + by) % TP) for i in range(TP)]
-
-
-def around(x, by):
-    return lax.ppermute(x, "tp", turned(by))
-
-
-def halo_from(shard, by):
-    count = lax.axis_size(SEQ)
-    pairs = [
-        (s * TP + t, (s + 1) * TP + (t + by) % TP) for s in range(count - 1) for t in range(TP)
-    ]
-    return lax.ppermute(shard[-HALO:], SEQ + ("tp",), pairs)
-
-
-def arriving_state(msg):
-    core, y = lax.axis_index("seq_2"), lax.axis_index("seq_1")
-
-    def opened(m):
-        m = m.astype(f32)
-        return m[:STATE], m[STATE : STATE + 1] + m[STATE + 1 : STATE + 2]
-
-    def closed(state, decay):
-        high = decay.astype(bf16).astype(f32)
-        blank = jnp.zeros((MSG - STATE - 2, LANES), f32)
-        return jnp.concatenate([state, high, decay - high, blank], axis=0).astype(bf16)
-
-    def after(a, b):
-        return b[0] + b[1] * a[0], a[1] * b[1]
-
-    def chosen(pred, a, b):
-        return jnp.where(pred, a[0], b[0]), jnp.where(pred, a[1], b[1])
-
-    nothing = (jnp.zeros((STATE, LANES), f32), jnp.ones((1, LANES), f32))
-    mine = opened(msg)
-    other = opened(lax.ppermute(msg, "seq_2", [(0, 1), (1, 0)]))
-    is_one = core == 1
-    both = after(chosen(is_one, other, mine), chosen(is_one, mine, other))
-    before_core = chosen(is_one, other, nothing)
-    both_msg = closed(*both)
-    ring = [both_msg] + [lax.ppermute(both_msg, "seq_1", turned(k)) for k in (1, 2, 3)]
-    ring = [opened(m) for m in ring]
-    row, before_y = nothing, nothing
+    )(order, mine, other, y, z, c, cum, ent, pri, gain, w)
+
+
+def small_call(kernel, name, outs, place, *operands):
+    return pl.pallas_call(
+        kernel,
+        out_shape=outs,
+        in_specs=[smem()] + [vmem()] * len(operands),
+        out_specs=[vmem()] * len(outs),
+        compiler_params=pltpu.CompilerParams(vmem_limit_bytes=VMEM_BYTES // 2),
+        name=name,
+    )(place, *operands)
+
+
+def chip_kernel(place, keep, got, out):
+    even = place[0] == 0
+    mine, other = opened(keep), opened(got)
+    out[...] = packed(*after(chosen(even, mine, other), chosen(even, other, mine))).astype(bf16)
+
+
+def row_kernel(place, chip, one, two, three, row_out, before_out):
+    y = place[1]
+    ring = [opened(r) for r in (chip, one, two, three)]
+    row, before = nothing(), nothing()
     for at in range(4):
         here = ring[0]
         for k in range(1, 4):
-            here = chosen((y - at) % 4 == k, ring[k], here)
-        before_y = chosen(at < y, after(before_y, here), before_y)
+            here = chosen((y + 4 - at) % 4 == k, ring[k], here)
+        before = chosen(at < y, after(before, here), before)
         row = after(row, here)
-    row_msg = closed(*row)
-    before = nothing
-    for k in (3, 2, 1):
-        pairs = [(i, i + k) for i in range(4 - k)]
-        before = after(before, opened(lax.ppermute(row_msg, "seq_0", pairs)))
-    return after(after(before, before_y), before_core)[0]
-
-
-def layer(shard, order, out_order, params):
+    row_out[...] = packed(*row).astype(bf16)
+    before_out[...] = packed(*before)
+
+
+def arrive_kernel(place, one, two, three, before, keep, got, mine_out, other_out):
+    even = place[0] == 0
+    came = nothing()
+    for r in (three, two, one):
+        came = after(came, opened(r))
+    first = after(came, opened(before))
+    second = after(first, chosen(even, opened(keep), opened(got)))
+    mine_out[...] = jnp.where(even, first[0], second[0]).astype(bf16)
+    other_out[...] = jnp.where(even, second[0], first[0]).astype(bf16)
+
+
+def turned(by):
+    return [(i, (i + by) % TP) for i in range(TP)]
+
+
+def around(x, by):
+    return lax.ppermute(x, "tp", turned(by))
+
+
+def swapped(x):
+    return lax.ppermute(x, "seq_2", [(0, 1), (1, 0)])
+
+
+def arriving_state(place, keep, send):
+    shape = jax.ShapeDtypeStruct
+    got = swapped(send)
+    msg = shape((MSG, HALF), bf16)
+    (chip,) = small_call(chip_kernel, "chip", [msg], place, keep, got)
+    ring = [lax.ppermute(chip, "seq_1", turned(k)) for k in (1, 2, 3)]
+    row, before = small_call(
+        row_kernel, "row", [msg, shape((MSG, HALF), f32)], place, chip, *ring
+    )
+    earlier = [
+        lax.ppermute(row, "seq_0", [(i, i + k) for i in range(4 - k)]) for k in (1, 2, 3)
+    ]
+    mine, other = small_call(
+        arrive_kernel,
+        "arrive",
+        [shape((STATE, HALF), bf16)] * 2,
+        place,
+        *earlier,
+        before,
+        keep,
+        got,
+    )
+    return mine, swapped(other)
+
+
+def behind(x, *done):
+    return lax.optimization_barrier((x, *done))[0]
+
+
+def layer(which, shard, order, out_order, place, params):
     gain, w, wbc, wdt, taps, dt_bias, a_log, skip, out_gain, w_out = params
-    halos = [halo_from(shard, by) for by in (0, 1, -1, 2)]
+    count = lax.axis_size(SEQ)
+    halo = lax.ppermute(shard[-HALO:], SEQ, [(i, i + 1) for i in range(count - 1)])
     half = shard.shape[0] // 2
-    own = [shard[:half], shard[half:]]
-    left = [around(own[0], 1), None]
-    right = [around(own[0], -1), None]
+    halves = [shard[:half], shard[half:]]
+    own = [jnp.concatenate([halo, halves[0]], axis=0), None]
+    left, right = [around(own[0], 1), None], [around(own[0], -1), None]
+    own[1] = behind(halves[1], left[0], right[0])
     opposite = [around(left[0], 1), None]
-    left[1], right[1] = around(own[1], 1), around(own[1], -1)
+    right[1] = around(own[1], -1)
+    left[1] = around(own[1], 1)
     opposite[1] = around(right[1], -1)
     carry = None
     kept = []
     for i in range(2):
         out = entry(
+            which,
             order,
             (own[i], left[i], right[i], opposite[i]),
-            halos,
             carry,
             gain,
             w,
@@ -402,25 +462,29 @@
         )
         kept.append(out[:8])
         carry = out[8:]
-    arriving = arriving_state(carry[0])
-    sums = []
+    mine, other = arriving_state(place, *carry)
+    results = []
     for i in range(2):
         z, xc, b, c, cum, step, ent, pri = kept[i]
         y = inside(xc, b, c, cum, step, skip)
-        mine, plus, minus, opp = leave(out_order, arriving, y, z, c, cum, ent, pri, out_gain, w_out)
+        own_part, plus_a, plus_b, minus_a, minus_b, opp_a, opp_b = leave(
+            which, out_order, mine, other, y, z, c, cum, ent, pri, out_gain, w_out
+        )
+        across_a, across_b = around(opp_a, 1), around(opp_b, -1)
+        down_a, up_b = around(minus_a, -1), around(plus_b, 1)
+        up_a = around((plus_a.astype(f32) + across_a.astype(f32)).astype(bf16), 1)
+        down_b = around((minus_b.astype(f32) + across_b.astype(f32)).astype(bf16), -1)
         quarter = half // 2
-        from_left = around(opp[:quarter], 1)
-        from_right = around(opp[quarter:], -1)
-        up = jnp.concatenate(
-            [(plus[:quarter].astype(f32) + from_left.astype(f32)).astype(bf16), plus[quarter:]], 0
-        )
-        down = jnp.concatenate(
-            [minus[:quarter], (minus[quarter:].astype(f32) + from_right.astype(f32)).astype(bf16)],
-            0,
-        )
-        up, down = around(up, 1), around(down, -1)
-        sums.append(own[i].astype(f32) + mine.astype(f32) + up.astype(f32) + down.astype(f32))
-    return jnp.concatenate(sums, axis=0).astype(bf16)
+        parts = []
+        for rows, up, down in ((slice(0, quarter), up_a, down_a), (slice(quarter, half), up_b, down_b)):
+            parts.append(
+                halves[i][rows].astype(f32)
+                + own_part[rows].astype(f32)
+                + up.astype(f32)
+                + down.astype(f32)
+            )
+        results.append(jnp.concatenate(parts, axis=0).astype(bf16))
+    return results
 
 
 def permuted(x, source):
@@ -444,37 +508,42 @@
     w_out,
 ):
     x = lax.axis_index("tp")
-    order = jnp.stack([x, (x + 3) % TP, (x + 1) % TP, (x + 2) % TP]).astype(jnp.int32)
-    out_order = jnp.stack([x, (x + 1) % TP, (x + 3) % TP, (x + 2) % TP]).astype(jnp.int32)
+    core, y = lax.axis_index("seq_2"), lax.axis_index("seq_1")
+    order = jnp.stack([x, (x + 3) % TP, (x + 1) % TP, (x + 2) % TP, core]).astype(jnp.int32)
+    out_order = jnp.stack([x, (x + 1) % TP, (x + 3) % TP, (x + 2) % TP, core]).astype(jnp.int32)
+    place = jnp.stack([core, y]).astype(jnp.int32)
+    w = w_in.reshape(2, 2048, 2 * LANES)
 
     def params(which):
         return (
             in_gain[which].reshape(TP, 1, 512),
-            w_in[which].reshape(2048, 2 * LANES),
-            w_bc[which],
+            w,
+            w_bc,
             w_dt[which].T.reshape(HEADS, TP, 512).transpose(1, 0, 2),
             jnp.concatenate([conv_x[which], conv_bc[which]], axis=1),
             dt_bias[which].reshape(HEADS, 1),
             a_log[which].reshape(HEADS, 1),
             jnp.repeat(d_skip[which], HEAD_DIM).reshape(1, LANES),
             out_gain[which].reshape(1, LANES),
-            w_out[which],
+            w_out,
         )
 
-    heads_of = col_order.reshape(16, 64)[:, 0]
-    columns = lax.all_gather(heads_of % 512, SEQ, axis=0, tiled=True)
-    upward = heads_of >= 512
-    slot = jnp.arange(1024)
-    give = (slot % 2) * 512 + columns[slot // 2]
-    visit, along = slot // 64, slot % 64
-    row = jnp.where(upward[visit], 63 - along, along)
-    take = (row // 2) * 32 + visit * 2 + row % 2
-
-    row_result = layer(tokens, order, out_order, params(0))
-    payload = permuted(row_result, give).reshape(32, 32, 512)
-    arrived = lax.all_to_all(payload, SEQ, 0, 0, tiled=True).reshape(1024, 512)
-    own_rows = permuted(arrived, take)
-    return layer(own_rows, order, out_order, params(1))
+    starts = col_order.reshape(16, 64)[:, 0]
+    columns = lax.all_to_all(
+        jnp.broadcast_to((starts % 512)[None], (32, 16)), SEQ, 0, 0, tiled=True
+    ).reshape(512)
+    visit = jnp.arange(16)[:, None]
+    along = jnp.arange(64)[None, :]
+    row = jnp.where((starts >= 512)[:, None], 63 - along, along)
+    take = ((row % 2) * 512 + (row // 2) * 16 + visit).reshape(1024)
+    order, columns, take = lax.optimization_barrier((order, columns, take))
+
+    arrived = []
+    for half in layer(0, tokens, order, out_order, place, params(0)):
+        payload = permuted(half, columns).reshape(32, 16, 512)
+        arrived.append(lax.all_to_all(payload, SEQ, 0, 0, tiled=True).reshape(512, 512))
+    own_rows = permuted(jnp.concatenate(arrived, axis=0), take)
+    return jnp.concatenate(layer(1, own_rows, order, out_order, place, params(1)), axis=0)
 
 
 def solution(mesh):

time: 393 us -> 354 us (0.901)
  Pallas kernels: 80 us -> 54.9 us
  other arithmetic: 29.9 us -> 5.13 us
  waiting for transfers between devices: 92 us -> 112 us
  starting transfers between devices: 110 us -> 97.5 us
  local copies, waits for them, and re-layouts: 53.5 us -> 59.6 us
    ppermute x28 -> x36, waiting for transfers between devices: 38.6 us -> 86.8 us  [around(): return lax.ppermute(x, 'tp', turned(by))]
    ppermute x22 -> x18, starting transfers between devices: 61.5 us -> 28.9 us  [the longest x6 15.3 us: arriving_state(): lax.ppermute(row, 'seq_0', [(i, i + k) for i in range(4 - k)])]
    ppermute x22 -> x18, waiting for transfers between devices: 47 us -> 15.3 us  [the longest x6 8.8 us: arriving_state(): ring = [lax.ppermute(chip, 'seq_1', turned(k)) for k in (1, 2, 3)]]
    unnamed x88 -> x160, local copies, waits for them, and re-layouts: 11.2 us -> 34.9 us
    slice x18 -> x5, local copies, waits for them, and re-layouts: 23.5 us -> 2.18 us  [the longest x2 1.34 us: layer(): halves = [shard[:half], shard[half:]]]
    pallas_call x8 -> x14, Pallas kernels: 66.4 us -> 49.8 us  [the longest x4 30.9 us: entry(): pl.pallas_call(functools.partial(entry_kernel, which, first, last, rows),...]
    reshape x1 -> x3, local copies, waits for them, and re-layouts: 0.07 us -> 16 us  [the longest x1 14.4 us: body(): w = w_in.reshape(2, 2048, 2 * LANES)]
    unnamed x1 -> x0, blocking collectives: 15.4 us -> none
  transfers between devices with their start and end apart: 51 -> 56, of which waited for: 26 -> 27; matrix products, arithmetic and copies ran while one was open for 18% -> 8% of each run, Pallas kernels for 12% -> 8%
where the time goes in v2:
time: 354 us; the launch traced here: 350 us
  waiting for transfers between devices  112 us (32%)
  starting transfers between devices  97.5 us (28%)
  local copies, waits for them, and re-layouts  59.6 us (17%)
  Pallas kernels  54.9 us (16%)
  blocking collectives  15.2 us (4%)
  other arithmetic  5.13 us (1%)
  matrix products  4 us (1%)
    ppermute x36, waiting for transfers between devices, around(): return lax.ppermute(x, 'tp', turned(by))  86.8 us
    ppermute x36, starting transfers between devices, around(): return lax.ppermute(x, 'tp', turned(by))  53.1 us
    unnamed x160, local copies, waits for them, and re-layouts  34.9 us
    pallas_call x4, Pallas kernels, entry(): pl.pallas_call(functools.partial(entry_kernel, which, first, last, rows),...  30.9 us
    ppermute x6, starting transfers between devices, arriving_state(): lax.ppermute(row, 'seq_0', [(i, i + k) for i in range(4 - k)])  15.3 us
    all_to_all x1, blocking collectives, body(): lax.all_to_all(payload, SEQ, 0, 0, tiled=True).reshape(512, 512)  15.2 us
    reshape x1, local copies, waits for them, and re-layouts, body(): w = w_in.reshape(2, 2048, 2 * LANES)  14.4 us
    pallas_call x4, Pallas kernels, leave(): pl.pallas_call(functools.partial(exit_kernel, which, rows), out_shape=out...  14.4 us
  transfers between devices with their start and end apart: 56, of which 27 were waited for; matrix products, arithmetic and copies ran while one was open for 8% of the time, Pallas kernels for 8%

profile of v2, /device:TPU:0, one launch (start us, length us, event | category | flops | bytes accessed | tf_op | source)
XLA Modules:
  0.0 349.8 jit_solution(13372382006468420754)
XLA Ops:
  1.6 8.4 %all-to-all-start = ((s32[32,1,16]{2,1,0:T(1,128)}), s32[32,1,16]{2,1,0:T(1,128)S(1)}, u32[]{:S(2)}, u32[]{:S(2)}) async-start(s32[32,1,16]{2,1,0:T(1,128)} %broadcast_in_dim.32), calls=%async_computation | async-start | bytes 32768 | tf_op jit(solution)/shard_map/all_to_all | solution.py:532
  20.2 10.7 %collective-permute-done.1.refs_2_ = bf16[528,512]{1,0:T(8,128)(2,1)} collective-permute-done((bf16[528,512]{1,0:T(8,128)(2,1)S(1)}, bf16[528,512]{1,0:T(8,128)(2,1)}, u32[]{:S(2)}, u32[]{:S(2)}) %collective-permute-start.1) | collective-permute-done | bytes 540704 | tf_op jit(solution)/shard_map/ppermute | solution.py:397
  36.4 10.3 %collective-permute-done.4.refs_3_ = bf16[512,512]{1,0:T(8,128)(2,1)} collective-permute-done((bf16[512,512]{1,0:T(8,128)(2,1)S(1)}, bf16[512,512]{1,0:T(8,128)(2,1)}, u32[]{:S(2)}, u32[]{:S(2)}) %collective-permute-start.4) | collective-permute-done | bytes 524320 | tf_op jit(solution)/shard_map/ppermute | solution.py:397
  46.7 3.9 %collective-permute-start.5 = (bf16[512,512]{1,0:T(8,128)(2,1)}, bf16[512,512]{1,0:T(8,128)(2,1)}, u32[]{:S(2)}, u32[]{:S(2)}) collective-permute-start(bf16[512,512]{1,0:T(8,128)(2,1)} %collective-permute-done.4.refs_3_), channel_id=1, source_target_pairs={{0,3},{1,0},{2,1},{3,2},{4,7},{5,4},{6,5},{7,6},{8,11},{9,8},{10,9... | collective-permute-start | bytes 1572872 | tf_op jit(solution)/shard_map/ppermute | solution.py:397
  50.7 14.4 %reshape.70.refs_6_.refs_9_ = bf16[2,2048,1024]{2,1,0:T(8,128)(2,1)} reshape(bf16[2,2048,2,512]{3,2,1,0:T(2,128)(2,1)} %param.16) | data formatting | bytes 16777216 | tf_op jit(solution)/shard_map/reshape | solution.py:515
  71.7 7.6 %entry.4 = (bf16[512,512]{1,0:T(8,128)(2,1)S(1)}, bf16[512,512]{1,0:T(8,128)(2,1)S(1)}, bf16[512,128]{1,0:T(8,128)(2,1)S(1)}, bf16[512,128]{1,0:T(8,128)(2,1)S(1...) custom-call(s32[5]{0:T(128)S(1)} %stack.38.refs_0_, ...), custom_call_target="tpu_custom_call" | custom-call | tf_op jit(solution)/shard_map/entry/pallas_call | solution.py:239
  82.6 7.9 %entry.5 = (bf16[512,512]{1,0:T(8,128)(2,1)S(1)}, bf16[512,512]{1,0:T(8,128)(2,1)S(1)}, bf16[512,128]{1,0:T(8,128)(2,1)S(1)}, bf16[512,128]{1,0:T(8,128)(2,1)S(1...) custom-call(s32[5]{0:T(128)S(1)} %stack.38.refs_0_, ...), custom_call_target="tpu_custom_call" | custom-call | tf_op jit(solution)/shard_map/entry/pallas_call | solution.py:239
  100.4 5.1 %collective-permute-done.8.one = bf16[144,256]{1,0:T(8,128)(2,1)S(1)} collective-permute-done((bf16[144,256]{1,0:T(8,128)(2,1)S(1)}, bf16[144,256]{1,0:T(8,128)(2,1)S(1)}, u32[]{:S(2)}, u32[]{:S(2)}) %collective-permute-start.8) | collective-permute-done | bytes 73760 | tf_op jit(solution)/shard_map/ppermute | solution.py:409
  128.7 3.9 %leave.5 = (bf16[512,512]{1,0:T(8,128)(2,1)S(1)}, bf16[256,512]{1,0:T(8,128)(2,1)S(1)}, bf16[256,512]{1,0:T(8,128)(2,1)S(1)}, bf16[256,512]{1,0:T(8,128)(2,1)S(1...) custom-call(s32[5]{0:T(128)S(1)} %copy-done.49, ...), custom_call_target="tpu_custom_call" | custom-call | tf_op jit(solution)/shard_map/leave/pallas_call | solution.py:339
  139.3 3.7 %leave.4 = (bf16[512,512]{1,0:T(8,128)(2,1)S(1)}, bf16[256,512]{1,0:T(8,128)(2,1)S(1)}, bf16[256,512]{1,0:T(8,128)(2,1)S(1)}, bf16[256,512]{1,0:T(8,128)(2,1)S(1...) custom-call(s32[5]{0:T(128)S(1)} %copy-done.49, ...), custom_call_target="tpu_custom_call" | custom-call | tf_op jit(solution)/shard_map/leave/pallas_call | solution.py:339
  147.9 5.9 %collective-permute-done.19 = bf16[256,512]{1,0:T(8,128)(2,1)S(1)} collective-permute-done((bf16[256,512]{1,0:T(8,128)(2,1)S(1)}, bf16[256,512]{1,0:T(8,128)(2,1)S(1)}, u32[]{:S(2)}, u32[]{:S(2)}) %collective-permute-start.19) | collective-permute-done | bytes 262176 | tf_op jit(solution)/shard_map/ppermute | solution.py:397
  160.2 4.5 %collective-permute-done.18 = bf16[256,512]{1,0:T(8,128)(2,1)S(1)} collective-permute-done((bf16[256,512]{1,0:T(8,128)(2,1)S(1)}, bf16[256,512]{1,0:T(8,128)(2,1)S(1)}, u32[]{:S(2)}, u32[]{:S(2)}) %collective-permute-start.18) | collective-permute-done | bytes 262176 | tf_op jit(solution)/shard_map/ppermute | solution.py:397
  164.7 5.6 %collective-permute-done.22 = bf16[256,512]{1,0:T(8,128)(2,1)S(1)} collective-permute-done((bf16[256,512]{1,0:T(8,128)(2,1)S(1)}, bf16[256,512]{1,0:T(8,128)(2,1)S(1)}, u32[]{:S(2)}, u32[]{:S(2)}) %collective-permute-start.22) | collective-permute-done | bytes 262176 | tf_op jit(solution)/shard_map/ppermute | solution.py:397
  176.5 7.1 %all-to-all-start.1 = ((bf16[32,16,512]{2,1,0:T(8,128)(2,1)}), bf16[32,16,512]{2,1,0:T(8,128)(2,1)S(1)}, u32[]{:S(2)}, u32[]{:S(2)}) async-start(bf16[32,16,512]{2,1,0:T(8,128)(2,1)} %bitcast.16), calls=%async_computation.1 | async-start | bytes 1048576 | tf_op jit(solution)/shard_map/all_to_all | solution.py:544
  185.0 10.3 %all-to-all-done.1 = bf16[32,16,512]{2,1,0:T(8,128)(2,1)S(1)} async-done(((bf16[32,16,512]{2,1,0:T(8,128)(2,1)}), bf16[32,16,512]{2,1,0:T(8,128)(2,1)S(1)}, u32[]{:S(2)}, u32[]{:S(2)}) %all-to-all-start.1) | async-done | bytes 524320 | tf_op jit(solution)/shard_map/all_to_all | solution.py:544
  195.3 15.2 %all_to_all.16 = bf16[32,16,512]{2,1,0:T(8,128)(2,1)S(1)} all-to-all(bf16[32,16,512]{2,1,0:T(8,128)(2,1)S(1)} %bitcast.55), channel_id=1, replica_groups=mesh['seq_0'=4,'seq_1'=4,'seq_2'=2,'tp'=4] {'seq_0','seq_1','seq_2'}, dimensions={0} | all-to-all | bytes 1048576 | tf_op jit(solution)/shard_map/all_to_all | solution.py:544
  218.2 12.9 %collective-permute-done.28.refs_2_ = bf16[528,512]{1,0:T(8,128)(2,1)} collective-permute-done((bf16[528,512]{1,0:T(8,128)(2,1)S(1)}, bf16[528,512]{1,0:T(8,128)(2,1)}, u32[]{:S(2)}, u32[]{:S(2)}) %collective-permute-start.28) | collective-permute-done | bytes 540704 | tf_op jit(solution)/shard_map/ppermute | solution.py:397
  234.7 10.9 %collective-permute-done.31.refs_3_ = bf16[512,512]{1,0:T(8,128)(2,1)} collective-permute-done((bf16[512,512]{1,0:T(8,128)(2,1)S(1)}, bf16[512,512]{1,0:T(8,128)(2,1)}, u32[]{:S(2)}, u32[]{:S(2)}) %collective-permute-start.31) | collective-permute-done | bytes 524320 | tf_op jit(solution)/shard_map/ppermute | solution.py:397
  245.6 3.9 %collective-permute-start.32 = (bf16[512,512]{1,0:T(8,128)(2,1)}, bf16[512,512]{1,0:T(8,128)(2,1)}, u32[]{:S(2)}, u32[]{:S(2)}) collective-permute-start(bf16[512,512]{1,0:T(8,128)(2,1)} %collective-permute-done.31.refs_3_), channel_id=1, source_target_pairs={{0,3},{1,0},{2,1},{3,2},{4,7},{5,4},{6,5},{7,6},{8,11},{9,8},{10,9... | collective-permute-start | bytes 1572872 | tf_op jit(solution)/shard_map/ppermute | solution.py:397
  255.9 7.5 %entry.6 = (bf16[512,512]{1,0:T(8,128)(2,1)S(1)}, bf16[512,512]{1,0:T(8,128)(2,1)S(1)}, bf16[512,128]{1,0:T(8,128)(2,1)S(1)}, bf16[512,128]{1,0:T(8,128)(2,1)S(1...) custom-call(s32[5]{0:T(128)S(1)} %copy-done.52, ...), custom_call_target="tpu_custom_call" | custom-call | tf_op jit(solution)/shard_map/entry/pallas_call | solution.py:239
  266.6 7.9 %entry.7 = (bf16[512,512]{1,0:T(8,128)(2,1)S(1)}, bf16[512,512]{1,0:T(8,128)(2,1)S(1)}, bf16[512,128]{1,0:T(8,128)(2,1)S(1)}, bf16[512,128]{1,0:T(8,128)(2,1)S(1...) custom-call(s32[5]{0:T(128)S(1)} %copy-done.52, ...), custom_call_target="tpu_custom_call" | custom-call | tf_op jit(solution)/shard_map/entry/pallas_call | solution.py:239
  321.8 6.2 %collective-permute-done.46 = bf16[256,512]{1,0:T(8,128)(2,1)S(1)} collective-permute-done((bf16[256,512]{1,0:T(8,128)(2,1)S(1)}, bf16[256,512]{1,0:T(8,128)(2,1)S(1)}, u32[]{:S(2)}, u32[]{:S(2)}) %collective-permute-start.46) | collective-permute-done | bytes 262176 | tf_op jit(solution)/shard_map/ppermute | solution.py:397
  334.0 4.9 %collective-permute-done.45 = bf16[256,512]{1,0:T(8,128)(2,1)S(1)} collective-permute-done((bf16[256,512]{1,0:T(8,128)(2,1)S(1)}, bf16[256,512]{1,0:T(8,128)(2,1)S(1)}, u32[]{:S(2)}, u32[]{:S(2)}) %collective-permute-start.45) | collective-permute-done | bytes 262176 | tf_op jit(solution)/shard_map/ppermute | solution.py:397
  338.9 5.6 %collective-permute-done.49 = bf16[256,512]{1,0:T(8,128)(2,1)S(1)} collective-permute-done((bf16[256,512]{1,0:T(8,128)(2,1)S(1)}, bf16[256,512]{1,0:T(8,128)(2,1)S(1)}, u32[]{:S(2)}, u32[]{:S(2)}) %collective-permute-start.49) | collective-permute-done | bytes 262176 | tf_op jit(solution)/shard_map/ppermute | solution.py:397
  (323 shorter events, 164.3 us)
Async XLA Ops:
  1.6 63.8 %all-to-all-start = ((s32[32,1,16]{2,1,0:T(1,128)}), s32[32,1,16]{2,1,0:T(1,128)S(1)}, u32[]{:S(2)}, u32[]{:S(2)}) async-start(s32[32,1,16]{2,1,0:T(1,128)} %broadcast_in_dim.32), calls=%async_computation | async-start | bytes 32768 | tf_op jit(solution)/shard_map/all_to_all | solution.py:532
  15.0 15.9 %collective-permute-start.1 = (bf16[528,512]{1,0:T(8,128)(2,1)S(1)}, bf16[528,512]{1,0:T(8,128)(2,1)}, u32[]{:S(2)}, u32[]{:S(2)}) collective-permute-start(bf16[528,512]{1,0:T(8,128)(2,1)S(1)} %pad_maximum_fusion.1.refs_1_), channel_id=1, source_target_pairs={{0,1},{1,2},{2,3},{3,0},{4,5},{5,6},{6,7},{7,4},{8,9},{9,10},{10,1... | collective-permute-start | bytes 1622024 | tf_op jit(solution)/shard_map/ppermute | solution.py:397
  16.6 14.8 %collective-permute-start.2 = (bf16[528,512]{1,0:T(8,128)(2,1)S(1)}, bf16[528,512]{1,0:T(8,128)(2,1)S(1)}, u32[]{:S(2)}, u32[]{:S(2)}) collective-permute-start(bf16[528,512]{1,0:T(8,128)(2,1)S(1)} %pad_maximum_fusion.1.refs_1_), channel_id=1, source_target_pairs={{0,3},{1,0},{2,1},{3,2},{4,7},{5,4},{6,5},{7,6},{8,11},{9,8},{10,9... | collective-permute-start | bytes 1622024 | tf_op jit(solution)/shard_map/ppermute | solution.py:397
  32.2 14.4 %collective-permute-start.4 = (bf16[512,512]{1,0:T(8,128)(2,1)S(1)}, bf16[512,512]{1,0:T(8,128)(2,1)}, u32[]{:S(2)}, u32[]{:S(2)}) collective-permute-start(bf16[512,512]{1,0:T(8,128)(2,1)S(1)} %get-tuple-element.91.refs_1_), channel_id=1, source_target_pairs={{0,3},{1,0},{2,1},{3,2},{4,7},{5,4},{6,5},{7,6},{8,11},{9,8},{10,9... | collective-permute-start | bytes 1572872 | tf_op jit(solution)/shard_map/ppermute | solution.py:397
  35.7 46.8 %collective-permute-start.3 = (bf16[512,512]{1,0:T(8,128)(2,1)S(1)}, bf16[512,512]{1,0:T(8,128)(2,1)}, u32[]{:S(2)}, u32[]{:S(2)}) collective-permute-start(bf16[512,512]{1,0:T(8,128)(2,1)S(1)} %get-tuple-element.91.refs_1_), channel_id=1, source_target_pairs={{0,1},{1,2},{2,3},{3,0},{4,5},{5,6},{6,7},{7,4},{8,9},{9,10},{10,1... | collective-permute-start | bytes 1572872 | tf_op jit(solution)/shard_map/ppermute | solution.py:397
  35.8 31.4 %collective-permute-start.6 = (bf16[528,512]{1,0:T(8,128)(2,1)}, bf16[528,512]{1,0:T(8,128)(2,1)}, u32[]{:S(2)}, u32[]{:S(2)}) collective-permute-start(bf16[528,512]{1,0:T(8,128)(2,1)} %collective-permute-done.1.refs_2_), channel_id=1, source_target_pairs={{0,1},{1,2},{2,3},{3,0},{4,5},{5,6},{6,7},{7,4},{8,9},{9,10},{10,1... | collective-permute-start | bytes 1622024 | tf_op jit(solution)/shard_map/ppermute | solution.py:397
  46.7 35.9 %collective-permute-start.5 = (bf16[512,512]{1,0:T(8,128)(2,1)}, bf16[512,512]{1,0:T(8,128)(2,1)}, u32[]{:S(2)}, u32[]{:S(2)}) collective-permute-start(bf16[512,512]{1,0:T(8,128)(2,1)} %collective-permute-done.4.refs_3_), channel_id=1, source_target_pairs={{0,3},{1,0},{2,1},{3,2},{4,7},{5,4},{6,5},{7,6},{8,11},{9,8},{10,9... | collective-permute-start | bytes 1572872 | tf_op jit(solution)/shard_map/ppermute | solution.py:397
  137.2 18.7 %collective-permute-start.23 = (bf16[256,512]{1,0:T(8,128)(2,1)S(1)}, bf16[256,512]{1,0:T(8,128)(2,1)S(1)}, u32[]{:S(2)}, u32[]{:S(2)}) collective-permute-start(bf16[256,512]{1,0:T(8,128)(2,1)S(1)} %get-tuple-element.127), channel_id=1, source_target_pairs={{0,3},{1,0},{2,1},{3,2},{4,7},{5,4},{6,5},{7,6},{8,11},{9,8},{10,9... | collective-permute-start | bytes 786440 | tf_op jit(solution)/shard_map/ppermute | solution.py:397
  137.3 20.5 %collective-permute-start.24 = (bf16[256,512]{1,0:T(8,128)(2,1)S(1)}, bf16[256,512]{1,0:T(8,128)(2,1)S(1)}, u32[]{:S(2)}, u32[]{:S(2)}) collective-permute-start(bf16[256,512]{1,0:T(8,128)(2,1)S(1)} %get-tuple-element.128), channel_id=1, source_target_pairs={{0,1},{1,2},{2,3},{3,0},{4,5},{5,6},{6,7},{7,4},{8,9},{9,10},{10,1... | collective-permute-start | bytes 786440 | tf_op jit(solution)/shard_map/ppermute | solution.py:397
  145.2 15.0 %collective-permute-start.17 = (bf16[256,512]{1,0:T(8,128)(2,1)S(1)}, bf16[256,512]{1,0:T(8,128)(2,1)S(1)}, u32[]{:S(2)}, u32[]{:S(2)}) collective-permute-start(bf16[256,512]{1,0:T(8,128)(2,1)S(1)} %get-tuple-element.112), channel_id=1, source_target_pairs={{0,3},{1,0},{2,1},{3,2},{4,7},{5,4},{6,5},{7,6},{8,11},{9,8},{10,9... | collective-permute-start | bytes 786440 | tf_op jit(solution)/shard_map/ppermute | solution.py:397
  153.9 16.4 %collective-permute-start.22 = (bf16[256,512]{1,0:T(8,128)(2,1)S(1)}, bf16[256,512]{1,0:T(8,128)(2,1)S(1)}, u32[]{:S(2)}, u32[]{:S(2)}) collective-permute-start(bf16[256,512]{1,0:T(8,128)(2,1)S(1)} %add_convert_fusion.11), channel_id=1, source_target_pairs={{0,1},{1,2},{2,3},{3,0},{4,5},{5,6},{6,7},{7,4},{8,9},{9,10},{10,1... | collective-permute-start | bytes 786440 | tf_op jit(solution)/shard_map/ppermute | solution.py:397
  155.9 14.5 %collective-permute-start.26 = (bf16[256,512]{1,0:T(8,128)(2,1)S(1)}, bf16[256,512]{1,0:T(8,128)(2,1)S(1)}, u32[]{:S(2)}, u32[]{:S(2)}) collective-permute-start(bf16[256,512]{1,0:T(8,128)(2,1)S(1)} %add_convert_fusion.9), channel_id=1, source_target_pairs={{0,3},{1,0},{2,1},{3,2},{4,7},{5,4},{6,5},{7,6},{8,11},{9,8},{10,9... | collective-permute-start | bytes 786440 | tf_op jit(solution)/shard_map/ppermute | solution.py:397
  176.5 18.9 %all-to-all-start.1 = ((bf16[32,16,512]{2,1,0:T(8,128)(2,1)}), bf16[32,16,512]{2,1,0:T(8,128)(2,1)S(1)}, u32[]{:S(2)}, u32[]{:S(2)}) async-start(bf16[32,16,512]{2,1,0:T(8,128)(2,1)} %bitcast.16), calls=%async_computation.1 | async-start | bytes 1048576 | tf_op jit(solution)/shard_map/all_to_all | solution.py:544
  214.9 16.2 %collective-permute-start.28 = (bf16[528,512]{1,0:T(8,128)(2,1)S(1)}, bf16[528,512]{1,0:T(8,128)(2,1)}, u32[]{:S(2)}, u32[]{:S(2)}) collective-permute-start(bf16[528,512]{1,0:T(8,128)(2,1)S(1)} %pad_maximum_fusion.2.refs_1_), channel_id=1, source_target_pairs={{0,1},{1,2},{2,3},{3,0},{4,5},{5,6},{6,7},{7,4},{8,9},{9,10},{10,1... | collective-permute-start | bytes 1622024 | tf_op jit(solution)/shard_map/ppermute | solution.py:397
  215.0 16.1 %collective-permute-start.29 = (bf16[528,512]{1,0:T(8,128)(2,1)S(1)}, bf16[528,512]{1,0:T(8,128)(2,1)S(1)}, u32[]{:S(2)}, u32[]{:S(2)}) collective-permute-start(bf16[528,512]{1,0:T(8,128)(2,1)S(1)} %pad_maximum_fusion.2.refs_1_), channel_id=1, source_target_pairs={{0,3},{1,0},{2,1},{3,2},{4,7},{5,4},{6,5},{7,6},{8,11},{9,8},{10,9... | collective-permute-start | bytes 1622024 | tf_op jit(solution)/shard_map/ppermute | solution.py:397
  234.7 16.7 %collective-permute-start.33 = (bf16[528,512]{1,0:T(8,128)(2,1)}, bf16[528,512]{1,0:T(8,128)(2,1)}, u32[]{:S(2)}, u32[]{:S(2)}) collective-permute-start(bf16[528,512]{1,0:T(8,128)(2,1)} %collective-permute-done.28.refs_2_), channel_id=1, source_target_pairs={{0,1},{1,2},{2,3},{3,0},{4,5},{5,6},{6,7},{7,4},{8,9},{9,10},{10,1... | collective-permute-start | bytes 1622024 | tf_op jit(solution)/shard_map/ppermute | solution.py:397
  234.7 31.8 %collective-permute-start.30 = (bf16[512,512]{1,0:T(8,128)(2,1)S(1)}, bf16[512,512]{1,0:T(8,128)(2,1)}, u32[]{:S(2)}, u32[]{:S(2)}) collective-permute-start(bf16[512,512]{1,0:T(8,128)(2,1)S(1)} %get-tuple-element.131.refs_1_), channel_id=1, source_target_pairs={{0,1},{1,2},{2,3},{3,0},{4,5},{5,6},{6,7},{7,4},{8,9},{9,10},{10,1... | collective-permute-start | bytes 1572872 | tf_op jit(solution)/shard_map/ppermute | solution.py:397
  245.6 20.9 %collective-permute-start.32 = (bf16[512,512]{1,0:T(8,128)(2,1)}, bf16[512,512]{1,0:T(8,128)(2,1)}, u32[]{:S(2)}, u32[]{:S(2)}) collective-permute-start(bf16[512,512]{1,0:T(8,128)(2,1)} %collective-permute-done.31.refs_3_), channel_id=1, source_target_pairs={{0,3},{1,0},{2,1},{3,2},{4,7},{5,4},{6,5},{7,6},{8,11},{9,8},{10,9... | collective-permute-start | bytes 1572872 | tf_op jit(solution)/shard_map/ppermute | solution.py:397
  311.4 18.7 %collective-permute-start.50 = (bf16[256,512]{1,0:T(8,128)(2,1)S(1)}, bf16[256,512]{1,0:T(8,128)(2,1)S(1)}, u32[]{:S(2)}, u32[]{:S(2)}) collective-permute-start(bf16[256,512]{1,0:T(8,128)(2,1)S(1)} %get-tuple-element.167), channel_id=1, source_target_pairs={{0,3},{1,0},{2,1},{3,2},{4,7},{5,4},{6,5},{7,6},{8,11},{9,8},{10,9... | collective-permute-start | bytes 786440 | tf_op jit(solution)/shard_map/ppermute | solution.py:397
  311.4 20.6 %collective-permute-start.51 = (bf16[256,512]{1,0:T(8,128)(2,1)S(1)}, bf16[256,512]{1,0:T(8,128)(2,1)S(1)}, u32[]{:S(2)}, u32[]{:S(2)}) collective-permute-start(bf16[256,512]{1,0:T(8,128)(2,1)S(1)} %get-tuple-element.168), channel_id=1, source_target_pairs={{0,1},{1,2},{2,3},{3,0},{4,5},{5,6},{6,7},{7,4},{8,9},{9,10},{10,1... | collective-permute-start | bytes 786440 | tf_op jit(solution)/shard_map/ppermute | solution.py:397
  319.1 14.9 %collective-permute-start.44 = (bf16[256,512]{1,0:T(8,128)(2,1)S(1)}, bf16[256,512]{1,0:T(8,128)(2,1)S(1)}, u32[]{:S(2)}, u32[]{:S(2)}) collective-permute-start(bf16[256,512]{1,0:T(8,128)(2,1)S(1)} %get-tuple-element.152), channel_id=1, source_target_pairs={{0,3},{1,0},{2,1},{3,2},{4,7},{5,4},{6,5},{7,6},{8,11},{9,8},{10,9... | collective-permute-start | bytes 786440 | tf_op jit(solution)/shard_map/ppermute | solution.py:397
  328.1 16.4 %collective-permute-start.49 = (bf16[256,512]{1,0:T(8,128)(2,1)S(1)}, bf16[256,512]{1,0:T(8,128)(2,1)S(1)}, u32[]{:S(2)}, u32[]{:S(2)}) collective-permute-start(bf16[256,512]{1,0:T(8,128)(2,1)S(1)} %add_convert_fusion.3), channel_id=1, source_target_pairs={{0,1},{1,2},{2,3},{3,0},{4,5},{5,6},{6,7},{7,4},{8,9},{9,10},{10,1... | collective-permute-start | bytes 786440 | tf_op jit(solution)/shard_map/ppermute | solution.py:397
  330.1 14.5 %collective-permute-start.53 = (bf16[256,512]{1,0:T(8,128)(2,1)S(1)}, bf16[256,512]{1,0:T(8,128)(2,1)S(1)}, u32[]{:S(2)}, u32[]{:S(2)}) collective-permute-start(bf16[256,512]{1,0:T(8,128)(2,1)S(1)} %add_convert_fusion.1), channel_id=1, source_target_pairs={{0,3},{1,0},{2,1},{3,2},{4,7},{5,4},{6,5},{7,6},{8,11},{9,8},{10,9... | collective-permute-start | bytes 786440 | tf_op jit(solution)/shard_map/ppermute | solution.py:397
  334.0 14.0 %collective-permute-start.43 = (bf16[256,512]{1,0:T(8,128)(2,1)S(1)}, bf16[256,512]{1,0:T(8,128)(2,1)S(1)}, u32[]{:S(2)}, u32[]{:S(2)}) collective-permute-start(bf16[256,512]{1,0:T(8,128)(2,1)S(1)} %add_convert_fusion.7), channel_id=1, source_target_pairs={{0,1},{1,2},{2,3},{3,0},{4,5},{5,6},{6,7},{7,4},{8,9},{9,10},{10,1... | collective-permute-start | bytes 786440 | tf_op jit(solution)/shard_map/ppermute | solution.py:397
  (112 other events, 1258.1 us)

commit v3 on v2

--- a/solution.py
+++ b/solution.py
@@ -24,7 +24,7 @@
 bf16 = jnp.bfloat16
 NT = (((1,), (1,)), ((), ()))
 TN = (((0,), (0,)), ((), ()))
-VMEM_BYTES = 18 * 2**20
+MIB = 2**20
 
 
 def dot(a, b, dims=None):
@@ -207,8 +207,12 @@
     return pl.BlockSpec(memory_space=pltpu.SMEM)
 
 
-def anywhere():
-    return pl.BlockSpec(memory_space=pl.ANY)
+def in_hbm():
+    return pl.BlockSpec(memory_space=pltpu.HBM)
+
+
+def kept_in_hbm(x):
+    return pltpu.with_memory_space_constraint(x, pltpu.HBM)
 
 
 def entry(which, order, pieces, carry, gain, w, wbc, wdt, taps, dt_bias, a_log, last):
@@ -216,26 +220,27 @@
     rows = pieces[0].shape[0] - (HALO if first else 0)
     shape = jax.ShapeDtypeStruct
     outs = [
-        shape((rows, LANES), bf16),
-        shape((rows, LANES), bf16),
-        shape((rows, STATE), bf16),
-        shape((rows, STATE), bf16),
-        shape((HEADS, rows), f32),
-        shape((HEADS, rows), f32),
-        shape((rows // STRETCH, STATE, LANES), f32),
-        shape((rows // STRETCH, 1, LANES), f32),
+        pltpu.VMEM((rows, LANES), bf16),
+        pltpu.VMEM((rows, LANES), bf16),
+        pltpu.VMEM((rows, STATE), bf16),
+        pltpu.VMEM((rows, STATE), bf16),
+        pltpu.VMEM((HEADS, rows), f32),
+        pltpu.VMEM((HEADS, rows), f32),
+        pltpu.VMEM((rows // STRETCH, STATE, LANES), f32),
+        pltpu.VMEM((rows // STRETCH, 1, LANES), f32),
     ]
     if last:
         outs += [shape((MSG, HALF), bf16)] * 2
     else:
         outs += [
-            shape((HALO, LANES + 2 * STATE), f32),
-            shape((STATE, LANES), f32),
-            shape((HEADS, STRETCH), f32),
+            pltpu.VMEM((HALO, LANES + 2 * STATE), f32),
+            pltpu.VMEM((STATE, LANES), f32),
+            pltpu.VMEM((HEADS, STRETCH), f32),
         ]
     extra = [] if first else list(carry)
+    w, wbc = kept_in_hbm(w), kept_in_hbm(wbc)
     operands = [order, *pieces, *extra, gain, w, wbc, wdt, taps, dt_bias, a_log]
-    specs = [smem()] + [vmem()] * (4 + len(extra) + 1) + [anywhere()] * 2 + [vmem()] * 4
+    specs = [smem()] + [vmem()] * (4 + len(extra) + 1) + [in_hbm()] * 2 + [vmem()] * 4
     return pl.pallas_call(
         functools.partial(entry_kernel, which, first, last, rows),
         out_shape=outs,
@@ -248,7 +253,7 @@
             pltpu.VMEM((HALO + BLOCK, LANES + 2 * STATE), f32),
             pltpu.SemaphoreType.DMA((2, 4)),
         ],
-        compiler_params=pltpu.CompilerParams(vmem_limit_bytes=VMEM_BYTES),
+        compiler_params=pltpu.CompilerParams(vmem_limit_bytes=12 * MIB),
         name="entry",
     )(*operands)
 
@@ -283,10 +288,10 @@
     rows = xc.shape[0]
     return pl.pallas_call(
         functools.partial(inside_kernel, rows),
-        out_shape=jax.ShapeDtypeStruct((rows, LANES), f32),
+        out_shape=pltpu.VMEM((rows, LANES), f32),
         in_specs=[vmem()] * 6,
         out_specs=vmem(),
-        compiler_params=pltpu.CompilerParams(vmem_limit_bytes=VMEM_BYTES),
+        compiler_params=pltpu.CompilerParams(vmem_limit_bytes=4 * MIB),
         name="inside",
     )(xc, b, c, cum, step, skip)
 
@@ -296,7 +301,7 @@
     outs = ((own, own), (plus_a, plus_b), (minus_a, minus_b), (opp_a, opp_b))
     copies = []
     for p in range(4):
-        source = pl.ds(pl.multiple_of(order[p] * 512, 512), 512)
+        source = pl.ds(pl.multiple_of(order[(0, 2, 1, 3)[p]] * 512, 512), 512)
         copies.append(pltpu.make_async_copy(w_any.at[which, :, source], wv.at[p], sems.at[p]))
     for k in copies:
         k.start()
@@ -333,16 +338,17 @@
 
 
 def leave(which, order, mine, other, y, z, c, cum, ent, pri, gain, w):
+    w = kept_in_hbm(w)
     rows = y.shape[0]
     shape = jax.ShapeDtypeStruct
     outs = [shape((rows, LANES), bf16)] + [shape((BLOCK, LANES), bf16)] * 6
     return pl.pallas_call(
         functools.partial(exit_kernel, which, rows),
         out_shape=outs,
-        in_specs=[smem()] + [vmem()] * 9 + [anywhere()],
+        in_specs=[smem()] + [vmem()] * 9 + [in_hbm()],
         out_specs=[vmem()] * len(outs),
         scratch_shapes=[pltpu.VMEM((4, LANES, LANES), bf16), pltpu.SemaphoreType.DMA((4,))],
-        compiler_params=pltpu.CompilerParams(vmem_limit_bytes=VMEM_BYTES),
+        compiler_params=pltpu.CompilerParams(vmem_limit_bytes=8 * MIB),
         name="leave",
     )(order, mine, other, y, z, c, cum, ent, pri, gain, w)
 
@@ -353,19 +359,19 @@
         out_shape=outs,
         in_specs=[smem()] + [vmem()] * len(operands),
         out_specs=[vmem()] * len(outs),
-        compiler_params=pltpu.CompilerParams(vmem_limit_bytes=VMEM_BYTES // 2),
+        compiler_params=pltpu.CompilerParams(vmem_limit_bytes=2 * MIB),
         name=name,
     )(place, *operands)
 
 
 def chip_kernel(place, keep, got, out):
-    even = place[0] == 0
+    even = place[4] == 0
     mine, other = opened(keep), opened(got)
     out[...] = packed(*after(chosen(even, mine, other), chosen(even, other, mine))).astype(bf16)
 
 
 def row_kernel(place, chip, one, two, three, row_out, before_out):
-    y = place[1]
+    y = place[5]
     ring = [opened(r) for r in (chip, one, two, three)]
     row, before = nothing(), nothing()
     for at in range(4):
@@ -379,7 +385,7 @@
 
 
 def arrive_kernel(place, one, two, three, before, keep, got, mine_out, other_out):
-    even = place[0] == 0
+    even = place[4] == 0
     came = nothing()
     for r in (three, two, one):
         came = after(came, opened(r))
@@ -401,7 +407,7 @@
     return lax.ppermute(x, "seq_2", [(0, 1), (1, 0)])
 
 
-def arriving_state(place, keep, send):
+def arriving_state(place, keep, send, beside):
     shape = jax.ShapeDtypeStruct
     got = swapped(send)
     msg = shape((MSG, HALF), bf16)
@@ -417,7 +423,7 @@
         arrive_kernel,
         "arrive",
         [shape((STATE, HALF), bf16)] * 2,
-        place,
+        behind(place, *beside),
         *earlier,
         before,
         keep,
@@ -430,25 +436,33 @@
     return lax.optimization_barrier((x, *done))[0]
 
 
-def layer(which, shard, order, out_order, place, params):
-    gain, w, wbc, wdt, taps, dt_bias, a_log, skip, out_gain, w_out = params
+def with_halo(shard):
     count = lax.axis_size(SEQ)
     halo = lax.ppermute(shard[-HALO:], SEQ, [(i, i + 1) for i in range(count - 1)])
+    return jnp.concatenate([halo, shard[: shard.shape[0] // 2]], axis=0)
+
+
+def layer(which, shard, first, place, params, large, early=(), later=None):
+    gain, wdt, taps, dt_bias, a_log, skip, out_gain = params
+    w, wbc, w_out = large
     half = shard.shape[0] // 2
     halves = [shard[:half], shard[half:]]
-    own = [jnp.concatenate([halo, halves[0]], axis=0), None]
+    own = [first, None]
     left, right = [around(own[0], 1), None], [around(own[0], -1), None]
-    own[1] = behind(halves[1], left[0], right[0])
+    own[1] = behind(halves[1], left[0], right[0], *early)
     opposite = [around(left[0], 1), None]
     right[1] = around(own[1], -1)
     left[1] = around(own[1], 1)
     opposite[1] = around(right[1], -1)
+    extras = later(left[0]) if later else None
+    if later:
+        place, extras = lax.optimization_barrier((place, extras))
     carry = None
     kept = []
     for i in range(2):
         out = entry(
             which,
-            order,
+            place,
             (own[i], left[i], right[i], opposite[i]),
             carry,
             gain,
@@ -462,13 +476,14 @@
         )
         kept.append(out[:8])
         carry = out[8:]
-    mine, other = arriving_state(place, *carry)
+    insides = [inside(*k[1:6], skip) for k in kept]
+    mine, other = arriving_state(place, *carry, insides)
     results = []
     for i in range(2):
         z, xc, b, c, cum, step, ent, pri = kept[i]
-        y = inside(xc, b, c, cum, step, skip)
+        y = insides[i]
         own_part, plus_a, plus_b, minus_a, minus_b, opp_a, opp_b = leave(
-            which, out_order, mine, other, y, z, c, cum, ent, pri, out_gain, w_out
+            which, place, mine, other, y, z, c, cum, ent, pri, out_gain, w_out
         )
         across_a, across_b = around(opp_a, 1), around(opp_b, -1)
         down_a, up_b = around(minus_a, -1), around(plus_b, 1)
@@ -483,8 +498,8 @@
                 + up.astype(f32)
                 + down.astype(f32)
             )
-        results.append(jnp.concatenate(parts, axis=0).astype(bf16))
-    return results
+        results += parts
+    return jnp.concatenate(results, axis=0).astype(bf16), extras
 
 
 def permuted(x, source):
@@ -507,43 +522,48 @@
     out_gain,
     w_out,
 ):
+    first = with_halo(tokens)
+    arguments = (in_gain, w_in, w_dt, conv_x, conv_bc, dt_bias, a_log, d_skip, out_gain, col_order)
+    in_gain, w_in, w_dt, conv_x, conv_bc, dt_bias, a_log, d_skip, out_gain, col_order = behind(
+        arguments, first
+    )
     x = lax.axis_index("tp")
     core, y = lax.axis_index("seq_2"), lax.axis_index("seq_1")
-    order = jnp.stack([x, (x + 3) % TP, (x + 1) % TP, (x + 2) % TP, core]).astype(jnp.int32)
-    out_order = jnp.stack([x, (x + 1) % TP, (x + 3) % TP, (x + 2) % TP, core]).astype(jnp.int32)
-    place = jnp.stack([core, y]).astype(jnp.int32)
+    place = jnp.stack([x, (x + 3) & 3, (x + 1) & 3, (x + 2) & 3, core, y]).astype(jnp.int32)
     w = w_in.reshape(2, 2048, 2 * LANES)
 
     def params(which):
         return (
             in_gain[which].reshape(TP, 1, 512),
-            w,
-            w_bc,
             w_dt[which].T.reshape(HEADS, TP, 512).transpose(1, 0, 2),
             jnp.concatenate([conv_x[which], conv_bc[which]], axis=1),
             dt_bias[which].reshape(HEADS, 1),
             a_log[which].reshape(HEADS, 1),
             jnp.repeat(d_skip[which], HEAD_DIM).reshape(1, LANES),
             out_gain[which].reshape(1, LANES),
-            w_out,
         )
 
+    place, small, w = lax.optimization_barrier((place, [params(0), params(1)], w))
+    large = (w, w_bc, w_out)
+
     starts = col_order.reshape(16, 64)[:, 0]
-    columns = lax.all_to_all(
-        jnp.broadcast_to((starts % 512)[None], (32, 16)), SEQ, 0, 0, tiled=True
-    ).reshape(512)
-    visit = jnp.arange(16)[:, None]
-    along = jnp.arange(64)[None, :]
-    row = jnp.where((starts >= 512)[:, None], 63 - along, along)
-    take = ((row % 2) * 512 + (row // 2) * 16 + visit).reshape(1024)
-    order, columns, take = lax.optimization_barrier((order, columns, take))
-
-    arrived = []
-    for half in layer(0, tokens, order, out_order, place, params(0)):
-        payload = permuted(half, columns).reshape(32, 16, 512)
-        arrived.append(lax.all_to_all(payload, SEQ, 0, 0, tiled=True).reshape(512, 512))
-    own_rows = permuted(jnp.concatenate(arrived, axis=0), take)
-    return jnp.concatenate(layer(1, own_rows, order, out_order, place, params(1)), axis=0)
+
+    def routes(gate):
+        own_columns = behind(starts % 512, gate)
+        columns = lax.all_to_all(
+            jnp.broadcast_to(own_columns[None], (32, 16)), SEQ, 0, 0, tiled=True
+        )
+        give = (columns.reshape(32, 1, 16) + 512 * jnp.arange(2)[None, :, None]).reshape(1024)
+        visit = jnp.arange(16)[:, None]
+        along = jnp.arange(64)[None, :]
+        row = jnp.where((starts >= 512)[:, None], 63 - along, along)
+        return give, ((row // 2) * 32 + (row % 2) * 16 + visit).reshape(1024)
+
+    row_result, (give, take) = layer(0, tokens, first, place, small[0], large, (w,), routes)
+    payload = permuted(row_result, give).reshape(32, 32, 512)
+    arrived = lax.all_to_all(payload, SEQ, 0, 0, tiled=True).reshape(1024, 512)
+    own_rows = permuted(arrived, take)
+    return layer(1, own_rows, with_halo(own_rows), place, small[1], large)[0]
 
 
 def solution(mesh):

time: 354 us -> 299 us (0.84)
  local copies, waits for them, and re-layouts: 59.6 us -> 18.3 us
  starting transfers between devices: 97.5 us -> 80.7 us
  blocking collectives: 15.2 us -> 21.4 us
  Pallas kernels: 54.9 us -> 60.9 us
  waiting for transfers between devices: 112 us -> 108 us
    unnamed x160 -> x24, local copies, waits for them, and re-layouts: 34.9 us -> 0.06 us
    all_to_all x2 -> x1, starting transfers between devices: 15.5 us -> 8.88 us  [routes(): lax.all_to_all(jnp.broadcast_to(own_columns[None], (32, 16)), SEQ, 0, 0,...]
    all_to_all x1, blocking collectives: 15.2 us -> 21.4 us  [body(): arrived = lax.all_to_all(payload, SEQ, 0, 0, tiled=True).reshape(1024, 512)]
    pallas_call x4, Pallas kernels: 30.9 us -> 36.1 us  [entry(): pl.pallas_call(functools.partial(entry_kernel, which, first, last, rows),...]
    ppermute x36, starting transfers between devices: 53.1 us -> 48 us  [around(): return lax.ppermute(x, 'tp', turned(by))]
    ppermute x6, starting transfers between devices: 9.01 us -> 4.81 us  [arriving_state(): ring = [lax.ppermute(chip, 'seq_1', turned(k)) for k in (1, 2, 3)]]
    all_to_all x2 -> x1, waiting for transfers between devices: 10.3 us -> 7.15 us  [routes(): lax.all_to_all(jnp.broadcast_to(own_columns[None], (32, 16)), SEQ, 0, 0,...]
  transfers between devices with their start and end apart: 56 -> 55, of which waited for: 27 -> 30; matrix products, arithmetic and copies ran while one was open for 8% -> 6% of each run, Pallas kernels for 8% -> 10%
where the time goes in v3:
time: 299 us; the launch traced here: 295 us
  waiting for transfers between devices  108 us (36%)
  starting transfers between devices  80.7 us (27%)
  Pallas kernels  60.9 us (20%)
  blocking collectives  21.4 us (7%)
  local copies, waits for them, and re-layouts  18.3 us (6%)
  other arithmetic  3.09 us (1%)
    ppermute x36, waiting for transfers between devices, around(): return lax.ppermute(x, 'tp', turned(by))  83.4 us
    ppermute x36, starting transfers between devices, around(): return lax.ppermute(x, 'tp', turned(by))  48 us
    pallas_call x4, Pallas kernels, entry(): pl.pallas_call(functools.partial(entry_kernel, which, first, last, rows),...  36.1 us
    all_to_all x1, blocking collectives, body(): arrived = lax.all_to_all(payload, SEQ, 0, 0, tiled=True).reshape(1024, 512)  21.4 us
    pallas_call x4, Pallas kernels, leave(): pl.pallas_call(functools.partial(exit_kernel, which, rows), out_shape=out...  15.8 us
    ppermute x6, starting transfers between devices, arriving_state(): lax.ppermute(row, 'seq_0', [(i, i + k) for i in range(4 - k)])  15.3 us
    reshape x1, local copies, waits for them, and re-layouts, body(): w = w_in.reshape(2, 2048, 2 * LANES)  14.3 us
    ppermute x6, waiting for transfers between devices, arriving_state(): ring = [lax.ppermute(chip, 'seq_1', turned(k)) for k in (1, 2, 3)]  11.3 us
  transfers between devices with their start and end apart: 55, of which 30 were waited for; matrix products, arithmetic and copies ran while one was open for 6% of the time, Pallas kernels for 10%

profile of v3, /device:TPU:0, one launch (start us, length us, event | category | flops | bytes accessed | tf_op | source)
XLA Modules:
  0.0 295.4 jit_solution(16596639410557192520)
XLA Ops:
  7.4 14.3 %reshape.51.refs_6_.refs_9_ = bf16[2,2048,1024]{2,1,0:T(8,128)(2,1)} reshape(bf16[2,2048,2,512]{3,2,1,0:T(2,128)(2,1)} %param.16) | data formatting | bytes 16777216 | tf_op jit(solution)/shard_map/reshape | solution.py:533
  25.5 11.7 %collective-permute-done.5.refs_3_ = bf16[512,512]{1,0:T(8,128)(2,1)S(1)} collective-permute-done((bf16[512,512]{1,0:T(8,128)(2,1)S(1)}, bf16[512,512]{1,0:T(8,128)(2,1)S(1)}, u32[]{:S(2)}, u32[]{:S(2)}) %collective-permute-start.5) | collective-permute-done | bytes 524320 | tf_op jit(solution)/shard_map/ppermute | solution.py:403
  41.4 8.9 %all-to-all-start = ((s32[32,1,16]{2,1,0:T(1,128)}), s32[32,1,16]{2,1,0:T(1,128)S(1)}, u32[]{:S(2)}, u32[]{:S(2)}) async-start(s32[32,1,16]{2,1,0:T(1,128)} %broadcast_in_dim.48), calls=%async_computation | async-start | bytes 32768 | tf_op jit(solution)/shard_map/all_to_all | solution.py:553
  50.5 7.2 %all-to-all-done = s32[32,1,16]{2,1,0:T(1,128)S(1)} async-done(((s32[32,1,16]{2,1,0:T(1,128)}), s32[32,1,16]{2,1,0:T(1,128)S(1)}, u32[]{:S(2)}, u32[]{:S(2)}) %all-to-all-start) | async-done | bytes 2080 | tf_op jit(solution)/shard_map/all_to_all | solution.py:553
  57.8 8.6 %entry.4 = (bf16[512,512]{1,0:T(8,128)(2,1)S(1)}, bf16[512,512]{1,0:T(8,128)(2,1)S(1)}, bf16[512,128]{1,0:T(8,128)(2,1)S(1)}, bf16[512,128]{1,0:T(8,128)(2,1)S(1...) custom-call(s32[6]{0:T(128)S(1)} %stack.27.refs_0_.place.order, ...), custom_call_target="tpu_custom_call" | custom-call | tf_op jit(solution)/shard_map/entry/pallas_call | solution.py:244
  66.5 9.4 %entry.5 = (bf16[512,512]{1,0:T(8,128)(2,1)S(1)}, bf16[512,512]{1,0:T(8,128)(2,1)S(1)}, bf16[512,128]{1,0:T(8,128)(2,1)S(1)}, bf16[512,128]{1,0:T(8,128)(2,1)S(1...) custom-call(s32[6]{0:T(128)S(1)} %stack.27.refs_0_.place.order, ...), custom_call_target="tpu_custom_call" | custom-call | tf_op jit(solution)/shard_map/entry/pallas_call | solution.py:244
  99.1 4.0 %leave.5 = (bf16[512,512]{1,0:T(8,128)(2,1)S(1)}, bf16[256,512]{1,0:T(8,128)(2,1)S(1)}, bf16[256,512]{1,0:T(8,128)(2,1)S(1)}, bf16[256,512]{1,0:T(8,128)(2,1)S(1...) custom-call(s32[6]{0:T(128)S(1)} %stack.27.refs_0_.place.order, ...), custom_call_target="tpu_custom_call" | custom-call | tf_op jit(solution)/shard_map/leave/pallas_call | solution.py:345
  108.4 4.0 %leave.4 = (bf16[512,512]{1,0:T(8,128)(2,1)S(1)}, bf16[256,512]{1,0:T(8,128)(2,1)S(1)}, bf16[256,512]{1,0:T(8,128)(2,1)S(1)}, bf16[256,512]{1,0:T(8,128)(2,1)S(1...) custom-call(s32[6]{0:T(128)S(1)} %stack.27.refs_0_.place.order, ...), custom_call_target="tpu_custom_call" | custom-call | tf_op jit(solution)/shard_map/leave/pallas_call | solution.py:345
  116.9 7.1 %collective-permute-done.15 = bf16[256,512]{1,0:T(8,128)(2,1)S(1)} collective-permute-done((bf16[256,512]{1,0:T(8,128)(2,1)S(1)}, bf16[256,512]{1,0:T(8,128)(2,1)S(1)}, u32[]{:S(2)}, u32[]{:S(2)}) %collective-permute-start.15) | collective-permute-done | bytes 262176 | tf_op jit(solution)/shard_map/ppermute | solution.py:403
  124.1 4.8 %collective-permute-done.19 = bf16[256,512]{1,0:T(8,128)(2,1)S(1)} collective-permute-done((bf16[256,512]{1,0:T(8,128)(2,1)S(1)}, bf16[256,512]{1,0:T(8,128)(2,1)S(1)}, u32[]{:S(2)}, u32[]{:S(2)}) %collective-permute-start.19) | collective-permute-done | bytes 262176 | tf_op jit(solution)/shard_map/ppermute | solution.py:403
  128.9 3.8 %collective-permute-start.26 = (bf16[256,512]{1,0:T(8,128)(2,1)S(1)}, bf16[256,512]{1,0:T(8,128)(2,1)S(1)}, u32[]{:S(2)}, u32[]{:S(2)}) collective-permute-start(bf16[256,512]{1,0:T(8,128)(2,1)S(1)} %add_convert_fusion.9), channel_id=1, source_target_pairs={{0,3},{1,0},{2,1},{3,2},{4,7},{5,4},{6,5},{7,6},{8,11},{9,8},{10,9... | collective-permute-start | bytes 786440 | tf_op jit(solution)/shard_map/ppermute | solution.py:403
  136.0 3.8 %collective-permute-done.22 = bf16[256,512]{1,0:T(8,128)(2,1)S(1)} collective-permute-done((bf16[256,512]{1,0:T(8,128)(2,1)S(1)}, bf16[256,512]{1,0:T(8,128)(2,1)S(1)}, u32[]{:S(2)}, u32[]{:S(2)}) %collective-permute-start.22) | collective-permute-done | bytes 262176 | tf_op jit(solution)/shard_map/ppermute | solution.py:403
  139.8 4.2 %collective-permute-done.16 = bf16[256,512]{1,0:T(8,128)(2,1)S(1)} collective-permute-done((bf16[256,512]{1,0:T(8,128)(2,1)S(1)}, bf16[256,512]{1,0:T(8,128)(2,1)S(1)}, u32[]{:S(2)}, u32[]{:S(2)}) %collective-permute-start.16) | collective-permute-done | bytes 262176 | tf_op jit(solution)/shard_map/ppermute | solution.py:403
  145.9 21.4 %all_to_all.11 = bf16[32,32,512]{2,1,0:T(8,128)(2,1)S(1)} all-to-all(bf16[32,32,512]{2,1,0:T(8,128)(2,1)S(1)} %bitcast.54), channel_id=1, replica_groups=mesh['seq_0'=4,'seq_1'=4,'seq_2'=2,'tp'=4] {'seq_0','seq_1','seq_2'}, dimensions={0} | all-to-all | bytes 2097152 | tf_op jit(solution)/shard_map/all_to_all | solution.py:564
  174.3 12.3 %collective-permute-done.29.refs_3_ = bf16[528,512]{1,0:T(8,128)(2,1)S(1)} collective-permute-done((bf16[528,512]{1,0:T(8,128)(2,1)S(1)}, bf16[528,512]{1,0:T(8,128)(2,1)S(1)}, u32[]{:S(2)}, u32[]{:S(2)}) %collective-permute-start.29) | collective-permute-done | bytes 540704 | tf_op jit(solution)/shard_map/ppermute | solution.py:403
  192.0 11.3 %collective-permute-done.32.refs_3_ = bf16[512,512]{1,0:T(8,128)(2,1)S(1)} collective-permute-done((bf16[512,512]{1,0:T(8,128)(2,1)S(1)}, bf16[512,512]{1,0:T(8,128)(2,1)S(1)}, u32[]{:S(2)}, u32[]{:S(2)}) %collective-permute-start.32) | collective-permute-done | bytes 524320 | tf_op jit(solution)/shard_map/ppermute | solution.py:403
  206.7 8.6 %entry.6 = (bf16[512,512]{1,0:T(8,128)(2,1)S(1)}, bf16[512,512]{1,0:T(8,128)(2,1)S(1)}, bf16[512,128]{1,0:T(8,128)(2,1)S(1)}, bf16[512,128]{1,0:T(8,128)(2,1)S(1...) custom-call(s32[6]{0:T(128)S(1)} %stack.27.refs_0_.place.order, ...), custom_call_target="tpu_custom_call" | custom-call | tf_op jit(solution)/shard_map/entry/pallas_call | solution.py:244
  216.6 9.5 %entry.7 = (bf16[512,512]{1,0:T(8,128)(2,1)S(1)}, bf16[512,512]{1,0:T(8,128)(2,1)S(1)}, bf16[512,128]{1,0:T(8,128)(2,1)S(1)}, bf16[512,128]{1,0:T(8,128)(2,1)S(1...) custom-call(s32[6]{0:T(128)S(1)} %stack.27.refs_0_.place.order, ...), custom_call_target="tpu_custom_call" | custom-call | tf_op jit(solution)/shard_map/entry/pallas_call | solution.py:244
  248.7 3.9 %leave.7 = (bf16[512,512]{1,0:T(8,128)(2,1)S(1)}, bf16[256,512]{1,0:T(8,128)(2,1)S(1)}, bf16[256,512]{1,0:T(8,128)(2,1)S(1)}, bf16[256,512]{1,0:T(8,128)(2,1)S(1...) custom-call(s32[6]{0:T(128)S(1)} %stack.27.refs_0_.place.order, ...), custom_call_target="tpu_custom_call" | custom-call | tf_op jit(solution)/shard_map/leave/pallas_call | solution.py:345
  258.0 3.9 %leave.6 = (bf16[512,512]{1,0:T(8,128)(2,1)S(1)}, bf16[256,512]{1,0:T(8,128)(2,1)S(1)}, bf16[256,512]{1,0:T(8,128)(2,1)S(1)}, bf16[256,512]{1,0:T(8,128)(2,1)S(1...) custom-call(s32[6]{0:T(128)S(1)} %stack.27.refs_0_.place.order, ...), custom_call_target="tpu_custom_call" | custom-call | tf_op jit(solution)/shard_map/leave/pallas_call | solution.py:345
  267.1 6.4 %collective-permute-done.42 = bf16[256,512]{1,0:T(8,128)(2,1)S(1)} collective-permute-done((bf16[256,512]{1,0:T(8,128)(2,1)S(1)}, bf16[256,512]{1,0:T(8,128)(2,1)S(1)}, u32[]{:S(2)}, u32[]{:S(2)}) %collective-permute-start.42) | collective-permute-done | bytes 262176 | tf_op jit(solution)/shard_map/ppermute | solution.py:403
  273.6 4.8 %collective-permute-done.46 = bf16[256,512]{1,0:T(8,128)(2,1)S(1)} collective-permute-done((bf16[256,512]{1,0:T(8,128)(2,1)S(1)}, bf16[256,512]{1,0:T(8,128)(2,1)S(1)}, u32[]{:S(2)}, u32[]{:S(2)}) %collective-permute-start.46) | collective-permute-done | bytes 262176 | tf_op jit(solution)/shard_map/ppermute | solution.py:403
  285.5 3.8 %collective-permute-done.49 = bf16[256,512]{1,0:T(8,128)(2,1)S(1)} collective-permute-done((bf16[256,512]{1,0:T(8,128)(2,1)S(1)}, bf16[256,512]{1,0:T(8,128)(2,1)S(1)}, u32[]{:S(2)}, u32[]{:S(2)}) %collective-permute-start.49) | collective-permute-done | bytes 262176 | tf_op jit(solution)/shard_map/ppermute | solution.py:403
  289.6 3.9 %collective-permute-done.43 = bf16[256,512]{1,0:T(8,128)(2,1)S(1)} collective-permute-done((bf16[256,512]{1,0:T(8,128)(2,1)S(1)}, bf16[256,512]{1,0:T(8,128)(2,1)S(1)}, u32[]{:S(2)}, u32[]{:S(2)}) %collective-permute-start.43) | collective-permute-done | bytes 262176 | tf_op jit(solution)/shard_map/ppermute | solution.py:403
  (180 shorter events, 112.9 us)
Async XLA Ops:
  3.6 18.1 %collective-permute-start.2 = (bf16[528,512]{1,0:T(8,128)(2,1)S(1)}, bf16[528,512]{1,0:T(8,128)(2,1)S(1)}, u32[]{:S(2)}, u32[]{:S(2)}) collective-permute-start(bf16[528,512]{1,0:T(8,128)(2,1)S(1)} %pad_maximum_fusion.1.refs_1_), channel_id=1, source_target_pairs={{0,3},{1,0},{2,1},{3,2},{4,7},{5,4},{6,5},{7,6},{8,11},{9,8},{10,9... | collective-permute-start | bytes 1622024 | tf_op jit(solution)/shard_map/ppermute | solution.py:403
  6.9 15.8 %collective-permute-start.1 = (bf16[528,512]{1,0:T(8,128)(2,1)S(1)}, bf16[528,512]{1,0:T(8,128)(2,1)S(1)}, u32[]{:S(2)}, u32[]{:S(2)}) collective-permute-start(bf16[528,512]{1,0:T(8,128)(2,1)S(1)} %pad_maximum_fusion.1.refs_1_), channel_id=1, source_target_pairs={{0,1},{1,2},{2,3},{3,0},{4,5},{5,6},{6,7},{7,4},{8,9},{9,10},{10,1... | collective-permute-start | bytes 1622024 | tf_op jit(solution)/shard_map/ppermute | solution.py:403
  22.7 14.5 %collective-permute-start.5 = (bf16[512,512]{1,0:T(8,128)(2,1)S(1)}, bf16[512,512]{1,0:T(8,128)(2,1)S(1)}, u32[]{:S(2)}, u32[]{:S(2)}) collective-permute-start(bf16[512,512]{1,0:T(8,128)(2,1)S(1)} %get-tuple-element.144.refs_1_), channel_id=1, source_target_pairs={{0,3},{1,0},{2,1},{3,2},{4,7},{5,4},{6,5},{7,6},{8,11},{9,8},{10,9... | collective-permute-start | bytes 1572872 | tf_op jit(solution)/shard_map/ppermute | solution.py:403
  25.4 41.0 %collective-permute-start.4 = (bf16[512,512]{1,0:T(8,128)(2,1)S(1)}, bf16[512,512]{1,0:T(8,128)(2,1)}, u32[]{:S(2)}, u32[]{:S(2)}) collective-permute-start(bf16[512,512]{1,0:T(8,128)(2,1)S(1)} %get-tuple-element.144.refs_1_), channel_id=1, source_target_pairs={{0,1},{1,2},{2,3},{3,0},{4,5},{5,6},{6,7},{7,4},{8,9},{9,10},{10,1... | collective-permute-start | bytes 1572872 | tf_op jit(solution)/shard_map/ppermute | solution.py:403
  25.5 32.4 %collective-permute-start.3 = (bf16[528,512]{1,0:T(8,128)(2,1)S(1)}, bf16[528,512]{1,0:T(8,128)(2,1)S(1)}, u32[]{:S(2)}, u32[]{:S(2)}) collective-permute-start(bf16[528,512]{1,0:T(8,128)(2,1)S(1)} %collective-permute-done.1.refs_2_), channel_id=1, source_target_pairs={{0,1},{1,2},{2,3},{3,0},{4,5},{5,6},{6,7},{7,4},{8,9},{9,10},{10,1... | collective-permute-start | bytes 1622024 | tf_op jit(solution)/shard_map/ppermute | solution.py:403
  37.2 29.3 %collective-permute-start.6 = (bf16[512,512]{1,0:T(8,128)(2,1)S(1)}, bf16[512,512]{1,0:T(8,128)(2,1)}, u32[]{:S(2)}, u32[]{:S(2)}) collective-permute-start(bf16[512,512]{1,0:T(8,128)(2,1)S(1)} %collective-permute-done.5.refs_3_), channel_id=1, source_target_pairs={{0,3},{1,0},{2,1},{3,2},{4,7},{5,4},{6,5},{7,6},{8,11},{9,8},{10,9... | collective-permute-start | bytes 1572872 | tf_op jit(solution)/shard_map/ppermute | solution.py:403
  41.4 16.2 %all-to-all-start = ((s32[32,1,16]{2,1,0:T(1,128)}), s32[32,1,16]{2,1,0:T(1,128)S(1)}, u32[]{:S(2)}, u32[]{:S(2)}) async-start(s32[32,1,16]{2,1,0:T(1,128)} %broadcast_in_dim.48), calls=%async_computation | async-start | bytes 32768 | tf_op jit(solution)/shard_map/all_to_all | solution.py:553
  103.2 12.6 %collective-permute-start.25 = (bf16[256,512]{1,0:T(8,128)(2,1)S(1)}, bf16[256,512]{1,0:T(8,128)(2,1)S(1)}, u32[]{:S(2)}, u32[]{:S(2)}) collective-permute-start(bf16[256,512]{1,0:T(8,128)(2,1)S(1)} %get-tuple-element.180), channel_id=1, source_target_pairs={{0,3},{1,0},{2,1},{3,2},{4,7},{5,4},{6,5},{7,6},{8,11},{9,8},{10,9... | collective-permute-start | bytes 786440 | tf_op jit(solution)/shard_map/ppermute | solution.py:403
  106.4 22.5 %collective-permute-start.23 = (bf16[256,512]{1,0:T(8,128)(2,1)S(1)}, bf16[256,512]{1,0:T(8,128)(2,1)S(1)}, u32[]{:S(2)}, u32[]{:S(2)}) collective-permute-start(bf16[256,512]{1,0:T(8,128)(2,1)S(1)} %get-tuple-element.177), channel_id=1, source_target_pairs={{0,3},{1,0},{2,1},{3,2},{4,7},{5,4},{6,5},{7,6},{8,11},{9,8},{10,9... | collective-permute-start | bytes 786440 | tf_op jit(solution)/shard_map/ppermute | solution.py:403
  106.4 26.3 %collective-permute-start.24 = (bf16[256,512]{1,0:T(8,128)(2,1)S(1)}, bf16[256,512]{1,0:T(8,128)(2,1)S(1)}, u32[]{:S(2)}, u32[]{:S(2)}) collective-permute-start(bf16[256,512]{1,0:T(8,128)(2,1)S(1)} %get-tuple-element.178), channel_id=1, source_target_pairs={{0,1},{1,2},{2,3},{3,0},{4,5},{5,6},{6,7},{7,4},{8,9},{9,10},{10,1... | collective-permute-start | bytes 786440 | tf_op jit(solution)/shard_map/ppermute | solution.py:403
  113.5 19.2 %collective-permute-start.17 = (bf16[256,512]{1,0:T(8,128)(2,1)S(1)}, bf16[256,512]{1,0:T(8,128)(2,1)S(1)}, u32[]{:S(2)}, u32[]{:S(2)}) collective-permute-start(bf16[256,512]{1,0:T(8,128)(2,1)S(1)} %get-tuple-element.167), channel_id=1, source_target_pairs={{0,3},{1,0},{2,1},{3,2},{4,7},{5,4},{6,5},{7,6},{8,11},{9,8},{10,9... | collective-permute-start | bytes 786440 | tf_op jit(solution)/shard_map/ppermute | solution.py:403
  115.8 13.1 %collective-permute-start.19 = (bf16[256,512]{1,0:T(8,128)(2,1)S(1)}, bf16[256,512]{1,0:T(8,128)(2,1)S(1)}, u32[]{:S(2)}, u32[]{:S(2)}) collective-permute-start(bf16[256,512]{1,0:T(8,128)(2,1)S(1)} %get-tuple-element.170), channel_id=1, source_target_pairs={{0,3},{1,0},{2,1},{3,2},{4,7},{5,4},{6,5},{7,6},{8,11},{9,8},{10,9... | collective-permute-start | bytes 786440 | tf_op jit(solution)/shard_map/ppermute | solution.py:403
  171.4 15.2 %collective-permute-start.29 = (bf16[528,512]{1,0:T(8,128)(2,1)S(1)}, bf16[528,512]{1,0:T(8,128)(2,1)S(1)}, u32[]{:S(2)}, u32[]{:S(2)}) collective-permute-start(bf16[528,512]{1,0:T(8,128)(2,1)S(1)} %pad_maximum_fusion.2.refs_1_), channel_id=1, source_target_pairs={{0,3},{1,0},{2,1},{3,2},{4,7},{5,4},{6,5},{7,6},{8,11},{9,8},{10,9... | collective-permute-start | bytes 1622024 | tf_op jit(solution)/shard_map/ppermute | solution.py:403
  174.3 15.7 %collective-permute-start.28 = (bf16[528,512]{1,0:T(8,128)(2,1)S(1)}, bf16[528,512]{1,0:T(8,128)(2,1)S(1)}, u32[]{:S(2)}, u32[]{:S(2)}) collective-permute-start(bf16[528,512]{1,0:T(8,128)(2,1)S(1)} %pad_maximum_fusion.2.refs_1_), channel_id=1, source_target_pairs={{0,1},{1,2},{2,3},{3,0},{4,5},{5,6},{6,7},{7,4},{8,9},{9,10},{10,1... | collective-permute-start | bytes 1622024 | tf_op jit(solution)/shard_map/ppermute | solution.py:403
  190.0 13.3 %collective-permute-start.32 = (bf16[512,512]{1,0:T(8,128)(2,1)S(1)}, bf16[512,512]{1,0:T(8,128)(2,1)S(1)}, u32[]{:S(2)}, u32[]{:S(2)}) collective-permute-start(bf16[512,512]{1,0:T(8,128)(2,1)S(1)} %get-tuple-element.192.refs_1_), channel_id=1, source_target_pairs={{0,3},{1,0},{2,1},{3,2},{4,7},{5,4},{6,5},{7,6},{8,11},{9,8},{10,9... | collective-permute-start | bytes 1572872 | tf_op jit(solution)/shard_map/ppermute | solution.py:403
  190.3 16.4 %collective-permute-start.30 = (bf16[528,512]{1,0:T(8,128)(2,1)S(1)}, bf16[528,512]{1,0:T(8,128)(2,1)S(1)}, u32[]{:S(2)}, u32[]{:S(2)}) collective-permute-start(bf16[528,512]{1,0:T(8,128)(2,1)S(1)} %collective-permute-done.28.refs_2_), channel_id=1, source_target_pairs={{0,1},{1,2},{2,3},{3,0},{4,5},{5,6},{6,7},{7,4},{8,9},{9,10},{10,1... | collective-permute-start | bytes 1622024 | tf_op jit(solution)/shard_map/ppermute | solution.py:403
  192.0 24.5 %collective-permute-start.31 = (bf16[512,512]{1,0:T(8,128)(2,1)S(1)}, bf16[512,512]{1,0:T(8,128)(2,1)}, u32[]{:S(2)}, u32[]{:S(2)}) collective-permute-start(bf16[512,512]{1,0:T(8,128)(2,1)S(1)} %get-tuple-element.192.refs_1_), channel_id=1, source_target_pairs={{0,1},{1,2},{2,3},{3,0},{4,5},{5,6},{6,7},{7,4},{8,9},{9,10},{10,1... | collective-permute-start | bytes 1572872 | tf_op jit(solution)/shard_map/ppermute | solution.py:403
  203.3 13.2 %collective-permute-start.33 = (bf16[512,512]{1,0:T(8,128)(2,1)S(1)}, bf16[512,512]{1,0:T(8,128)(2,1)}, u32[]{:S(2)}, u32[]{:S(2)}) collective-permute-start(bf16[512,512]{1,0:T(8,128)(2,1)S(1)} %collective-permute-done.32.refs_3_), channel_id=1, source_target_pairs={{0,3},{1,0},{2,1},{3,2},{4,7},{5,4},{6,5},{7,6},{8,11},{9,8},{10,9... | collective-permute-start | bytes 1572872 | tf_op jit(solution)/shard_map/ppermute | solution.py:403
  252.9 12.4 %collective-permute-start.52 = (bf16[256,512]{1,0:T(8,128)(2,1)S(1)}, bf16[256,512]{1,0:T(8,128)(2,1)S(1)}, u32[]{:S(2)}, u32[]{:S(2)}) collective-permute-start(bf16[256,512]{1,0:T(8,128)(2,1)S(1)} %get-tuple-element.228), channel_id=1, source_target_pairs={{0,3},{1,0},{2,1},{3,2},{4,7},{5,4},{6,5},{7,6},{8,11},{9,8},{10,9... | collective-permute-start | bytes 786440 | tf_op jit(solution)/shard_map/ppermute | solution.py:403
  256.0 24.3 %collective-permute-start.50 = (bf16[256,512]{1,0:T(8,128)(2,1)S(1)}, bf16[256,512]{1,0:T(8,128)(2,1)S(1)}, u32[]{:S(2)}, u32[]{:S(2)}) collective-permute-start(bf16[256,512]{1,0:T(8,128)(2,1)S(1)} %get-tuple-element.225), channel_id=1, source_target_pairs={{0,3},{1,0},{2,1},{3,2},{4,7},{5,4},{6,5},{7,6},{8,11},{9,8},{10,9... | collective-permute-start | bytes 786440 | tf_op jit(solution)/shard_map/ppermute | solution.py:403
  257.6 24.7 %collective-permute-start.51 = (bf16[256,512]{1,0:T(8,128)(2,1)S(1)}, bf16[256,512]{1,0:T(8,128)(2,1)S(1)}, u32[]{:S(2)}, u32[]{:S(2)}) collective-permute-start(bf16[256,512]{1,0:T(8,128)(2,1)S(1)} %get-tuple-element.226), channel_id=1, source_target_pairs={{0,1},{1,2},{2,3},{3,0},{4,5},{5,6},{6,7},{7,4},{8,9},{9,10},{10,1... | collective-permute-start | bytes 786440 | tf_op jit(solution)/shard_map/ppermute | solution.py:403
  263.1 19.3 %collective-permute-start.44 = (bf16[256,512]{1,0:T(8,128)(2,1)S(1)}, bf16[256,512]{1,0:T(8,128)(2,1)S(1)}, u32[]{:S(2)}, u32[]{:S(2)}) collective-permute-start(bf16[256,512]{1,0:T(8,128)(2,1)S(1)} %get-tuple-element.215), channel_id=1, source_target_pairs={{0,3},{1,0},{2,1},{3,2},{4,7},{5,4},{6,5},{7,6},{8,11},{9,8},{10,9... | collective-permute-start | bytes 786440 | tf_op jit(solution)/shard_map/ppermute | solution.py:403
  265.3 13.1 %collective-permute-start.46 = (bf16[256,512]{1,0:T(8,128)(2,1)S(1)}, bf16[256,512]{1,0:T(8,128)(2,1)S(1)}, u32[]{:S(2)}, u32[]{:S(2)}) collective-permute-start(bf16[256,512]{1,0:T(8,128)(2,1)S(1)} %get-tuple-element.218), channel_id=1, source_target_pairs={{0,3},{1,0},{2,1},{3,2},{4,7},{5,4},{6,5},{7,6},{8,11},{9,8},{10,9... | collective-permute-start | bytes 786440 | tf_op jit(solution)/shard_map/ppermute | solution.py:403
  273.5 12.0 %collective-permute-start.45 = (bf16[256,512]{1,0:T(8,128)(2,1)S(1)}, bf16[256,512]{1,0:T(8,128)(2,1)S(1)}, u32[]{:S(2)}, u32[]{:S(2)}) collective-permute-start(bf16[256,512]{1,0:T(8,128)(2,1)S(1)} %get-tuple-element.216), channel_id=1, source_target_pairs={{0,1},{1,2},{2,3},{3,0},{4,5},{5,6},{6,7},{7,4},{8,9},{9,10},{10,1... | collective-permute-start | bytes 786440 | tf_op jit(solution)/shard_map/ppermute | solution.py:403
  (43 other events, 396.0 us)

commit v4 on v3

--- a/solution.py
+++ b/solution.py
@@ -46,16 +46,21 @@
     return dot(jnp.concatenate([high, low], axis=0), fan, TN)
 
 
-def packed(state, decay):
+def packed(state, decay, columns):
     high = decay.astype(bf16).astype(f32)
-    row = lax.broadcasted_iota(jnp.int32, (MSG - STATE, decay.shape[1]), 0)
+    row = lax.broadcasted_iota(jnp.int32, (8, decay.shape[1]), 0)
     rest = jnp.where(row == 0, high, jnp.where(row == 1, decay - high, 0.0))
-    return jnp.concatenate([state, rest], axis=0)
+    return jnp.concatenate([state, columns, rest], axis=0)
 
 
 def opened(msg):
     msg = msg[...].astype(f32)
-    return msg[:STATE], msg[STATE : STATE + 1] + msg[STATE + 1 : STATE + 2]
+    at = STATE + 8
+    return msg[:STATE], msg[at : at + 1] + msg[at + 1 : at + 2]
+
+
+def columns_in(msg):
+    return msg[...].astype(f32)[STATE : STATE + 8]
 
 
 def after(a, b):
@@ -76,39 +81,30 @@
     return (row % HEADS == lane // HEAD_DIM).astype(bf16)
 
 
-def entry_kernel(which, first, last, rows, *refs):
+def entry_kernel(first, last, rows, *refs):
     (order, own, left, right, opposite) = refs[:5]
     refs = refs[5:]
     ahead = HALO if first else 0
+    columns = ()
+    if last:
+        columns, refs = refs[:1], refs[1:]
     if not first:
         tail_in, state_in, total_in, refs = *refs[:3], refs[3:]
-    (gain, w_any, wbc_any, wdt, taps, dt_bias, a_log), refs = refs[:7], refs[7:]
+    (gain, wv, wbcv, wdt, taps, dt_bias, a_log), refs = refs[:7], refs[7:]
     (z_out, xc_out, b_out, c_out, cum_out, step_out, ent_out, pri_out), refs = refs[:8], refs[8:]
     if last:
         (keep_out, send_out), refs = refs[:2], refs[2:]
+        columns = columns[0]
     else:
         (tail_out, state_out, total_out), refs = refs[:3], refs[3:]
-    wv, wbcv, nbuf, xbuf, sems = refs
-
-    copies = []
-    for p in range(4):
-        source = pl.ds(pl.multiple_of(order[p] * 512, 512), 512)
-        target = pl.ds(p * 512, 512)
-        copies.append(pltpu.make_async_copy(w_any.at[which, source, :], wv.at[target, :], sems.at[0, p]))
-        copies.append(
-            pltpu.make_async_copy(
-                wbc_any.at[which, source, :], wbcv.at[target, :], sems.at[1, p]
-            )
-        )
-    for c in copies:
-        c.start()
+    nbuf, xbuf = refs
 
     fan = head_fan()
     k_pos = lax.broadcasted_iota(jnp.int32, (STRETCH, STRETCH), 0)
     q_pos = lax.broadcasted_iota(jnp.int32, (STRETCH, STRETCH), 1)
     upto = (k_pos <= q_pos).astype(f32)
     lane = lax.broadcasted_iota(jnp.int32, (HEADS, STRETCH), 1)
-    rate = jnp.exp(a_log[...])
+    rate = jnp.exp(a_log[:, 0:1])
     if first:
         state = jnp.zeros((STATE, LANES), f32)
         total = jnp.zeros((HEADS, 1), f32)
@@ -116,7 +112,6 @@
         state = state_in[...]
         total = total_in[:, 0:1]
         xbuf[0:HALO, :] = tail_in[...]
-    waited = False
     for i in range(rows // BLOCK):
         span = pl.ds(i * BLOCK, BLOCK)
         above = pl.ds(ahead + i * BLOCK, BLOCK)
@@ -136,10 +131,6 @@
                 nbuf[0:HALO, p * 512 : (p + 1) * 512] = (
                     widen[p] * scale * gain[order[p]]
                 ).astype(bf16)
-        if not waited:
-            for c in copies:
-                c.wait()
-            waited = True
         low = 0 if first and i == 0 else HALO
         if low and i > 0:
             xbuf[0:HALO, :] = xbuf[BLOCK : BLOCK + HALO, :]
@@ -159,7 +150,7 @@
         xc_out[span, :] = xc.astype(bf16)
         b_out[span, :] = b
         c_out[span, :] = mixed[:, LANES + STATE :].astype(bf16)
-        step = softplus(dt + dt_bias[...])
+        step = softplus(dt + dt_bias[:, 0:1])
         decay = -step * rate
         step_out[:, i * BLOCK : (i + 1) * BLOCK] = step
         cums, marks = [], jnp.zeros((HEADS, STRETCH), f32)
@@ -188,8 +179,9 @@
             pri_out[2 * i + j] = marks[2 + j : 3 + j, :]
             state = state * marks[j : j + 1, :] + fresh
     if last:
-        whole = packed(state, marks[4:5, :])
-        near, far = whole[:, 0:HALF], whole[:, HALF:]
+        decayed = marks[4:5, :]
+        near = packed(state[:, 0:HALF], decayed[:, 0:HALF], columns[...])
+        far = packed(state[:, HALF:], decayed[:, HALF:], columns[...])
         even = order[4] == 0
         keep_out[...] = jnp.where(even, near, far).astype(bf16)
         send_out[...] = jnp.where(even, far, near).astype(bf16)
@@ -199,6 +191,58 @@
         total_out[...] = jnp.broadcast_to(total, (HEADS, STRETCH))
 
 
+def stage_kernel(which, order, w, wbc, w_out, wbc_out, sems):
+    copies = []
+    for p in range(4):
+        source = pl.ds(pl.multiple_of(order[p] * 512, 512), 512)
+        target = pl.ds(p * 512, 512)
+        copies.append(
+            pltpu.make_async_copy(w.at[which, source, :], w_out.at[target, :], sems.at[0, p])
+        )
+        copies.append(
+            pltpu.make_async_copy(wbc.at[which, source, :], wbc_out.at[target, :], sems.at[1, p])
+        )
+    for c in copies:
+        c.start()
+    for c in copies:
+        c.wait()
+
+
+def staged(which, order, w, wbc):
+    return pl.pallas_call(
+        functools.partial(stage_kernel, which),
+        out_shape=[pltpu.VMEM((2048, 2 * LANES), bf16), pltpu.VMEM((2048, 2 * STATE), bf16)],
+        in_specs=[smem(), in_hbm(), in_hbm()],
+        out_specs=[vmem()] * 2,
+        scratch_shapes=[pltpu.SemaphoreType.DMA((2, 4))],
+        compiler_params=pltpu.CompilerParams(vmem_limit_bytes=2 * MIB),
+        name="stage",
+    )(order, kept_in_hbm(w), kept_in_hbm(wbc))
+
+
+def stage_out_kernel(which, order, w, out, sems):
+    copies = []
+    for p in range(4):
+        source = pl.ds(pl.multiple_of(order[(0, 2, 1, 3)[p]] * 512, 512), 512)
+        copies.append(pltpu.make_async_copy(w.at[which, :, source], out.at[p], sems.at[p]))
+    for c in copies:
+        c.start()
+    for c in copies:
+        c.wait()
+
+
+def staged_out(which, order, w):
+    return pl.pallas_call(
+        functools.partial(stage_out_kernel, which),
+        out_shape=pltpu.VMEM((4, LANES, LANES), bf16),
+        in_specs=[smem(), in_hbm()],
+        out_specs=vmem(),
+        scratch_shapes=[pltpu.SemaphoreType.DMA((4,))],
+        compiler_params=pltpu.CompilerParams(vmem_limit_bytes=2 * MIB),
+        name="stage_out",
+    )(order, kept_in_hbm(w))
+
+
 def vmem():
     return pl.BlockSpec(memory_space=pltpu.VMEM)
 
@@ -215,7 +259,7 @@
     return pltpu.with_memory_space_constraint(x, pltpu.HBM)
 
 
-def entry(which, order, pieces, carry, gain, w, wbc, wdt, taps, dt_bias, a_log, last):
+def entry(order, pieces, columns, carry, gain, w, wbc, wdt, taps, dt_bias, a_log, last):
     first = carry is None
     rows = pieces[0].shape[0] - (HALO if first else 0)
     shape = jax.ShapeDtypeStruct
@@ -238,22 +282,18 @@
             pltpu.VMEM((HEADS, STRETCH), f32),
         ]
     extra = [] if first else list(carry)
-    w, wbc = kept_in_hbm(w), kept_in_hbm(wbc)
-    operands = [order, *pieces, *extra, gain, w, wbc, wdt, taps, dt_bias, a_log]
-    specs = [smem()] + [vmem()] * (4 + len(extra) + 1) + [in_hbm()] * 2 + [vmem()] * 4
+    operands = [order, *pieces, *([columns] if last else []), *extra, gain, w, wbc, wdt, taps, dt_bias, a_log]
+    specs = [smem()] + [vmem()] * (len(operands) - 1)
     return pl.pallas_call(
-        functools.partial(entry_kernel, which, first, last, rows),
+        functools.partial(entry_kernel, first, last, rows),
         out_shape=outs,
         in_specs=specs,
         out_specs=[vmem()] * len(outs),
         scratch_shapes=[
-            pltpu.VMEM((2048, 2 * LANES), bf16),
-            pltpu.VMEM((2048, 2 * STATE), bf16),
             pltpu.VMEM((HALO + BLOCK, 2048), bf16),
             pltpu.VMEM((HALO + BLOCK, LANES + 2 * STATE), f32),
-            pltpu.SemaphoreType.DMA((2, 4)),
         ],
-        compiler_params=pltpu.CompilerParams(vmem_limit_bytes=12 * MIB),
+        compiler_params=pltpu.CompilerParams(vmem_limit_bytes=8 * MIB),
         name="entry",
     )(*operands)
 
@@ -263,6 +303,7 @@
     k_pos = lax.broadcasted_iota(jnp.int32, (STRETCH, STRETCH), 1)
     causal = k_pos <= q_pos
     low_half = k_pos < HEAD_DIM
+    skips = spread_heads(skip[...], head_fan())[0:1, :]
     for j in range(rows // STRETCH):
         here = slice(j * STRETCH, (j + 1) * STRETCH)
         match = jnp.where(causal, dot(c[here, :], b[here, :], NT), 0.0)
@@ -280,7 +321,7 @@
                 [jnp.where(low_half, x, 0.0), jnp.where(low_half, 0.0, x)], axis=0
             ).astype(bf16)
             y_out[here, lanes] = (
-                dot(jnp.concatenate(weights, axis=1), stacked) + skip[:, lanes] * x
+                dot(jnp.concatenate(weights, axis=1), stacked) + skips[:, lanes] * x
             )
 
 
@@ -296,15 +337,11 @@
     )(xc, b, c, cum, step, skip)
 
 
-def exit_kernel(which, rows, order, mine, other, y, z, c, cum, ent, pri, gain, w_any, *refs):
-    (own, plus_a, plus_b, minus_a, minus_b, opp_a, opp_b), (wv, sems) = refs[:7], refs[7:]
-    outs = ((own, own), (plus_a, plus_b), (minus_a, minus_b), (opp_a, opp_b))
-    copies = []
-    for p in range(4):
-        source = pl.ds(pl.multiple_of(order[(0, 2, 1, 3)[p]] * 512, 512), 512)
-        copies.append(pltpu.make_async_copy(w_any.at[which, :, source], wv.at[p], sems.at[p]))
-    for k in copies:
-        k.start()
+def exit_kernel(chunks, order, mine, other, gain, wv, *refs):
+    parts = [refs[6 * i : 6 * i + 6] for i in range(chunks)]
+    own, plus_a, plus_b, minus_a, minus_b, opp_a, opp_b = refs[6 * chunks :]
+    split = chunks * BLOCK // 2
+    outs = ((plus_a, plus_b), (minus_a, minus_b), (opp_a, opp_b))
     fan = head_fan()
     row = lax.broadcasted_iota(jnp.int32, (BLOCK, BLOCK), 0) // HEAD_DIM
     lane = lax.broadcasted_iota(jnp.int32, (BLOCK, BLOCK), 1) // HEAD_DIM
@@ -312,10 +349,10 @@
     here, there = mine[...].astype(f32), other[...].astype(f32)
     even = order[4] == 0
     came = jnp.concatenate([jnp.where(even, here, there), jnp.where(even, there, here)], axis=1)
-    waited = False
-    for i in range(rows // BLOCK):
+    for i in range(chunks):
+        y, z, c, cum, ent, pri = parts[i]
         mixed = []
-        for j in (2 * i, 2 * i + 1):
+        for j in range(2):
             here = slice(j * STRETCH, (j + 1) * STRETCH)
             entering = (ent[j] + pri[j] * came).astype(bf16)
             carried = dot(c[here, :], entering) * spread_heads(jnp.exp(cum[:, here]), fan)
@@ -327,30 +364,29 @@
             scale = lax.rsqrt(sums * (1.0 / HEAD_DIM) + epsilon)
             mixed.append((gated * scale * gain[...]).astype(bf16))
         mixed = jnp.concatenate(mixed, axis=0)
-        if not waited:
-            for k in copies:
-                k.wait()
-            waited = True
-        for p in range(4):
-            out = outs[p][i]
-            at = i * BLOCK if p == 0 else 0
-            out[at : at + BLOCK, :] = dot(mixed, wv[p]).astype(bf16)
-
-
-def leave(which, order, mine, other, y, z, c, cum, ent, pri, gain, w):
-    w = kept_in_hbm(w)
-    rows = y.shape[0]
+        own[i * BLOCK : (i + 1) * BLOCK, :] = dot(mixed, wv[0]).astype(bf16)
+        for p in range(3):
+            product = dot(mixed, wv[p + 1]).astype(bf16)
+            for j in range(2):
+                at = i * BLOCK + j * STRETCH
+                out = outs[p][at // split]
+                at = at % split
+                out[at : at + STRETCH, :] = product[j * STRETCH : (j + 1) * STRETCH, :]
+
+
+def leave(order, mine, other, gain, w, parts):
+    rows = len(parts) * BLOCK
     shape = jax.ShapeDtypeStruct
-    outs = [shape((rows, LANES), bf16)] + [shape((BLOCK, LANES), bf16)] * 6
+    outs = [shape((rows, LANES), bf16)] + [shape((rows // 2, LANES), bf16)] * 6
+    operands = [order, mine, other, gain, w, *(a for part in parts for a in part)]
     return pl.pallas_call(
-        functools.partial(exit_kernel, which, rows),
+        functools.partial(exit_kernel, len(parts)),
         out_shape=outs,
-        in_specs=[smem()] + [vmem()] * 9 + [in_hbm()],
+        in_specs=[smem()] + [vmem()] * (len(operands) - 1),
         out_specs=[vmem()] * len(outs),
-        scratch_shapes=[pltpu.VMEM((4, LANES, LANES), bf16), pltpu.SemaphoreType.DMA((4,))],
-        compiler_params=pltpu.CompilerParams(vmem_limit_bytes=8 * MIB),
+        compiler_params=pltpu.CompilerParams(vmem_limit_bytes=6 * MIB),
         name="leave",
-    )(order, mine, other, y, z, c, cum, ent, pri, gain, w)
+    )(*operands)
 
 
 def small_call(kernel, name, outs, place, *operands):
@@ -367,7 +403,8 @@
 def chip_kernel(place, keep, got, out):
     even = place[4] == 0
     mine, other = opened(keep), opened(got)
-    out[...] = packed(*after(chosen(even, mine, other), chosen(even, other, mine))).astype(bf16)
+    both = after(chosen(even, mine, other), chosen(even, other, mine))
+    out[...] = packed(*both, columns_in(keep) + columns_in(got)).astype(bf16)
 
 
 def row_kernel(place, chip, one, two, three, row_out, before_out):
@@ -380,19 +417,43 @@
             here = chosen((y + 4 - at) % 4 == k, ring[k], here)
         before = chosen(at < y, after(before, here), before)
         row = after(row, here)
-    row_out[...] = packed(*row).astype(bf16)
-    before_out[...] = packed(*before)
-
-
-def arrive_kernel(place, one, two, three, before, keep, got, mine_out, other_out):
+    columns = sum(columns_in(r) for r in (chip, one, two, three))
+    row_out[...] = packed(*row, columns).astype(bf16)
+    before_out[...] = packed(*before, columns)
+
+
+def arrive_kernel(place, one, two, three, before, keep, got, mine_out, other_out, columns_out):
     even = place[4] == 0
+    z = place[6]
     came = nothing()
-    for r in (three, two, one):
-        came = after(came, opened(r))
+    for k, r in ((3, three), (2, two), (1, one)):
+        came = chosen(z >= k, after(came, opened(r)), came)
     first = after(came, opened(before))
     second = after(first, chosen(even, opened(keep), opened(got)))
     mine_out[...] = jnp.where(even, first[0], second[0]).astype(bf16)
     other_out[...] = jnp.where(even, second[0], first[0]).astype(bf16)
+    columns_out[...] = sum(columns_in(r) for r in (before, one, two, three))
+
+
+def give_kernel(columns, x, out):
+    cell = lax.broadcasted_iota(jnp.int32, (512, HALF), 0)
+    for part in range(2):
+        wanted = 2.0 * columns[2 * part : 2 * part + 1, :] + columns[2 * part + 1 : 2 * part + 2, :]
+        pick = (cell == wanted.astype(jnp.int32)).astype(bf16)
+        for r in range(2):
+            rows = dot(pick, x[r * 512 : (r + 1) * 512, :], TN).astype(bf16)
+            out[part * 16 : (part + 1) * 16, r * 16 : (r + 1) * 16, :] = rows.reshape(16, 16, 512)
+
+
+def given(columns, x):
+    return pl.pallas_call(
+        give_kernel,
+        out_shape=jax.ShapeDtypeStruct((32, 32, 512), bf16),
+        in_specs=[vmem()] * 2,
+        out_specs=vmem(),
+        compiler_params=pltpu.CompilerParams(vmem_limit_bytes=6 * MIB),
+        name="give",
+    )(columns, x)
 
 
 def turned(by):
@@ -407,7 +468,7 @@
     return lax.ppermute(x, "seq_2", [(0, 1), (1, 0)])
 
 
-def arriving_state(place, keep, send, beside):
+def arriving_state(place, keep, send, beside, wrapped):
     shape = jax.ShapeDtypeStruct
     got = swapped(send)
     msg = shape((MSG, HALF), bf16)
@@ -417,19 +478,19 @@
         row_kernel, "row", [msg, shape((MSG, HALF), f32)], place, chip, *ring
     )
     earlier = [
-        lax.ppermute(row, "seq_0", [(i, i + k) for i in range(4 - k)]) for k in (1, 2, 3)
+        lax.ppermute(row, "seq_0", turned(k)[: 4 if wrapped else 4 - k]) for k in (1, 2, 3)
     ]
-    mine, other = small_call(
+    mine, other, columns = small_call(
         arrive_kernel,
         "arrive",
-        [shape((STATE, HALF), bf16)] * 2,
+        [shape((STATE, HALF), bf16)] * 2 + [shape((8, HALF), f32)],
         behind(place, *beside),
         *earlier,
         before,
         keep,
         got,
     )
-    return mine, swapped(other)
+    return mine, swapped(other), columns
 
 
 def behind(x, *done):
@@ -439,67 +500,61 @@
 def with_halo(shard):
     count = lax.axis_size(SEQ)
     halo = lax.ppermute(shard[-HALO:], SEQ, [(i, i + 1) for i in range(count - 1)])
-    return jnp.concatenate([halo, shard[: shard.shape[0] // 2]], axis=0)
-
-
-def layer(which, shard, first, place, params, large, early=(), later=None):
+    return jnp.concatenate([halo, shard[:BLOCK]], axis=0)
+
+
+def gathered(shard, first, ahead, early):
+    count = shard.shape[0] // BLOCK
+    rows = [shard[i * BLOCK : (i + 1) * BLOCK] for i in range(count)]
+    own, left, right, opposite = [first], [], [], []
+    for i in range(count):
+        up = down = first
+        if i:
+            gates_up = [left[i - ahead], right[i - ahead]] if i >= ahead else []
+            gates_down = list(gates_up)
+            if i > ahead:
+                gates_up.append(opposite[i - ahead - 1])
+            if i == ahead:
+                gates_up += early
+                gates_down += early
+            own.append(rows[i])
+            up = behind(rows[i], first, *gates_up)
+            down = behind(rows[i], first, *gates_down)
+        left.append(around(up, 1))
+        right.append(around(down, -1))
+        opposite.append(around(left[i], 1) if i % 2 == 0 else around(right[i], -1))
+    return list(zip(own, left, right, opposite)), rows
+
+
+def layer(which, shard, first, place, params, large, columns, ahead, early=()):
     gain, wdt, taps, dt_bias, a_log, skip, out_gain = params
     w, wbc, w_out = large
-    half = shard.shape[0] // 2
-    halves = [shard[:half], shard[half:]]
-    own = [first, None]
-    left, right = [around(own[0], 1), None], [around(own[0], -1), None]
-    own[1] = behind(halves[1], left[0], right[0], *early)
-    opposite = [around(left[0], 1), None]
-    right[1] = around(own[1], -1)
-    left[1] = around(own[1], 1)
-    opposite[1] = around(right[1], -1)
-    extras = later(left[0]) if later else None
-    if later:
-        place, extras = lax.optimization_barrier((place, extras))
+    blocks, rows = gathered(shard, first, ahead, list(early))
+    wv, wbcv = staged(which, behind(place, first), w, wbc)
     carry = None
     kept = []
-    for i in range(2):
-        out = entry(
-            which,
-            place,
-            (own[i], left[i], right[i], opposite[i]),
-            carry,
-            gain,
-            w,
-            wbc,
-            wdt,
-            taps,
-            dt_bias,
-            a_log,
-            i == 1,
-        )
-        kept.append(out[:8])
+    for i, pieces in enumerate(blocks):
+        last = i == len(blocks) - 1
+        out = entry(place, pieces, columns, carry, gain, wv, wbcv, wdt, taps, dt_bias, a_log, last)
+        z, xc, b, c, cum, step, ent, pri = out[:8]
         carry = out[8:]
-    insides = [inside(*k[1:6], skip) for k in kept]
-    mine, other = arriving_state(place, *carry, insides)
+        kept.append((inside(xc, b, c, cum, step, skip), z, c, cum, ent, pri))
+    wov = staged_out(which, behind(place, carry[0]), w_out)
+    mine, other, columns = arriving_state(place, *carry, [k[0] for k in kept], which == 0)
     results = []
-    for i in range(2):
-        z, xc, b, c, cum, step, ent, pri = kept[i]
-        y = insides[i]
+    for low, high in ((0, 1), (1, 4)):
         own_part, plus_a, plus_b, minus_a, minus_b, opp_a, opp_b = leave(
-            which, place, mine, other, y, z, c, cum, ent, pri, out_gain, w_out
+            place, mine, other, out_gain, wov, kept[low:high]
         )
         across_a, across_b = around(opp_a, 1), around(opp_b, -1)
         down_a, up_b = around(minus_a, -1), around(plus_b, 1)
         up_a = around((plus_a.astype(f32) + across_a.astype(f32)).astype(bf16), 1)
         down_b = around((minus_b.astype(f32) + across_b.astype(f32)).astype(bf16), -1)
-        quarter = half // 2
-        parts = []
-        for rows, up, down in ((slice(0, quarter), up_a, down_a), (slice(quarter, half), up_b, down_b)):
-            parts.append(
-                halves[i][rows].astype(f32)
-                + own_part[rows].astype(f32)
-                + up.astype(f32)
-                + down.astype(f32)
-            )
-        results += parts
-    return jnp.concatenate(results, axis=0).astype(bf16), extras
+        here = jnp.concatenate(rows[low:high], axis=0).astype(f32) + own_part.astype(f32)
+        half = here.shape[0] // 2
+        for span, up, down in ((slice(0, half), up_a, down_a), (slice(half, 2 * half), up_b, down_b)):
+            results.append(here[span] + up.astype(f32) + down.astype(f32))
+    return jnp.concatenate(results, axis=0).astype(bf16), columns
 
 
 def permuted(x, source):
@@ -528,42 +583,45 @@
         arguments, first
     )
     x = lax.axis_index("tp")
-    core, y = lax.axis_index("seq_2"), lax.axis_index("seq_1")
-    place = jnp.stack([x, (x + 3) & 3, (x + 1) & 3, (x + 2) & 3, core, y]).astype(jnp.int32)
+    core, y, z = (lax.axis_index(a) for a in ("seq_2", "seq_1", "seq_0"))
+    place = jnp.stack([x, (x + 3) & 3, (x + 1) & 3, (x + 2) & 3, core, y, z]).astype(jnp.int32)
     w = w_in.reshape(2, 2048, 2 * LANES)
+
+    def on_lanes(heads):
+        return jnp.broadcast_to(heads[:, None], (HEADS, STRETCH))
 
     def params(which):
         return (
             in_gain[which].reshape(TP, 1, 512),
             w_dt[which].T.reshape(HEADS, TP, 512).transpose(1, 0, 2),
             jnp.concatenate([conv_x[which], conv_bc[which]], axis=1),
-            dt_bias[which].reshape(HEADS, 1),
-            a_log[which].reshape(HEADS, 1),
-            jnp.repeat(d_skip[which], HEAD_DIM).reshape(1, LANES),
+            on_lanes(dt_bias[which]),
+            on_lanes(a_log[which]),
+            on_lanes(d_skip[which]),
             out_gain[which].reshape(1, LANES),
         )
 
-    place, small, w = lax.optimization_barrier((place, [params(0), params(1)], w))
+    starts = col_order.reshape(16, 64)[:, 0]
+    slot = jnp.arange(512)
+    columns = jnp.where(
+        slot // 16 == lax.axis_index(SEQ), jnp.tile(starts % 512, 32), 0
+    ).reshape(2, 256)
+    columns = jnp.stack([columns[0] // 2, columns[0] % 2, columns[1] // 2, columns[1] % 2])
+    columns = jnp.pad(columns.astype(f32), ((0, 4), (0, 0)))
+    visit = jnp.arange(16)[:, None]
+    along = jnp.arange(64)[None, :]
+    row = jnp.where((starts >= 512)[:, None], 63 - along, along)
+    take = ((row // 2) * 32 + (row % 2) * 16 + visit).reshape(1024)
+    place, small, w, columns, take = lax.optimization_barrier(
+        (place, [params(0), params(1)], w, columns, take)
+    )
     large = (w, w_bc, w_out)
 
-    starts = col_order.reshape(16, 64)[:, 0]
-
-    def routes(gate):
-        own_columns = behind(starts % 512, gate)
-        columns = lax.all_to_all(
-            jnp.broadcast_to(own_columns[None], (32, 16)), SEQ, 0, 0, tiled=True
-        )
-        give = (columns.reshape(32, 1, 16) + 512 * jnp.arange(2)[None, :, None]).reshape(1024)
-        visit = jnp.arange(16)[:, None]
-        along = jnp.arange(64)[None, :]
-        row = jnp.where((starts >= 512)[:, None], 63 - along, along)
-        return give, ((row // 2) * 32 + (row % 2) * 16 + visit).reshape(1024)
-
-    row_result, (give, take) = layer(0, tokens, first, place, small[0], large, (w,), routes)
-    payload = permuted(row_result, give).reshape(32, 32, 512)
+    row_result, columns = layer(0, tokens, first, place, small[0], large, columns, 3, (w,))
+    payload = given(columns, row_result)
     arrived = lax.all_to_all(payload, SEQ, 0, 0, tiled=True).reshape(1024, 512)
     own_rows = permuted(arrived, take)
-    return layer(1, own_rows, with_halo(own_rows), place, small[1], large)[0]
+    return layer(1, own_rows, with_halo(own_rows), place, small[1], large, columns, 3)[0]
 
 
 def solution(mesh):

time: 299 us -> 295 us (0.987)
  waiting for transfers between devices: 108 us -> 82 us
  starting transfers between devices: 80.7 us -> 98.5 us
    ppermute x36 -> x48, starting transfers between devices: 48 us -> 66.5 us  [around(): return lax.ppermute(x, 'tp', turned(by))]
    ppermute x36 -> x48, waiting for transfers between devices: 83.4 us -> 71.4 us  [around(): return lax.ppermute(x, 'tp', turned(by))]
    all_to_all x1 -> x0, starting transfers between devices: 8.88 us -> none  [routes(): lax.all_to_all(jnp.broadcast_to(own_columns[None], (32, 16)), SEQ, 0, 0,...]
    ppermute x6, starting transfers between devices: 4.81 us -> 12.4 us  [arriving_state(): ring = [lax.ppermute(chip, 'seq_1', turned(k)) for k in (1, 2, 3)]]
    all_to_all x1 -> x0, waiting for transfers between devices: 7.15 us -> none  [routes(): lax.all_to_all(jnp.broadcast_to(own_columns[None], (32, 16)), SEQ, 0, 0,...]
    ppermute x6, waiting for transfers between devices: 11.3 us -> 7.42 us  [arriving_state(): ring = [lax.ppermute(chip, 'seq_1', turned(k)) for k in (1, 2, 3)]]
    pallas_call x4 -> x8, Pallas kernels: 5.16 us -> 6.41 us  [inside(): pl.pallas_call(functools.partial(inside_kernel, rows), out_shape=pltpu.VM...]
    pallas_call x8 -> x17, Pallas kernels: 51.9 us -> 52.3 us  [the longest x8 29.5 us: entry(): pl.pallas_call(functools.partial(entry_kernel, first, last, rows), out_sh...]
  transfers between devices with their start and end apart: 55 -> 66, of which waited for: 30 -> 26; matrix products, arithmetic and copies ran while one was open for 6% -> 6% of each run, Pallas kernels for 10% -> 16%
where the time goes in v4:
time: 295 us; the launch traced here: 290 us
  starting transfers between devices  98.5 us (33%)
  waiting for transfers between devices  82 us (28%)
  Pallas kernels  63.1 us (21%)
  blocking collectives  22.9 us (8%)
  local copies, waits for them, and re-layouts  17.4 us (6%)
  other arithmetic  3.49 us (1%)
    ppermute x48, waiting for transfers between devices, around(): return lax.ppermute(x, 'tp', turned(by))  71.4 us
    ppermute x48, starting transfers between devices, around(): return lax.ppermute(x, 'tp', turned(by))  66.5 us
    pallas_call x8, Pallas kernels, entry(): pl.pallas_call(functools.partial(entry_kernel, first, last, rows), out_sh...  29.5 us
    all_to_all x1, blocking collectives, body(): arrived = lax.all_to_all(payload, SEQ, 0, 0, tiled=True).reshape(1024, 512)  22.9 us
    ppermute x6, starting transfers between devices, arriving_state(): lax.ppermute(row, 'seq_0', turned(k)[:4 if wrapped else 4 - k])  15.9 us
    reshape x1, local copies, waits for them, and re-layouts, body(): w = w_in.reshape(2, 2048, 2 * LANES)  14.2 us
    ppermute x6, starting transfers between devices, arriving_state(): ring = [lax.ppermute(chip, 'seq_1', turned(k)) for k in (1, 2, 3)]  12.4 us
    pallas_call x4, Pallas kernels, leave(): pl.pallas_call(functools.partial(exit_kernel, len(parts)), out_shape=outs...  11.7 us
  transfers between devices with their start and end apart: 66, of which 26 were waited for; matrix products, arithmetic and copies ran while one was open for 6% of the time, Pallas kernels for 16%

profile of v4, /device:TPU:0, one launch (start us, length us, event | category | flops | bytes accessed | tf_op | source)
XLA Modules:
  0.0 290.1 jit_solution(7115993822585924651)
XLA Ops:
  14.7 14.2 %reshape.61.w = bf16[2,2048,1024]{2,1,0:T(8,128)(2,1)} reshape(bf16[2,2048,2,512]{3,2,1,0:T(2,128)(2,1)} %param.16) | data formatting | bytes 16777216 | tf_op jit(solution)/shard_map/reshape | solution.py:588
  34.7 4.5 %collective-permute-done.7.refs_2_ = bf16[256,512]{1,0:T(8,128)(2,1)S(1)} collective-permute-done((bf16[256,512]{1,0:T(8,128)(2,1)S(1)}, bf16[256,512]{1,0:T(8,128)(2,1)S(1)}, u32[]{:S(2)}, u32[]{:S(2)}) %collective-permute-start.7) | collective-permute-done | bytes 262176 | tf_op jit(solution)/shard_map/ppermute | solution.py:464
  62.9 4.8 %collective-permute-start.14 = (bf16[144,256]{1,0:T(8,128)(2,1)S(1)}, bf16[144,256]{1,0:T(8,128)(2,1)S(1)}, u32[]{:S(2)}, u32[]{:S(2)}) collective-permute-start(bf16[144,256]{1,0:T(8,128)(2,1)S(1)} %chip.2), channel_id=1, source_target_pairs={{0,8},{8,16},{16,24},{24,0},{1,9},{9,17},{17,25},{25,1},{2,10},{10... | collective-permute-start | bytes 221192 | tf_op jit(solution)/shard_map/ppermute | solution.py:476
  78.7 4.1 %collective-permute-start.18 = (bf16[144,256]{1,0:T(8,128)(2,1)S(1)}, bf16[144,256]{1,0:T(8,128)(2,1)S(1)}, u32[]{:S(2)}, u32[]{:S(2)}) collective-permute-start(bf16[144,256]{1,0:T(8,128)(2,1)S(1)} %get-tuple-element.230), channel_id=1, source_target_pairs={{0,64},{32,96},{64,0},{96,32},{1,65},{33,97},{65,1},{97,33},{2,66}... | collective-permute-start | bytes 221192 | tf_op jit(solution)/shard_map/ppermute | solution.py:481
  96.8 4.0 %leave.5 = (bf16[768,512]{1,0:T(8,128)(2,1)S(1)}, bf16[384,512]{1,0:T(8,128)(2,1)S(1)}, bf16[384,512]{1,0:T(8,128)(2,1)S(1)}, bf16[384,512]{1,0:T(8,128)(2,1)S(1...) custom-call(s32[7]{0:T(128)S(1)} %stack.46.order.refs_0_.place, ...), custom_call_target="tpu_custom_call" | custom-call | tf_op jit(solution)/shard_map/leave/pallas_call | solution.py:382
  107.9 5.9 %collective-permute-done.31 = bf16[384,512]{1,0:T(8,128)(2,1)S(1)} collective-permute-done((bf16[384,512]{1,0:T(8,128)(2,1)S(1)}, bf16[384,512]{1,0:T(8,128)(2,1)S(1)}, u32[]{:S(2)}, u32[]{:S(2)}) %collective-permute-start.31) | collective-permute-done | bytes 393248 | tf_op jit(solution)/shard_map/ppermute | solution.py:464
  121.0 3.9 %collective-permute-done.26 = bf16[128,512]{1,0:T(8,128)(2,1)S(1)} collective-permute-done((bf16[128,512]{1,0:T(8,128)(2,1)S(1)}, bf16[128,512]{1,0:T(8,128)(2,1)S(1)}, u32[]{:S(2)}, u32[]{:S(2)}) %collective-permute-start.26) | collective-permute-done | bytes 131104 | tf_op jit(solution)/shard_map/ppermute | solution.py:464
  127.7 4.1 %collective-permute-done.32 = bf16[384,512]{1,0:T(8,128)(2,1)S(1)} collective-permute-done((bf16[384,512]{1,0:T(8,128)(2,1)S(1)}, bf16[384,512]{1,0:T(8,128)(2,1)S(1)}, u32[]{:S(2)}, u32[]{:S(2)}) %collective-permute-start.32) | collective-permute-done | bytes 393248 | tf_op jit(solution)/shard_map/ppermute | solution.py:464
  131.8 3.7 %collective-permute-done.28 = bf16[384,512]{1,0:T(8,128)(2,1)S(1)} collective-permute-done((bf16[384,512]{1,0:T(8,128)(2,1)S(1)}, bf16[384,512]{1,0:T(8,128)(2,1)S(1)}, u32[]{:S(2)}, u32[]{:S(2)}) %collective-permute-start.28) | collective-permute-done | bytes 393248 | tf_op jit(solution)/shard_map/ppermute | solution.py:464
  136.7 22.9 %all_to_all.5 = bf16[32,32,512]{2,1,0:T(8,128)(2,1)S(1)} all-to-all(bf16[32,32,512]{2,1,0:T(8,128)(2,1)S(1)} %give.1), channel_id=1, replica_groups=mesh['seq_0'=4,'seq_1'=4,'seq_2'=2,'tp'=4] {'seq_0','seq_1','seq_2'}, dimensions={0} | all-to-all | bytes 2097152 | tf_op jit(solution)/shard_map/all_to_all | solution.py:622
  167.1 7.1 %collective-permute-done.34.refs_2_ = bf16[272,512]{1,0:T(8,128)(2,1)S(1)} collective-permute-done((bf16[272,512]{1,0:T(8,128)(2,1)S(1)}, bf16[272,512]{1,0:T(8,128)(2,1)S(1)}, u32[]{:S(2)}, u32[]{:S(2)}) %collective-permute-start.34) | collective-permute-done | bytes 278560 | tf_op jit(solution)/shard_map/ppermute | solution.py:464
  184.2 3.7 %collective-permute-start.39 = (bf16[256,512]{1,0:T(8,128)(2,1)S(1)}, bf16[256,512]{1,0:T(8,128)(2,1)S(1)}, u32[]{:S(2)}, u32[]{:S(2)}) collective-permute-start(bf16[256,512]{1,0:T(8,128)(2,1)S(1)} %collective-permute-done.38.refs_3_), channel_id=1, source_target_pairs={{0,3},{1,0},{2,1},{3,2},{4,7},{5,4},{6,5},{7,6},{8,11},{9,8},{10,9... | collective-permute-start | bytes 786440 | tf_op jit(solution)/shard_map/ppermute | solution.py:464
  187.9 7.2 %collective-permute-done.40.refs_2_ = bf16[256,512]{1,0:T(8,128)(2,1)S(1)} collective-permute-done((bf16[256,512]{1,0:T(8,128)(2,1)S(1)}, bf16[256,512]{1,0:T(8,128)(2,1)S(1)}, u32[]{:S(2)}, u32[]{:S(2)}) %collective-permute-start.40) | collective-permute-done | bytes 262176 | tf_op jit(solution)/shard_map/ppermute | solution.py:464
  203.6 3.7 %entry.12 = (bf16[256,512]{1,0:T(8,128)(2,1)S(1)}, bf16[256,512]{1,0:T(8,128)(2,1)S(1)}, bf16[256,128]{1,0:T(8,128)(2,1)S(1)}, bf16[256,128]{1,0:T(8,128)(2,1)S(...) custom-call(s32[7]{0:T(128)S(1)} %stack.46.order.refs_0_.place, ...), custom_call_target="tpu_custom_call" | custom-call | tf_op jit(solution)/shard_map/entry/pallas_call | solution.py:287
  207.3 3.7 %entry.13 = (bf16[256,512]{1,0:T(8,128)(2,1)S(1)}, bf16[256,512]{1,0:T(8,128)(2,1)S(1)}, bf16[256,128]{1,0:T(8,128)(2,1)S(1)}, bf16[256,128]{1,0:T(8,128)(2,1)S(...) custom-call(s32[7]{0:T(128)S(1)} %stack.46.order.refs_0_.place, ...), custom_call_target="tpu_custom_call" | custom-call | tf_op jit(solution)/shard_map/entry/pallas_call | solution.py:287
  211.0 3.7 %entry.14 = (bf16[256,512]{1,0:T(8,128)(2,1)S(1)}, bf16[256,512]{1,0:T(8,128)(2,1)S(1)}, bf16[256,128]{1,0:T(8,128)(2,1)S(1)}, bf16[256,128]{1,0:T(8,128)(2,1)S(...) custom-call(s32[7]{0:T(128)S(1)} %stack.46.order.refs_0_.place, ...), custom_call_target="tpu_custom_call" | custom-call | tf_op jit(solution)/shard_map/entry/pallas_call | solution.py:287
  214.7 3.7 %entry.15 = (bf16[256,512]{1,0:T(8,128)(2,1)S(1)}, bf16[256,512]{1,0:T(8,128)(2,1)S(1)}, bf16[256,128]{1,0:T(8,128)(2,1)S(1)}, bf16[256,128]{1,0:T(8,128)(2,1)S(...) custom-call(s32[7]{0:T(128)S(1)} %stack.46.order.refs_0_.place, ...), custom_call_target="tpu_custom_call" | custom-call | tf_op jit(solution)/shard_map/entry/pallas_call | solution.py:287
  223.7 3.9 %collective-permute-done.47.one = bf16[144,256]{1,0:T(8,128)(2,1)S(1)} collective-permute-done((bf16[144,256]{1,0:T(8,128)(2,1)S(1)}, bf16[144,256]{1,0:T(8,128)(2,1)S(1)}, u32[]{:S(2)}, u32[]{:S(2)}) %collective-permute-start.47) | collective-permute-done | bytes 73760 | tf_op jit(solution)/shard_map/ppermute | solution.py:476
  230.9 4.3 %collective-permute-start.51 = (bf16[144,256]{1,0:T(8,128)(2,1)S(1)}, bf16[144,256]{1,0:T(8,128)(2,1)S(1)}, u32[]{:S(2)}, u32[]{:S(2)}) collective-permute-start(bf16[144,256]{1,0:T(8,128)(2,1)S(1)} %get-tuple-element.307), channel_id=1, source_target_pairs={{0,64},{32,96},{1,65},{33,97},{2,66},{34,98},{3,67},{35,99},{4,68}... | collective-permute-start | bytes 221192 | tf_op jit(solution)/shard_map/ppermute | solution.py:481
  249.5 4.1 %leave.7 = (bf16[768,512]{1,0:T(8,128)(2,1)S(1)}, bf16[384,512]{1,0:T(8,128)(2,1)S(1)}, bf16[384,512]{1,0:T(8,128)(2,1)S(1)}, bf16[384,512]{1,0:T(8,128)(2,1)S(1...) custom-call(s32[7]{0:T(128)S(1)} %stack.46.order.refs_0_.place, ...), custom_call_target="tpu_custom_call" | custom-call | tf_op jit(solution)/shard_map/leave/pallas_call | solution.py:382
  260.6 5.9 %collective-permute-done.64 = bf16[384,512]{1,0:T(8,128)(2,1)S(1)} collective-permute-done((bf16[384,512]{1,0:T(8,128)(2,1)S(1)}, bf16[384,512]{1,0:T(8,128)(2,1)S(1)}, u32[]{:S(2)}, u32[]{:S(2)}) %collective-permute-start.64) | collective-permute-done | bytes 393248 | tf_op jit(solution)/shard_map/ppermute | solution.py:464
  273.7 3.9 %collective-permute-done.59 = bf16[128,512]{1,0:T(8,128)(2,1)S(1)} collective-permute-done((bf16[128,512]{1,0:T(8,128)(2,1)S(1)}, bf16[128,512]{1,0:T(8,128)(2,1)S(1)}, u32[]{:S(2)}, u32[]{:S(2)}) %collective-permute-start.59) | collective-permute-done | bytes 131104 | tf_op jit(solution)/shard_map/ppermute | solution.py:464
  280.5 3.9 %collective-permute-done.65 = bf16[384,512]{1,0:T(8,128)(2,1)S(1)} collective-permute-done((bf16[384,512]{1,0:T(8,128)(2,1)S(1)}, bf16[384,512]{1,0:T(8,128)(2,1)S(1)}, u32[]{:S(2)}, u32[]{:S(2)}) %collective-permute-start.65) | collective-permute-done | bytes 393248 | tf_op jit(solution)/shard_map/ppermute | solution.py:464
  284.5 3.7 %collective-permute-done.61 = bf16[384,512]{1,0:T(8,128)(2,1)S(1)} collective-permute-done((bf16[384,512]{1,0:T(8,128)(2,1)S(1)}, bf16[384,512]{1,0:T(8,128)(2,1)S(1)}, u32[]{:S(2)}, u32[]{:S(2)}) %collective-permute-start.61) | collective-permute-done | bytes 393248 | tf_op jit(solution)/shard_map/ppermute | solution.py:464
  (217 shorter events, 154.1 us)
Async XLA Ops:
  6.0 24.8 %collective-permute-start.2 = (bf16[272,512]{1,0:T(8,128)(2,1)S(1)}, bf16[272,512]{1,0:T(8,128)(2,1)S(1)}, u32[]{:S(2)}, u32[]{:S(2)}) collective-permute-start(bf16[272,512]{1,0:T(8,128)(2,1)S(1)} %pad_maximum_fusion.2.refs_1_), channel_id=1, source_target_pairs={{0,3},{1,0},{2,1},{3,2},{4,7},{5,4},{6,5},{7,6},{8,11},{9,8},{10,9... | collective-permute-start | bytes 835592 | tf_op jit(solution)/shard_map/ppermute | solution.py:464
  7.4 25.2 %collective-permute-start.5 = (bf16[256,512]{1,0:T(8,128)(2,1)S(1)}, bf16[256,512]{1,0:T(8,128)(2,1)S(1)}, u32[]{:S(2)}, u32[]{:S(2)}) collective-permute-start(bf16[256,512]{1,0:T(8,128)(2,1)S(1)} %get-tuple-element.199.refs_1_), channel_id=1, source_target_pairs={{0,3},{1,0},{2,1},{3,2},{4,7},{5,4},{6,5},{7,6},{8,11},{9,8},{10,9... | collective-permute-start | bytes 786440 | tf_op jit(solution)/shard_map/ppermute | solution.py:464
  9.3 24.0 %collective-permute-start.4 = (bf16[256,512]{1,0:T(8,128)(2,1)S(1)}, bf16[256,512]{1,0:T(8,128)(2,1)S(1)}, u32[]{:S(2)}, u32[]{:S(2)}) collective-permute-start(bf16[256,512]{1,0:T(8,128)(2,1)S(1)} %get-tuple-element.199.refs_1_), channel_id=1, source_target_pairs={{0,1},{1,2},{2,3},{3,0},{4,5},{5,6},{6,7},{7,4},{8,9},{9,10},{10,1... | collective-permute-start | bytes 786440 | tf_op jit(solution)/shard_map/ppermute | solution.py:464
  13.4 27.5 %collective-permute-start.3 = (bf16[272,512]{1,0:T(8,128)(2,1)S(1)}, bf16[272,512]{1,0:T(8,128)(2,1)S(1)}, u32[]{:S(2)}, u32[]{:S(2)}) collective-permute-start(bf16[272,512]{1,0:T(8,128)(2,1)S(1)} %collective-permute-done.1.refs_2_), channel_id=1, source_target_pairs={{0,1},{1,2},{2,3},{3,0},{4,5},{5,6},{6,7},{7,4},{8,9},{9,10},{10,1... | collective-permute-start | bytes 835592 | tf_op jit(solution)/shard_map/ppermute | solution.py:464
  32.6 17.2 %collective-permute-start.6 = (bf16[256,512]{1,0:T(8,128)(2,1)S(1)}, bf16[256,512]{1,0:T(8,128)(2,1)S(1)}, u32[]{:S(2)}, u32[]{:S(2)}) collective-permute-start(bf16[256,512]{1,0:T(8,128)(2,1)S(1)} %collective-permute-done.5.refs_3_), channel_id=1, source_target_pairs={{0,3},{1,0},{2,1},{3,2},{4,7},{5,4},{6,5},{7,6},{8,11},{9,8},{10,9... | collective-permute-start | bytes 786440 | tf_op jit(solution)/shard_map/ppermute | solution.py:464
  33.4 20.2 %collective-permute-start.8 = (bf16[256,512]{1,0:T(8,128)(2,1)S(1)}, bf16[256,512]{1,0:T(8,128)(2,1)S(1)}, u32[]{:S(2)}, u32[]{:S(2)}) collective-permute-start(bf16[256,512]{1,0:T(8,128)(2,1)S(1)} %get-tuple-element.208.refs_1_), channel_id=1, source_target_pairs={{0,3},{1,0},{2,1},{3,2},{4,7},{5,4},{6,5},{7,6},{8,11},{9,8},{10,9... | collective-permute-start | bytes 786440 | tf_op jit(solution)/shard_map/ppermute | solution.py:464
  39.2 14.4 %collective-permute-start.9 = (bf16[256,512]{1,0:T(8,128)(2,1)S(1)}, bf16[256,512]{1,0:T(8,128)(2,1)S(1)}, u32[]{:S(2)}, u32[]{:S(2)}) collective-permute-start(bf16[256,512]{1,0:T(8,128)(2,1)S(1)} %collective-permute-done.7.refs_2_), channel_id=1, source_target_pairs={{0,1},{1,2},{2,3},{3,0},{4,5},{5,6},{6,7},{7,4},{8,9},{9,10},{10,1... | collective-permute-start | bytes 786440 | tf_op jit(solution)/shard_map/ppermute | solution.py:464
  39.7 17.6 %collective-permute-start.10 = (bf16[256,512]{1,0:T(8,128)(2,1)S(1)}, bf16[256,512]{1,0:T(8,128)(2,1)S(1)}, u32[]{:S(2)}, u32[]{:S(2)}) collective-permute-start(bf16[256,512]{1,0:T(8,128)(2,1)S(1)} %get-tuple-element.217.refs_1_), channel_id=1, source_target_pairs={{0,1},{1,2},{2,3},{3,0},{4,5},{5,6},{6,7},{7,4},{8,9},{9,10},{10,1... | collective-permute-start | bytes 786440 | tf_op jit(solution)/shard_map/ppermute | solution.py:464
  40.9 16.4 %collective-permute-start.12 = (bf16[256,512]{1,0:T(8,128)(2,1)S(1)}, bf16[256,512]{1,0:T(8,128)(2,1)S(1)}, u32[]{:S(2)}, u32[]{:S(2)}) collective-permute-start(bf16[256,512]{1,0:T(8,128)(2,1)S(1)} %collective-permute-done.11.refs_3_), channel_id=1, source_target_pairs={{0,3},{1,0},{2,1},{3,2},{4,7},{5,4},{6,5},{7,6},{8,11},{9,8},{10,9... | collective-permute-start | bytes 786440 | tf_op jit(solution)/shard_map/ppermute | solution.py:464
  93.9 23.9 %collective-permute-start.23 = (bf16[128,512]{1,0:T(8,128)(2,1)S(1)}, bf16[128,512]{1,0:T(8,128)(2,1)S(1)}, u32[]{:S(2)}, u32[]{:S(2)}) collective-permute-start(bf16[128,512]{1,0:T(8,128)(2,1)S(1)} %get-tuple-element.243), channel_id=1, source_target_pairs={{0,3},{1,0},{2,1},{3,2},{4,7},{5,4},{6,5},{7,6},{8,11},{9,8},{10,9... | collective-permute-start | bytes 393224 | tf_op jit(solution)/shard_map/ppermute | solution.py:464
  96.8 21.9 %collective-permute-start.24 = (bf16[128,512]{1,0:T(8,128)(2,1)S(1)}, bf16[128,512]{1,0:T(8,128)(2,1)S(1)}, u32[]{:S(2)}, u32[]{:S(2)}) collective-permute-start(bf16[128,512]{1,0:T(8,128)(2,1)S(1)} %get-tuple-element.244), channel_id=1, source_target_pairs={{0,1},{1,2},{2,3},{3,0},{4,5},{5,6},{6,7},{7,4},{8,9},{9,10},{10,1... | collective-permute-start | bytes 393224 | tf_op jit(solution)/shard_map/ppermute | solution.py:464
  104.6 23.1 %collective-permute-start.29 = (bf16[384,512]{1,0:T(8,128)(2,1)S(1)}, bf16[384,512]{1,0:T(8,128)(2,1)S(1)}, u32[]{:S(2)}, u32[]{:S(2)}) collective-permute-start(bf16[384,512]{1,0:T(8,128)(2,1)S(1)} %get-tuple-element.259), channel_id=1, source_target_pairs={{0,3},{1,0},{2,1},{3,2},{4,7},{5,4},{6,5},{7,6},{8,11},{9,8},{10,9... | collective-permute-start | bytes 1179656 | tf_op jit(solution)/shard_map/ppermute | solution.py:464
  174.2 23.0 %collective-permute-start.36 = (bf16[272,512]{1,0:T(8,128)(2,1)S(1)}, bf16[272,512]{1,0:T(8,128)(2,1)S(1)}, u32[]{:S(2)}, u32[]{:S(2)}) collective-permute-start(bf16[272,512]{1,0:T(8,128)(2,1)S(1)} %collective-permute-done.34.refs_2_), channel_id=1, source_target_pairs={{0,1},{1,2},{2,3},{3,0},{4,5},{5,6},{6,7},{7,4},{8,9},{9,10},{10,1... | collective-permute-start | bytes 835592 | tf_op jit(solution)/shard_map/ppermute | solution.py:464
  177.4 17.6 %collective-permute-start.37 = (bf16[256,512]{1,0:T(8,128)(2,1)S(1)}, bf16[256,512]{1,0:T(8,128)(2,1)S(1)}, u32[]{:S(2)}, u32[]{:S(2)}) collective-permute-start(bf16[256,512]{1,0:T(8,128)(2,1)S(1)} %get-tuple-element.277.refs_1_), channel_id=1, source_target_pairs={{0,1},{1,2},{2,3},{3,0},{4,5},{5,6},{6,7},{7,4},{8,9},{9,10},{10,1... | collective-permute-start | bytes 786440 | tf_op jit(solution)/shard_map/ppermute | solution.py:464
  177.4 17.6 %collective-permute-start.40 = (bf16[256,512]{1,0:T(8,128)(2,1)S(1)}, bf16[256,512]{1,0:T(8,128)(2,1)S(1)}, u32[]{:S(2)}, u32[]{:S(2)}) collective-permute-start(bf16[256,512]{1,0:T(8,128)(2,1)S(1)} %get-tuple-element.286.refs_1_), channel_id=1, source_target_pairs={{0,1},{1,2},{2,3},{3,0},{4,5},{5,6},{6,7},{7,4},{8,9},{9,10},{10,1... | collective-permute-start | bytes 786440 | tf_op jit(solution)/shard_map/ppermute | solution.py:464
  177.5 19.6 %collective-permute-start.44 = (bf16[256,512]{1,0:T(8,128)(2,1)S(1)}, bf16[256,512]{1,0:T(8,128)(2,1)S(1)}, u32[]{:S(2)}, u32[]{:S(2)}) collective-permute-start(bf16[256,512]{1,0:T(8,128)(2,1)S(1)} %get-tuple-element.295.refs_1_), channel_id=1, source_target_pairs={{0,3},{1,0},{2,1},{3,2},{4,7},{5,4},{6,5},{7,6},{8,11},{9,8},{10,9... | collective-permute-start | bytes 786440 | tf_op jit(solution)/shard_map/ppermute | solution.py:464
  184.2 23.1 %collective-permute-start.39 = (bf16[256,512]{1,0:T(8,128)(2,1)S(1)}, bf16[256,512]{1,0:T(8,128)(2,1)S(1)}, u32[]{:S(2)}, u32[]{:S(2)}) collective-permute-start(bf16[256,512]{1,0:T(8,128)(2,1)S(1)} %collective-permute-done.38.refs_3_), channel_id=1, source_target_pairs={{0,3},{1,0},{2,1},{3,2},{4,7},{5,4},{6,5},{7,6},{8,11},{9,8},{10,9... | collective-permute-start | bytes 786440 | tf_op jit(solution)/shard_map/ppermute | solution.py:464
  195.1 15.9 %collective-permute-start.41 = (bf16[256,512]{1,0:T(8,128)(2,1)S(1)}, bf16[256,512]{1,0:T(8,128)(2,1)S(1)}, u32[]{:S(2)}, u32[]{:S(2)}) collective-permute-start(bf16[256,512]{1,0:T(8,128)(2,1)S(1)} %get-tuple-element.286.refs_1_), channel_id=1, source_target_pairs={{0,3},{1,0},{2,1},{3,2},{4,7},{5,4},{6,5},{7,6},{8,11},{9,8},{10,9... | collective-permute-start | bytes 786440 | tf_op jit(solution)/shard_map/ppermute | solution.py:464
  195.1 16.0 %collective-permute-start.42 = (bf16[256,512]{1,0:T(8,128)(2,1)S(1)}, bf16[256,512]{1,0:T(8,128)(2,1)S(1)}, u32[]{:S(2)}, u32[]{:S(2)}) collective-permute-start(bf16[256,512]{1,0:T(8,128)(2,1)S(1)} %collective-permute-done.40.refs_2_), channel_id=1, source_target_pairs={{0,1},{1,2},{2,3},{3,0},{4,5},{5,6},{6,7},{7,4},{8,9},{9,10},{10,1... | collective-permute-start | bytes 786440 | tf_op jit(solution)/shard_map/ppermute | solution.py:464
  197.1 17.6 %collective-permute-start.43 = (bf16[256,512]{1,0:T(8,128)(2,1)S(1)}, bf16[256,512]{1,0:T(8,128)(2,1)S(1)}, u32[]{:S(2)}, u32[]{:S(2)}) collective-permute-start(bf16[256,512]{1,0:T(8,128)(2,1)S(1)} %get-tuple-element.295.refs_1_), channel_id=1, source_target_pairs={{0,1},{1,2},{2,3},{3,0},{4,5},{5,6},{6,7},{7,4},{8,9},{9,10},{10,1... | collective-permute-start | bytes 786440 | tf_op jit(solution)/shard_map/ppermute | solution.py:464
  197.2 17.6 %collective-permute-start.45 = (bf16[256,512]{1,0:T(8,128)(2,1)S(1)}, bf16[256,512]{1,0:T(8,128)(2,1)S(1)}, u32[]{:S(2)}, u32[]{:S(2)}) collective-permute-start(bf16[256,512]{1,0:T(8,128)(2,1)S(1)} %collective-permute-done.44.refs_3_), channel_id=1, source_target_pairs={{0,3},{1,0},{2,1},{3,2},{4,7},{5,4},{6,5},{7,6},{8,11},{9,8},{10,9... | collective-permute-start | bytes 786440 | tf_op jit(solution)/shard_map/ppermute | solution.py:464
  247.3 23.1 %collective-permute-start.56 = (bf16[128,512]{1,0:T(8,128)(2,1)S(1)}, bf16[128,512]{1,0:T(8,128)(2,1)S(1)}, u32[]{:S(2)}, u32[]{:S(2)}) collective-permute-start(bf16[128,512]{1,0:T(8,128)(2,1)S(1)} %get-tuple-element.319), channel_id=1, source_target_pairs={{0,3},{1,0},{2,1},{3,2},{4,7},{5,4},{6,5},{7,6},{8,11},{9,8},{10,9... | collective-permute-start | bytes 393224 | tf_op jit(solution)/shard_map/ppermute | solution.py:464
  249.5 21.9 %collective-permute-start.57 = (bf16[128,512]{1,0:T(8,128)(2,1)S(1)}, bf16[128,512]{1,0:T(8,128)(2,1)S(1)}, u32[]{:S(2)}, u32[]{:S(2)}) collective-permute-start(bf16[128,512]{1,0:T(8,128)(2,1)S(1)} %get-tuple-element.320), channel_id=1, source_target_pairs={{0,1},{1,2},{2,3},{3,0},{4,5},{5,6},{6,7},{7,4},{8,9},{9,10},{10,1... | collective-permute-start | bytes 393224 | tf_op jit(solution)/shard_map/ppermute | solution.py:464
  257.2 23.3 %collective-permute-start.62 = (bf16[384,512]{1,0:T(8,128)(2,1)S(1)}, bf16[384,512]{1,0:T(8,128)(2,1)S(1)}, u32[]{:S(2)}, u32[]{:S(2)}) collective-permute-start(bf16[384,512]{1,0:T(8,128)(2,1)S(1)} %get-tuple-element.335), channel_id=1, source_target_pairs={{0,3},{1,0},{2,1},{3,2},{4,7},{5,4},{6,5},{7,6},{8,11},{9,8},{10,9... | collective-permute-start | bytes 1179656 | tf_op jit(solution)/shard_map/ppermute | solution.py:464
  (52 other events, 461.1 us)

commit v5 on v4

--- a/solution.py
+++ b/solution.py
@@ -81,10 +81,9 @@
     return (row % HEADS == lane // HEAD_DIM).astype(bf16)
 
 
-def entry_kernel(first, last, rows, *refs):
+def entry_kernel(first, last, offset, rows, *refs):
     (order, own, left, right, opposite) = refs[:5]
     refs = refs[5:]
-    ahead = HALO if first else 0
     columns = ()
     if last:
         columns, refs = refs[:1], refs[1:]
@@ -114,7 +113,7 @@
         xbuf[0:HALO, :] = tail_in[...]
     for i in range(rows // BLOCK):
         span = pl.ds(i * BLOCK, BLOCK)
-        above = pl.ds(ahead + i * BLOCK, BLOCK)
+        above = pl.ds(offset + i * BLOCK, BLOCK)
         pieces = [r[above, :] for r in (own, left, right, opposite)]
         widen = [x.astype(f32) for x in pieces]
         square = sum(jnp.sum(x * x, axis=1, keepdims=True) for x in widen)
@@ -259,9 +258,9 @@
     return pltpu.with_memory_space_constraint(x, pltpu.HBM)
 
 
-def entry(order, pieces, columns, carry, gain, w, wbc, wdt, taps, dt_bias, a_log, last):
+def entry(order, pieces, offset, columns, carry, gain, w, wbc, wdt, taps, dt_bias, a_log, last):
     first = carry is None
-    rows = pieces[0].shape[0] - (HALO if first else 0)
+    rows = BLOCK
     shape = jax.ShapeDtypeStruct
     outs = [
         pltpu.VMEM((rows, LANES), bf16),
@@ -285,7 +284,7 @@
     operands = [order, *pieces, *([columns] if last else []), *extra, gain, w, wbc, wdt, taps, dt_bias, a_log]
     specs = [smem()] + [vmem()] * (len(operands) - 1)
     return pl.pallas_call(
-        functools.partial(entry_kernel, first, last, rows),
+        functools.partial(entry_kernel, first, last, offset, rows),
         out_shape=outs,
         in_specs=specs,
         out_specs=[vmem()] * len(outs),
@@ -339,9 +338,9 @@
 
 def exit_kernel(chunks, order, mine, other, gain, wv, *refs):
     parts = [refs[6 * i : 6 * i + 6] for i in range(chunks)]
-    own, plus_a, plus_b, minus_a, minus_b, opp_a, opp_b = refs[6 * chunks :]
+    own, up, down, plus_a, minus_b = refs[6 * chunks :]
     split = chunks * BLOCK // 2
-    outs = ((plus_a, plus_b), (minus_a, minus_b), (opp_a, opp_b))
+    outs = (((plus_a, 0), (up, split)), ((down, split), (minus_b, 0)), ((up, 0), (down, 0)))
     fan = head_fan()
     row = lax.broadcasted_iota(jnp.int32, (BLOCK, BLOCK), 0) // HEAD_DIM
     lane = lax.broadcasted_iota(jnp.int32, (BLOCK, BLOCK), 1) // HEAD_DIM
@@ -369,15 +368,15 @@
             product = dot(mixed, wv[p + 1]).astype(bf16)
             for j in range(2):
                 at = i * BLOCK + j * STRETCH
-                out = outs[p][at // split]
-                at = at % split
+                out, base = outs[p][at // split]
+                at = base + at % split
                 out[at : at + STRETCH, :] = product[j * STRETCH : (j + 1) * STRETCH, :]
 
 
 def leave(order, mine, other, gain, w, parts):
     rows = len(parts) * BLOCK
     shape = jax.ShapeDtypeStruct
-    outs = [shape((rows, LANES), bf16)] + [shape((rows // 2, LANES), bf16)] * 6
+    outs = [shape((rows, LANES), bf16)] * 3 + [shape((rows // 2, LANES), bf16)] * 2
     operands = [order, mine, other, gain, w, *(a for part in parts for a in part)]
     return pl.pallas_call(
         functools.partial(exit_kernel, len(parts)),
@@ -407,32 +406,36 @@
     out[...] = packed(*both, columns_in(keep) + columns_in(got)).astype(bf16)
 
 
-def row_kernel(place, chip, one, two, three, row_out, before_out):
-    y = place[5]
-    ring = [opened(r) for r in (chip, one, two, three)]
-    row, before = nothing(), nothing()
-    for at in range(4):
-        here = ring[0]
-        for k in range(1, 4):
-            here = chosen((y + 4 - at) % 4 == k, ring[k], here)
-        before = chosen(at < y, after(before, here), before)
-        row = after(row, here)
-    columns = sum(columns_in(r) for r in (chip, one, two, three))
-    row_out[...] = packed(*row, columns).astype(bf16)
-    before_out[...] = packed(*before, columns)
-
-
-def arrive_kernel(place, one, two, three, before, keep, got, mine_out, other_out, columns_out):
+def pair_kernel(axis, place, mine, other, pair_out, before_out):
+    odd = place[axis] % 2 == 1
+    here, there = opened(mine), opened(other)
+    pair = after(chosen(odd, there, here), chosen(odd, here, there))
+    columns = columns_in(mine) + columns_in(other)
+    pair_out[...] = packed(*pair, columns).astype(bf16)
+    before_out[...] = packed(*chosen(odd, there, nothing()), columns)
+
+
+def ring_kernel(axis, place, mine, other, before, ring_out, before_out):
+    upper = place[axis] >= 2
+    here, there = opened(mine), opened(other)
+    ring = after(chosen(upper, there, here), chosen(upper, here, there))
+    columns = columns_in(mine) + columns_in(other)
+    ring_out[...] = packed(*ring, columns).astype(bf16)
+    came = after(chosen(upper, there, nothing()), opened(before))
+    before_out[...] = packed(*came, columns)
+
+
+def arrive_kernel(
+    place, mine, other, before_z, before_y, keep, got, mine_out, other_out, columns_out
+):
     even = place[4] == 0
-    z = place[6]
-    came = nothing()
-    for k, r in ((3, three), (2, two), (1, one)):
-        came = chosen(z >= k, after(came, opened(r)), came)
-    first = after(came, opened(before))
+    upper = place[6] >= 2
+    came = after(chosen(upper, opened(other), nothing()), opened(before_z))
+    first = after(came, opened(before_y))
     second = after(first, chosen(even, opened(keep), opened(got)))
     mine_out[...] = jnp.where(even, first[0], second[0]).astype(bf16)
     other_out[...] = jnp.where(even, second[0], first[0]).astype(bf16)
-    columns_out[...] = sum(columns_in(r) for r in (before, one, two, three))
+    columns_out[...] = columns_in(mine) + columns_in(other)
 
 
 def give_kernel(columns, x, out):
@@ -468,24 +471,33 @@
     return lax.ppermute(x, "seq_2", [(0, 1), (1, 0)])
 
 
-def arriving_state(place, keep, send, beside, wrapped):
+def arriving_state(place, keep, send, weights, beside):
     shape = jax.ShapeDtypeStruct
+    msg, wide = shape((MSG, HALF), bf16), shape((MSG, HALF), f32)
+    within, across = [(0, 1), (1, 0), (2, 3), (3, 2)], [(0, 3), (3, 0), (1, 2), (2, 1)]
+
+    def scanned(kernel, axis, name, place, *operands):
+        return small_call(functools.partial(kernel, axis), name, [msg, wide], place, *operands)
+
     got = swapped(send)
-    msg = shape((MSG, HALF), bf16)
     (chip,) = small_call(chip_kernel, "chip", [msg], place, keep, got)
-    ring = [lax.ppermute(chip, "seq_1", turned(k)) for k in (1, 2, 3)]
-    row, before = small_call(
-        row_kernel, "row", [msg, shape((MSG, HALF), f32)], place, chip, *ring
+    pair, before = scanned(
+        pair_kernel, 5, "pair_y", behind(place, weights), chip, lax.ppermute(chip, "seq_1", within)
     )
-    earlier = [
-        lax.ppermute(row, "seq_0", turned(k)[: 4 if wrapped else 4 - k]) for k in (1, 2, 3)
-    ]
+    ring, before = scanned(
+        ring_kernel, 5, "ring_y", place, pair, lax.ppermute(pair, "seq_1", across), before
+    )
+    pair, before_z = scanned(
+        pair_kernel, 6, "pair_z", behind(place, *beside[:1]), ring, lax.ppermute(ring, "seq_0", within)
+    )
     mine, other, columns = small_call(
         arrive_kernel,
         "arrive",
         [shape((STATE, HALF), bf16)] * 2 + [shape((8, HALF), f32)],
         behind(place, *beside),
-        *earlier,
+        pair,
+        lax.ppermute(pair, "seq_0", across),
+        before_z,
         before,
         keep,
         got,
@@ -500,60 +512,55 @@
 def with_halo(shard):
     count = lax.axis_size(SEQ)
     halo = lax.ppermute(shard[-HALO:], SEQ, [(i, i + 1) for i in range(count - 1)])
-    return jnp.concatenate([halo, shard[:BLOCK]], axis=0)
-
-
-def gathered(shard, first, ahead, early):
-    count = shard.shape[0] // BLOCK
-    rows = [shard[i * BLOCK : (i + 1) * BLOCK] for i in range(count)]
-    own, left, right, opposite = [first], [], [], []
-    for i in range(count):
-        up = down = first
-        if i:
-            gates_up = [left[i - ahead], right[i - ahead]] if i >= ahead else []
-            gates_down = list(gates_up)
-            if i > ahead:
-                gates_up.append(opposite[i - ahead - 1])
-            if i == ahead:
-                gates_up += early
-                gates_down += early
-            own.append(rows[i])
-            up = behind(rows[i], first, *gates_up)
-            down = behind(rows[i], first, *gates_down)
-        left.append(around(up, 1))
-        right.append(around(down, -1))
-        opposite.append(around(left[i], 1) if i % 2 == 0 else around(right[i], -1))
-    return list(zip(own, left, right, opposite)), rows
-
-
-def layer(which, shard, first, place, params, large, columns, ahead, early=()):
+    return jnp.concatenate([halo, shard[: 2 * BLOCK]], axis=0)
+
+
+def layer(which, shard, first, place, params, large, columns, early):
     gain, wdt, taps, dt_bias, a_log, skip, out_gain = params
     w, wbc, w_out = large
-    blocks, rows = gathered(shard, first, ahead, list(early))
+    rows = [first, shard[2 * BLOCK : 3 * BLOCK], shard[3 * BLOCK :]]
     wv, wbcv = staged(which, behind(place, first), w, wbc)
-    carry = None
-    kept = []
-    for i, pieces in enumerate(blocks):
-        last = i == len(blocks) - 1
-        out = entry(place, pieces, columns, carry, gain, wv, wbcv, wdt, taps, dt_bias, a_log, last)
+    carry, kept, gate = None, [], place
+
+    def enter(i, pieces, offset, last=False):
+        nonlocal carry, gate
+        out = entry(
+            gate, pieces, offset, columns, carry, gain, wv, wbcv, wdt, taps, dt_bias, a_log, last
+        )
         z, xc, b, c, cum, step, ent, pri = out[:8]
         carry = out[8:]
-        kept.append((inside(xc, b, c, cum, step, skip), z, c, cum, ent, pri))
+        y = inside(xc, b, c, cum, step, skip)
+        kept.append((y, z, c, cum, ent, pri))
+        if i < 2:
+            gate = behind(place, y)
+
+    own = [first, behind(rows[1], first), behind(rows[2], first)]
+    left, right = [around(first, 1)], [around(first, -1)]
+    right.append(around(own[1], -1))
+    opposite = [around(left[0], 1)]
+    right.append(around(behind(rows[2], right[0], wbcv) if which else own[2], -1))
+    left.append(around(behind(rows[1], right[1], *early), 1))
+    opposite.append(around(right[1], -1))
+    pieces = (own[0], left[0], right[0], opposite[0])
+    enter(0, pieces, HALO)
+    left.append(around(behind(rows[2], carry[0]), 1))
+    opposite.append(around(right[2], -1))
+    enter(1, pieces, HALO + BLOCK)
+    enter(2, (own[1], left[1], right[1], opposite[1]), 0)
+    enter(3, (own[2], left[2], right[2], opposite[2]), 0, True)
     wov = staged_out(which, behind(place, carry[0]), w_out)
-    mine, other, columns = arriving_state(place, *carry, [k[0] for k in kept], which == 0)
+    mine, other, columns = arriving_state(place, *carry, wov, [k[0] for k in kept])
     results = []
-    for low, high in ((0, 1), (1, 4)):
-        own_part, plus_a, plus_b, minus_a, minus_b, opp_a, opp_b = leave(
-            place, mine, other, out_gain, wov, kept[low:high]
+    for low in (0, 2):
+        own_part, up, down, plus_a, minus_b = leave(
+            place, mine, other, out_gain, wov, kept[low : low + 2]
         )
-        across_a, across_b = around(opp_a, 1), around(opp_b, -1)
-        down_a, up_b = around(minus_a, -1), around(plus_b, 1)
-        up_a = around((plus_a.astype(f32) + across_a.astype(f32)).astype(bf16), 1)
-        down_b = around((minus_b.astype(f32) + across_b.astype(f32)).astype(bf16), -1)
-        here = jnp.concatenate(rows[low:high], axis=0).astype(f32) + own_part.astype(f32)
-        half = here.shape[0] // 2
-        for span, up, down in ((slice(0, half), up_a, down_a), (slice(half, 2 * half), up_b, down_b)):
-            results.append(here[span] + up.astype(f32) + down.astype(f32))
+        up, down = around(up, 1), around(down, -1)
+        plus_a = around((plus_a.astype(f32) + up[:BLOCK].astype(f32)).astype(bf16), 1)
+        minus_b = around((minus_b.astype(f32) + down[:BLOCK].astype(f32)).astype(bf16), -1)
+        here = shard[low * BLOCK : (low + 2) * BLOCK].astype(f32) + own_part.astype(f32)
+        results.append(here[:BLOCK] + plus_a.astype(f32) + down[BLOCK:].astype(f32))
+        results.append(here[BLOCK:] + up[BLOCK:].astype(f32) + minus_b.astype(f32))
     return jnp.concatenate(results, axis=0).astype(bf16), columns
 
 
@@ -617,11 +624,11 @@
     )
     large = (w, w_bc, w_out)
 
-    row_result, columns = layer(0, tokens, first, place, small[0], large, columns, 3, (w,))
+    row_result, columns = layer(0, tokens, first, place, small[0], large, columns, (w,))
     payload = given(columns, row_result)
     arrived = lax.all_to_all(payload, SEQ, 0, 0, tiled=True).reshape(1024, 512)
     own_rows = permuted(arrived, take)
-    return layer(1, own_rows, with_halo(own_rows), place, small[1], large, columns, 3)[0]
+    return layer(1, own_rows, with_halo(own_rows), place, small[1], large, columns, ())[0]
 
 
 def solution(mesh):

time: 295 us -> 293 us (level)
  starting transfers between devices: 98.5 us -> 76.7 us
  waiting for transfers between devices: 82 us -> 99.4 us
    ppermute x48 -> x34, starting transfers between devices: 66.5 us -> 55.1 us  [around(): return lax.ppermute(x, 'tp', turned(by))]
    ppermute x12 -> x8, waiting for transfers between devices: 7.58 us -> 18.6 us  [the longest x2 6.67 us: arriving_state(): lax.ppermute(ring, 'seq_0', within)]
    ppermute x12 -> x8, starting transfers between devices: 28.3 us -> 17.4 us  [the longest x2 5.58 us: arriving_state(): lax.ppermute(pair, 'seq_0', across)]
    ppermute x48 -> x34, waiting for transfers between devices: 71.4 us -> 75.1 us  [around(): return lax.ppermute(x, 'tp', turned(by))]
    pallas_call x6 -> x10, Pallas kernels: 4.39 us -> 6.47 us  [small_call(): pl.pallas_call(kernel, out_shape=outs, in_specs=[smem()] + [vmem()] * len...]
  transfers between devices with their start and end apart: 66 -> 48, of which waited for: 26 -> 29; matrix products, arithmetic and copies ran while one was open for 6% -> 6% of each run, Pallas kernels for 16% -> 16%
where the time goes in v5:
time: 293 us; the launch traced here: 288 us
  waiting for transfers between devices  99.4 us (34%)
  starting transfers between devices  76.7 us (26%)
  Pallas kernels  65.3 us (22%)
  blocking collectives  23.2 us (8%)
  local copies, waits for them, and re-layouts  17.2 us (6%)
  other arithmetic  3.57 us (1%)
    ppermute x34, waiting for transfers between devices, around(): return lax.ppermute(x, 'tp', turned(by))  75.1 us
    ppermute x34, starting transfers between devices, around(): return lax.ppermute(x, 'tp', turned(by))  55.1 us
    pallas_call x8, Pallas kernels, entry(): pl.pallas_call(functools.partial(entry_kernel, first, last, offset, rows)...  29.6 us
    all_to_all x1, blocking collectives, body(): arrived = lax.all_to_all(payload, SEQ, 0, 0, tiled=True).reshape(1024, 512)  23.2 us
    reshape x1, local copies, waits for them, and re-layouts, body(): w = w_in.reshape(2, 2048, 2 * LANES)  14.3 us
    pallas_call x4, Pallas kernels, leave(): pl.pallas_call(functools.partial(exit_kernel, len(parts)), out_shape=outs...  11.8 us
    ppermute x2, waiting for transfers between devices, arriving_state(): lax.ppermute(ring, 'seq_0', within)  6.67 us
    pallas_call x10, Pallas kernels, small_call(): pl.pallas_call(kernel, out_shape=outs, in_specs=[smem()] + [vmem()] * len...  6.47 us
  transfers between devices with their start and end apart: 48, of which 29 were waited for; matrix products, arithmetic and copies ran while one was open for 6% of the time, Pallas kernels for 16%

profile of v5, /device:TPU:0, one launch (start us, length us, event | category | flops | bytes accessed | tf_op | source)
XLA Modules:
  0.0 287.6 jit_solution(13656593328526406537)
XLA Ops:
  10.4 8.4 %collective-permute-done.1.refs_2_ = bf16[528,512]{1,0:T(8,128)(2,1)S(1)} collective-permute-done((bf16[528,512]{1,0:T(8,128)(2,1)S(1)}, bf16[528,512]{1,0:T(8,128)(2,1)S(1)}, u32[]{:S(2)}, u32[]{:S(2)}) %collective-permute-start.1) | collective-permute-done | bytes 540704 | tf_op jit(solution)/shard_map/ppermute | solution.py:467
  20.2 14.3 %reshape.61.w = bf16[2,2048,1024]{2,1,0:T(8,128)(2,1)} reshape(bf16[2,2048,2,512]{3,2,1,0:T(2,128)(2,1)} %param.16) | data formatting | bytes 16777216 | tf_op jit(solution)/shard_map/reshape | solution.py:595
  52.5 3.7 %entry.10 = (bf16[256,512]{1,0:T(8,128)(2,1)S(1)}, bf16[256,512]{1,0:T(8,128)(2,1)S(1)}, bf16[256,128]{1,0:T(8,128)(2,1)S(1)}, bf16[256,128]{1,0:T(8,128)(2,1)S(...) custom-call(s32[7]{0:T(128)S(1)} %stack.46.order.refs_0_.place, ...), custom_call_target="tpu_custom_call" | custom-call | tf_op jit(solution)/shard_map/entry/pallas_call | solution.py:286
  80.4 4.2 %collective-permute-start.14 = (bf16[144,256]{1,0:T(8,128)(2,1)S(1)}, bf16[144,256]{1,0:T(8,128)(2,1)S(1)}, u32[]{:S(2)}, u32[]{:S(2)}) collective-permute-start(bf16[144,256]{1,0:T(8,128)(2,1)S(1)} %get-tuple-element.247.mine), channel_id=1, source_target_pairs={{0,96},{96,0},{32,64},{64,32},{1,97},{97,1},{33,65},{65,33},{2,98}... | collective-permute-start | bytes 221192 | tf_op jit(solution)/shard_map/ppermute | solution.py:499
  101.3 5.8 %collective-permute-done.18 = bf16[512,512]{1,0:T(8,128)(2,1)S(1)} collective-permute-done((bf16[512,512]{1,0:T(8,128)(2,1)S(1)}, bf16[512,512]{1,0:T(8,128)(2,1)S(1)}, u32[]{:S(2)}, u32[]{:S(2)}) %collective-permute-start.18) | collective-permute-done | bytes 524320 | tf_op jit(solution)/shard_map/ppermute | solution.py:467
  107.2 3.7 %collective-permute-start.19 = (bf16[256,512]{1,0:T(8,128)(2,1)S(1)}, bf16[256,512]{1,0:T(8,128)(2,1)S(1)}, u32[]{:S(2)}, u32[]{:S(2)}) collective-permute-start(bf16[256,512]{1,0:T(8,128)(2,1)S(1)} %add_convert_fusion.6), channel_id=1, source_target_pairs={{0,3},{1,0},{2,1},{3,2},{4,7},{5,4},{6,5},{7,6},{8,11},{9,8},{10,9... | collective-permute-start | bytes 786440 | tf_op jit(solution)/shard_map/ppermute | solution.py:467
  111.1 7.3 %collective-permute-done.22 = bf16[512,512]{1,0:T(8,128)(2,1)S(1)} collective-permute-done((bf16[512,512]{1,0:T(8,128)(2,1)S(1)}, bf16[512,512]{1,0:T(8,128)(2,1)S(1)}, u32[]{:S(2)}, u32[]{:S(2)}) %collective-permute-start.22) | collective-permute-done | bytes 524320 | tf_op jit(solution)/shard_map/ppermute | solution.py:467
  118.4 3.7 %collective-permute-start.23 = (bf16[256,512]{1,0:T(8,128)(2,1)S(1)}, bf16[256,512]{1,0:T(8,128)(2,1)S(1)}, u32[]{:S(2)}, u32[]{:S(2)}) collective-permute-start(bf16[256,512]{1,0:T(8,128)(2,1)S(1)} %add_convert_fusion.4), channel_id=1, source_target_pairs={{0,3},{1,0},{2,1},{3,2},{4,7},{5,4},{6,5},{7,6},{8,11},{9,8},{10,9... | collective-permute-start | bytes 786440 | tf_op jit(solution)/shard_map/ppermute | solution.py:467
  133.2 23.2 %all_to_all.5 = bf16[32,32,512]{2,1,0:T(8,128)(2,1)S(1)} all-to-all(bf16[32,32,512]{2,1,0:T(8,128)(2,1)S(1)} %give.1), channel_id=1, replica_groups=mesh['seq_0'=4,'seq_1'=4,'seq_2'=2,'tp'=4] {'seq_0','seq_1','seq_2'}, dimensions={0} | all-to-all | bytes 2097152 | tf_op jit(solution)/shard_map/all_to_all | solution.py:629
  163.9 12.8 %collective-permute-done.25.refs_2_ = bf16[528,512]{1,0:T(8,128)(2,1)S(1)} collective-permute-done((bf16[528,512]{1,0:T(8,128)(2,1)S(1)}, bf16[528,512]{1,0:T(8,128)(2,1)S(1)}, u32[]{:S(2)}, u32[]{:S(2)}) %collective-permute-start.25) | collective-permute-done | bytes 540704 | tf_op jit(solution)/shard_map/ppermute | solution.py:467
  183.1 6.7 %collective-permute-done.28.refs_3_ = bf16[256,512]{1,0:T(8,128)(2,1)S(1)} collective-permute-done((bf16[256,512]{1,0:T(8,128)(2,1)S(1)}, bf16[256,512]{1,0:T(8,128)(2,1)S(1)}, u32[]{:S(2)}, u32[]{:S(2)}) %collective-permute-start.28) | collective-permute-done | bytes 262176 | tf_op jit(solution)/shard_map/ppermute | solution.py:467
  189.8 3.7 %collective-permute-start.30 = (bf16[256,512]{1,0:T(8,128)(2,1)S(1)}, bf16[256,512]{1,0:T(8,128)(2,1)S(1)}, u32[]{:S(2)}, u32[]{:S(2)}) collective-permute-start(bf16[256,512]{1,0:T(8,128)(2,1)S(1)} %collective-permute-done.28.refs_3_), channel_id=1, source_target_pairs={{0,3},{1,0},{2,1},{3,2},{4,7},{5,4},{6,5},{7,6},{8,11},{9,8},{10,9... | collective-permute-start | bytes 786440 | tf_op jit(solution)/shard_map/ppermute | solution.py:467
  195.4 3.7 %collective-permute-start.33 = (bf16[256,512]{1,0:T(8,128)(2,1)S(1)}, bf16[256,512]{1,0:T(8,128)(2,1)S(1)}, u32[]{:S(2)}, u32[]{:S(2)}) collective-permute-start(bf16[256,512]{1,0:T(8,128)(2,1)S(1)} %collective-permute-done.32.refs_3_), channel_id=1, source_target_pairs={{0,3},{1,0},{2,1},{3,2},{4,7},{5,4},{6,5},{7,6},{8,11},{9,8},{10,9... | collective-permute-start | bytes 786440 | tf_op jit(solution)/shard_map/ppermute | solution.py:467
  199.1 3.7 %entry.12 = (bf16[256,512]{1,0:T(8,128)(2,1)S(1)}, bf16[256,512]{1,0:T(8,128)(2,1)S(1)}, bf16[256,128]{1,0:T(8,128)(2,1)S(1)}, bf16[256,128]{1,0:T(8,128)(2,1)S(...) custom-call(s32[7]{0:T(128)S(1)} %stack.46.order.refs_0_.place, ...), custom_call_target="tpu_custom_call" | custom-call | tf_op jit(solution)/shard_map/entry/pallas_call | solution.py:286
  203.9 3.7 %entry.13 = (bf16[256,512]{1,0:T(8,128)(2,1)S(1)}, bf16[256,512]{1,0:T(8,128)(2,1)S(1)}, bf16[256,128]{1,0:T(8,128)(2,1)S(1)}, bf16[256,128]{1,0:T(8,128)(2,1)S(...) custom-call(s32[7]{0:T(128)S(1)} %stack.46.order.refs_0_.place, ...), custom_call_target="tpu_custom_call" | custom-call | tf_op jit(solution)/shard_map/entry/pallas_call | solution.py:286
  208.4 3.7 %entry.14 = (bf16[256,512]{1,0:T(8,128)(2,1)S(1)}, bf16[256,512]{1,0:T(8,128)(2,1)S(1)}, bf16[256,128]{1,0:T(8,128)(2,1)S(1)}, bf16[256,128]{1,0:T(8,128)(2,1)S(...) custom-call(s32[7]{0:T(128)S(1)} %stack.46.order.refs_0_.place, ...), custom_call_target="tpu_custom_call" | custom-call | tf_op jit(solution)/shard_map/entry/pallas_call | solution.py:286
  212.2 3.7 %entry.15 = (bf16[256,512]{1,0:T(8,128)(2,1)S(1)}, bf16[256,512]{1,0:T(8,128)(2,1)S(1)}, bf16[256,128]{1,0:T(8,128)(2,1)S(1)}, bf16[256,128]{1,0:T(8,128)(2,1)S(...) custom-call(s32[7]{0:T(128)S(1)} %stack.46.order.refs_0_.place, ...), custom_call_target="tpu_custom_call" | custom-call | tf_op jit(solution)/shard_map/entry/pallas_call | solution.py:286
  224.5 4.1 %collective-permute-done.36.other = bf16[144,256]{1,0:T(8,128)(2,1)S(1)} collective-permute-done((bf16[144,256]{1,0:T(8,128)(2,1)S(1)}, bf16[144,256]{1,0:T(8,128)(2,1)S(1)}, u32[]{:S(2)}, u32[]{:S(2)}) %collective-permute-start.36) | collective-permute-done | bytes 73760 | tf_op jit(solution)/shard_map/ppermute | solution.py:488
  229.3 4.3 %collective-permute-done.37.other = bf16[144,256]{1,0:T(8,128)(2,1)S(1)} collective-permute-done((bf16[144,256]{1,0:T(8,128)(2,1)S(1)}, bf16[144,256]{1,0:T(8,128)(2,1)S(1)}, u32[]{:S(2)}, u32[]{:S(2)}) %collective-permute-start.37) | collective-permute-done | bytes 73760 | tf_op jit(solution)/shard_map/ppermute | solution.py:491
  255.3 5.7 %collective-permute-done.42 = bf16[512,512]{1,0:T(8,128)(2,1)S(1)} collective-permute-done((bf16[512,512]{1,0:T(8,128)(2,1)S(1)}, bf16[512,512]{1,0:T(8,128)(2,1)S(1)}, u32[]{:S(2)}, u32[]{:S(2)}) %collective-permute-start.42) | collective-permute-done | bytes 524320 | tf_op jit(solution)/shard_map/ppermute | solution.py:467
  261.1 3.8 %collective-permute-start.43 = (bf16[256,512]{1,0:T(8,128)(2,1)S(1)}, bf16[256,512]{1,0:T(8,128)(2,1)S(1)}, u32[]{:S(2)}, u32[]{:S(2)}) collective-permute-start(bf16[256,512]{1,0:T(8,128)(2,1)S(1)} %add_convert_fusion.2), channel_id=1, source_target_pairs={{0,3},{1,0},{2,1},{3,2},{4,7},{5,4},{6,5},{7,6},{8,11},{9,8},{10,9... | collective-permute-start | bytes 786440 | tf_op jit(solution)/shard_map/ppermute | solution.py:467
  265.0 7.2 %collective-permute-done.46 = bf16[512,512]{1,0:T(8,128)(2,1)S(1)} collective-permute-done((bf16[512,512]{1,0:T(8,128)(2,1)S(1)}, bf16[512,512]{1,0:T(8,128)(2,1)S(1)}, u32[]{:S(2)}, u32[]{:S(2)}) %collective-permute-start.46) | collective-permute-done | bytes 524320 | tf_op jit(solution)/shard_map/ppermute | solution.py:467
  272.3 3.8 %collective-permute-start.47 = (bf16[256,512]{1,0:T(8,128)(2,1)S(1)}, bf16[256,512]{1,0:T(8,128)(2,1)S(1)}, u32[]{:S(2)}, u32[]{:S(2)}) collective-permute-start(bf16[256,512]{1,0:T(8,128)(2,1)S(1)} %add_convert_fusion), channel_id=1, source_target_pairs={{0,3},{1,0},{2,1},{3,2},{4,7},{5,4},{6,5},{7,6},{8,11},{9,8},{10,9... | collective-permute-start | bytes 786440 | tf_op jit(solution)/shard_map/ppermute | solution.py:467
  277.8 3.7 %collective-permute-done.41 = bf16[256,512]{1,0:T(8,128)(2,1)S(1)} collective-permute-done((bf16[256,512]{1,0:T(8,128)(2,1)S(1)}, bf16[256,512]{1,0:T(8,128)(2,1)S(1)}, u32[]{:S(2)}, u32[]{:S(2)}) %collective-permute-start.41) | collective-permute-done | bytes 262176 | tf_op jit(solution)/shard_map/ppermute | solution.py:467
  (186 shorter events, 138.1 us)
Async XLA Ops:
  3.8 15.1 %collective-permute-start.1 = (bf16[528,512]{1,0:T(8,128)(2,1)S(1)}, bf16[528,512]{1,0:T(8,128)(2,1)S(1)}, u32[]{:S(2)}, u32[]{:S(2)}) collective-permute-start(bf16[528,512]{1,0:T(8,128)(2,1)S(1)} %pad_maximum_fusion.2.refs_1_), channel_id=1, source_target_pairs={{0,1},{1,2},{2,3},{3,0},{4,5},{5,6},{6,7},{7,4},{8,9},{9,10},{10,1... | collective-permute-start | bytes 1622024 | tf_op jit(solution)/shard_map/ppermute | solution.py:467
  5.9 36.2 %collective-permute-start.2 = (bf16[528,512]{1,0:T(8,128)(2,1)S(1)}, bf16[528,512]{1,0:T(8,128)(2,1)S(1)}, u32[]{:S(2)}, u32[]{:S(2)}) collective-permute-start(bf16[528,512]{1,0:T(8,128)(2,1)S(1)} %pad_maximum_fusion.2.refs_1_), channel_id=1, source_target_pairs={{0,3},{1,0},{2,1},{3,2},{4,7},{5,4},{6,5},{7,6},{8,11},{9,8},{10,9... | collective-permute-start | bytes 1622024 | tf_op jit(solution)/shard_map/ppermute | solution.py:467
  7.5 30.5 %collective-permute-start.4 = (bf16[256,512]{1,0:T(8,128)(2,1)S(1)}, bf16[256,512]{1,0:T(8,128)(2,1)S(1)}, u32[]{:S(2)}, u32[]{:S(2)}) collective-permute-start(bf16[256,512]{1,0:T(8,128)(2,1)S(1)} %get-tuple-element.219.refs_1_), channel_id=1, source_target_pairs={{0,3},{1,0},{2,1},{3,2},{4,7},{5,4},{6,5},{7,6},{8,11},{9,8},{10,9... | collective-permute-start | bytes 786440 | tf_op jit(solution)/shard_map/ppermute | solution.py:467
  9.5 31.9 %collective-permute-start.8 = (bf16[256,512]{1,0:T(8,128)(2,1)S(1)}, bf16[256,512]{1,0:T(8,128)(2,1)S(1)}, u32[]{:S(2)}, u32[]{:S(2)}) collective-permute-start(bf16[256,512]{1,0:T(8,128)(2,1)S(1)} %get-tuple-element.229.refs_1_), channel_id=1, source_target_pairs={{0,3},{1,0},{2,1},{3,2},{4,7},{5,4},{6,5},{7,6},{8,11},{9,8},{10,9... | collective-permute-start | bytes 786440 | tf_op jit(solution)/shard_map/ppermute | solution.py:467
  18.9 23.2 %collective-permute-start.3 = (bf16[528,512]{1,0:T(8,128)(2,1)S(1)}, bf16[528,512]{1,0:T(8,128)(2,1)S(1)}, u32[]{:S(2)}, u32[]{:S(2)}) collective-permute-start(bf16[528,512]{1,0:T(8,128)(2,1)S(1)} %collective-permute-done.1.refs_2_), channel_id=1, source_target_pairs={{0,1},{1,2},{2,3},{3,0},{4,5},{5,6},{6,7},{7,4},{8,9},{9,10},{10,1... | collective-permute-start | bytes 1622024 | tf_op jit(solution)/shard_map/ppermute | solution.py:467
  41.3 14.9 %collective-permute-start.9 = (bf16[256,512]{1,0:T(8,128)(2,1)S(1)}, bf16[256,512]{1,0:T(8,128)(2,1)S(1)}, u32[]{:S(2)}, u32[]{:S(2)}) collective-permute-start(bf16[256,512]{1,0:T(8,128)(2,1)S(1)} %collective-permute-done.8.refs_3_), channel_id=1, source_target_pairs={{0,3},{1,0},{2,1},{3,2},{4,7},{5,4},{6,5},{7,6},{8,11},{9,8},{10,9... | collective-permute-start | bytes 786440 | tf_op jit(solution)/shard_map/ppermute | solution.py:467
  92.3 14.8 %collective-permute-start.18 = (bf16[512,512]{1,0:T(8,128)(2,1)S(1)}, bf16[512,512]{1,0:T(8,128)(2,1)S(1)}, u32[]{:S(2)}, u32[]{:S(2)}) collective-permute-start(bf16[512,512]{1,0:T(8,128)(2,1)S(1)} %get-tuple-element.263), channel_id=1, source_target_pairs={{0,3},{1,0},{2,1},{3,2},{4,7},{5,4},{6,5},{7,6},{8,11},{9,8},{10,9... | collective-permute-start | bytes 1572872 | tf_op jit(solution)/shard_map/ppermute | solution.py:467
  94.8 16.1 %collective-permute-start.16 = (bf16[512,512]{1,0:T(8,128)(2,1)S(1)}, bf16[512,512]{1,0:T(8,128)(2,1)S(1)}, u32[]{:S(2)}, u32[]{:S(2)}) collective-permute-start(bf16[512,512]{1,0:T(8,128)(2,1)S(1)} %get-tuple-element.262), channel_id=1, source_target_pairs={{0,1},{1,2},{2,3},{3,0},{4,5},{5,6},{6,7},{7,4},{8,9},{9,10},{10,1... | collective-permute-start | bytes 1572872 | tf_op jit(solution)/shard_map/ppermute | solution.py:467
  97.7 20.6 %collective-permute-start.22 = (bf16[512,512]{1,0:T(8,128)(2,1)S(1)}, bf16[512,512]{1,0:T(8,128)(2,1)S(1)}, u32[]{:S(2)}, u32[]{:S(2)}) collective-permute-start(bf16[512,512]{1,0:T(8,128)(2,1)S(1)} %get-tuple-element.274), channel_id=1, source_target_pairs={{0,3},{1,0},{2,1},{3,2},{4,7},{5,4},{6,5},{7,6},{8,11},{9,8},{10,9... | collective-permute-start | bytes 1572872 | tf_op jit(solution)/shard_map/ppermute | solution.py:467
  101.0 21.1 %collective-permute-start.20 = (bf16[512,512]{1,0:T(8,128)(2,1)S(1)}, bf16[512,512]{1,0:T(8,128)(2,1)S(1)}, u32[]{:S(2)}, u32[]{:S(2)}) collective-permute-start(bf16[512,512]{1,0:T(8,128)(2,1)S(1)} %get-tuple-element.273), channel_id=1, source_target_pairs={{0,1},{1,2},{2,3},{3,0},{4,5},{5,6},{6,7},{7,4},{8,9},{9,10},{10,1... | collective-permute-start | bytes 1572872 | tf_op jit(solution)/shard_map/ppermute | solution.py:467
  107.2 16.8 %collective-permute-start.19 = (bf16[256,512]{1,0:T(8,128)(2,1)S(1)}, bf16[256,512]{1,0:T(8,128)(2,1)S(1)}, u32[]{:S(2)}, u32[]{:S(2)}) collective-permute-start(bf16[256,512]{1,0:T(8,128)(2,1)S(1)} %add_convert_fusion.6), channel_id=1, source_target_pairs={{0,3},{1,0},{2,1},{3,2},{4,7},{5,4},{6,5},{7,6},{8,11},{9,8},{10,9... | collective-permute-start | bytes 786440 | tf_op jit(solution)/shard_map/ppermute | solution.py:467
  111.0 16.7 %collective-permute-start.17 = (bf16[256,512]{1,0:T(8,128)(2,1)S(1)}, bf16[256,512]{1,0:T(8,128)(2,1)S(1)}, u32[]{:S(2)}, u32[]{:S(2)}) collective-permute-start(bf16[256,512]{1,0:T(8,128)(2,1)S(1)} %add_convert_fusion.7), channel_id=1, source_target_pairs={{0,1},{1,2},{2,3},{3,0},{4,5},{5,6},{6,7},{7,4},{8,9},{9,10},{10,1... | collective-permute-start | bytes 786440 | tf_op jit(solution)/shard_map/ppermute | solution.py:467
  160.6 16.1 %collective-permute-start.25 = (bf16[528,512]{1,0:T(8,128)(2,1)S(1)}, bf16[528,512]{1,0:T(8,128)(2,1)S(1)}, u32[]{:S(2)}, u32[]{:S(2)}) collective-permute-start(bf16[528,512]{1,0:T(8,128)(2,1)S(1)} %pad_maximum_fusion.3.refs_1_), channel_id=1, source_target_pairs={{0,1},{1,2},{2,3},{3,0},{4,5},{5,6},{6,7},{7,4},{8,9},{9,10},{10,1... | collective-permute-start | bytes 1622024 | tf_op jit(solution)/shard_map/ppermute | solution.py:467
  160.6 22.4 %collective-permute-start.26 = (bf16[528,512]{1,0:T(8,128)(2,1)S(1)}, bf16[528,512]{1,0:T(8,128)(2,1)S(1)}, u32[]{:S(2)}, u32[]{:S(2)}) collective-permute-start(bf16[528,512]{1,0:T(8,128)(2,1)S(1)} %pad_maximum_fusion.3.refs_1_), channel_id=1, source_target_pairs={{0,3},{1,0},{2,1},{3,2},{4,7},{5,4},{6,5},{7,6},{8,11},{9,8},{10,9... | collective-permute-start | bytes 1622024 | tf_op jit(solution)/shard_map/ppermute | solution.py:467
  176.6 22.5 %collective-permute-start.27 = (bf16[528,512]{1,0:T(8,128)(2,1)S(1)}, bf16[528,512]{1,0:T(8,128)(2,1)S(1)}, u32[]{:S(2)}, u32[]{:S(2)}) collective-permute-start(bf16[528,512]{1,0:T(8,128)(2,1)S(1)} %collective-permute-done.25.refs_2_), channel_id=1, source_target_pairs={{0,1},{1,2},{2,3},{3,0},{4,5},{5,6},{6,7},{7,4},{8,9},{9,10},{10,1... | collective-permute-start | bytes 1622024 | tf_op jit(solution)/shard_map/ppermute | solution.py:467
  189.8 18.6 %collective-permute-start.29 = (bf16[256,512]{1,0:T(8,128)(2,1)S(1)}, bf16[256,512]{1,0:T(8,128)(2,1)S(1)}, u32[]{:S(2)}, u32[]{:S(2)}) collective-permute-start(bf16[256,512]{1,0:T(8,128)(2,1)S(1)} %get-tuple-element.301.refs_1_), channel_id=1, source_target_pairs={{0,1},{1,2},{2,3},{3,0},{4,5},{5,6},{6,7},{7,4},{8,9},{9,10},{10,1... | collective-permute-start | bytes 786440 | tf_op jit(solution)/shard_map/ppermute | solution.py:467
  189.8 18.6 %collective-permute-start.30 = (bf16[256,512]{1,0:T(8,128)(2,1)S(1)}, bf16[256,512]{1,0:T(8,128)(2,1)S(1)}, u32[]{:S(2)}, u32[]{:S(2)}) collective-permute-start(bf16[256,512]{1,0:T(8,128)(2,1)S(1)} %collective-permute-done.28.refs_3_), channel_id=1, source_target_pairs={{0,3},{1,0},{2,1},{3,2},{4,7},{5,4},{6,5},{7,6},{8,11},{9,8},{10,9... | collective-permute-start | bytes 786440 | tf_op jit(solution)/shard_map/ppermute | solution.py:467
  195.4 16.8 %collective-permute-start.33 = (bf16[256,512]{1,0:T(8,128)(2,1)S(1)}, bf16[256,512]{1,0:T(8,128)(2,1)S(1)}, u32[]{:S(2)}, u32[]{:S(2)}) collective-permute-start(bf16[256,512]{1,0:T(8,128)(2,1)S(1)} %collective-permute-done.32.refs_3_), channel_id=1, source_target_pairs={{0,3},{1,0},{2,1},{3,2},{4,7},{5,4},{6,5},{7,6},{8,11},{9,8},{10,9... | collective-permute-start | bytes 786440 | tf_op jit(solution)/shard_map/ppermute | solution.py:467
  245.4 15.6 %collective-permute-start.42 = (bf16[512,512]{1,0:T(8,128)(2,1)S(1)}, bf16[512,512]{1,0:T(8,128)(2,1)S(1)}, u32[]{:S(2)}, u32[]{:S(2)}) collective-permute-start(bf16[512,512]{1,0:T(8,128)(2,1)S(1)} %get-tuple-element.344), channel_id=1, source_target_pairs={{0,3},{1,0},{2,1},{3,2},{4,7},{5,4},{6,5},{7,6},{8,11},{9,8},{10,9... | collective-permute-start | bytes 1572872 | tf_op jit(solution)/shard_map/ppermute | solution.py:467
  248.7 16.1 %collective-permute-start.40 = (bf16[512,512]{1,0:T(8,128)(2,1)S(1)}, bf16[512,512]{1,0:T(8,128)(2,1)S(1)}, u32[]{:S(2)}, u32[]{:S(2)}) collective-permute-start(bf16[512,512]{1,0:T(8,128)(2,1)S(1)} %get-tuple-element.343), channel_id=1, source_target_pairs={{0,1},{1,2},{2,3},{3,0},{4,5},{5,6},{6,7},{7,4},{8,9},{9,10},{10,1... | collective-permute-start | bytes 1572872 | tf_op jit(solution)/shard_map/ppermute | solution.py:467
  251.7 20.6 %collective-permute-start.46 = (bf16[512,512]{1,0:T(8,128)(2,1)S(1)}, bf16[512,512]{1,0:T(8,128)(2,1)S(1)}, u32[]{:S(2)}, u32[]{:S(2)}) collective-permute-start(bf16[512,512]{1,0:T(8,128)(2,1)S(1)} %get-tuple-element.355), channel_id=1, source_target_pairs={{0,3},{1,0},{2,1},{3,2},{4,7},{5,4},{6,5},{7,6},{8,11},{9,8},{10,9... | collective-permute-start | bytes 1572872 | tf_op jit(solution)/shard_map/ppermute | solution.py:467
  255.0 21.1 %collective-permute-start.44 = (bf16[512,512]{1,0:T(8,128)(2,1)S(1)}, bf16[512,512]{1,0:T(8,128)(2,1)S(1)}, u32[]{:S(2)}, u32[]{:S(2)}) collective-permute-start(bf16[512,512]{1,0:T(8,128)(2,1)S(1)} %get-tuple-element.354), channel_id=1, source_target_pairs={{0,1},{1,2},{2,3},{3,0},{4,5},{5,6},{6,7},{7,4},{8,9},{9,10},{10,1... | collective-permute-start | bytes 1572872 | tf_op jit(solution)/shard_map/ppermute | solution.py:467
  261.1 16.8 %collective-permute-start.43 = (bf16[256,512]{1,0:T(8,128)(2,1)S(1)}, bf16[256,512]{1,0:T(8,128)(2,1)S(1)}, u32[]{:S(2)}, u32[]{:S(2)}) collective-permute-start(bf16[256,512]{1,0:T(8,128)(2,1)S(1)} %add_convert_fusion.2), channel_id=1, source_target_pairs={{0,3},{1,0},{2,1},{3,2},{4,7},{5,4},{6,5},{7,6},{8,11},{9,8},{10,9... | collective-permute-start | bytes 786440 | tf_op jit(solution)/shard_map/ppermute | solution.py:467
  264.9 16.7 %collective-permute-start.41 = (bf16[256,512]{1,0:T(8,128)(2,1)S(1)}, bf16[256,512]{1,0:T(8,128)(2,1)S(1)}, u32[]{:S(2)}, u32[]{:S(2)}) collective-permute-start(bf16[256,512]{1,0:T(8,128)(2,1)S(1)} %add_convert_fusion.3), channel_id=1, source_target_pairs={{0,1},{1,2},{2,3},{3,0},{4,5},{5,6},{6,7},{7,4},{8,9},{9,10},{10,1... | collective-permute-start | bytes 786440 | tf_op jit(solution)/shard_map/ppermute | solution.py:467
  (35 other events, 258.8 us)
